TPU v7x, 256 devices: a whole 4x4x8 slice. The times are simulated.
256 devices in a mesh: row: 32 (over y, z), col: 8 (over x, core).
Axes of the slice: x: 4, y: 4, z: 8, core: 2. Of those that a mesh axis runs over, the one named last changes fastest.
Arguments:
- ancestor_inverse: float32 [12288, 12288], P('row', 'col'), may hold values from -5 to 320, as said below
- panel_one: float32 [12288, 256], P(('row', 'col')), may hold values from -0.015625 to 0.015625
- struct_one: int32 [10752], replicated, may hold values from 0 to 12287, as said below
- lower_one: float32 [256, 256], replicated, may hold values from -1 to 2, as said below
- panel_two: float32 [12288, 256], P(('row', 'col')), may hold values from -0.015625 to 0.015625
- struct_two: int32 [9216], replicated, may hold values from 0 to 12287, as said below
- panel_above: float32 [256, 256], replicated, may hold values from -0.375 to 0.375
- lower_two: float32 [256, 256], replicated, may hold values from -1 to 2, as said below
- tile_owner: int32 [1536, 1], P(('col', 'row')), may hold values from 0 to 7; in each aligned block of 6 rows (0 to 5, 6 to 11, ...) at most 2 rows name the same one
Outputs:
- inverse_one: float32 [12288, 256], P(('col', 'row'))
- diag_one: float32 [256, 256], replicated
- cross_two: float32 [256, 256], replicated
- diag_two: float32 [256, 256], replicated
- delivered: float32 [4096, 8, 256], P(('row', 'col'))
Inputs may be any that keep to these rules, and one draw needn't show every extreme that they name: ancestor_inverse is exactly symmetric and positive definite. `struct_one`: 10752 distinct row numbers of the ancestor block. `struct_two`: 9216 distinct entries of struct_one. `lower_one`: lower triangular with a positive diagonal. `lower_two`: lower triangular with a positive diagonal. `tile_owner`: within each aligned block of 6 entries (the tiles of one device) no value appears more than 2 times; in some block a value appears exactly 2 times.
All inputs are finite; a program needn't handle non-finite values.
Results may differ from a plain program's by a relative error of at most 0.00007.
Values sent between devices are 32-bit elements; how exact they have to be, the bound alone decides.
No kernel may reach another device: no remote copies, remote signals or barrier semaphores. Data moves between devices by JAX's collectives and lax.ppermute only.
A program may use at most 64 MiB of HBM per device.

v0:
```python
import jax
import jax.numpy as jnp
from jax import lax
from jax.sharding import Mesh
from jax.sharding import PartitionSpec as P

ANC = 12288
CAP = 2
COL = ("col_0", "col_1")
ROW = ("row_0", "row_1")
ROW_COL = ("row_0", "row_1", "col_0", "col_1")
COL_ROW = ("col_0", "col_1", "row_0", "row_1")


def sent_together(arrays, axis, dim, along):
    widths = [a.shape[along] for a in arrays]
    both = jnp.concatenate(arrays, axis=along)
    whole = lax.all_gather(both, axis, axis=dim, tiled=True)
    return tuple(jnp.split(whole, [sum(widths[:k]) for k in range(1, len(widths))], axis=along))


def summed_rows(running, axes):
    for axis in axes:
        running = lax.psum_scatter(running, axis, scatter_dimension=0, tiled=True)
    return running


def split_up(value, dim, length):
    shape = value.shape
    tiles = value.reshape(*shape[:dim], length, shape[dim] // length, *shape[dim + 1 :])
    return jnp.moveaxis(tiles, dim, 0)


def sum_at_owner(value, axis, dim):
    length = lax.axis_size(axis)
    tiles = lax.all_to_all(split_up(value, dim, length), axis, 0, 0, tiled=True)
    return jnp.sum(tiles, axis=0)


def sum_in_two_steps(value, axes, dim):
    far, near = axes
    own = sum_at_owner(split_up(value, dim, lax.axis_size(far)), near, dim + 1)
    return jnp.sum(lax.all_to_all(own, far, 0, 0, tiled=True), axis=0)


def padded_to(lines, length):
    spare = -len(lines) % length
    return jnp.pad(lines, [(0, spare)] + [(0, 0)] * (lines.ndim - 1))


def copy_for_each(value, axis):
    copies = jnp.broadcast_to(value, (lax.axis_size(axis), *value.shape))
    return lax.all_to_all(copies, axis, split_axis=0, concat_axis=0, tiled=True)


def in_order(tiles, dim):
    shape = list(tiles.shape[1:])
    shape[dim] *= tiles.shape[0]
    return jnp.moveaxis(tiles, 0, dim).reshape(shape)


def whole_of(value, axes, dim):
    far, near = axes
    tiles = copy_for_each(copy_for_each(value, far), near)
    return in_order(tiles.swapaxes(0, 1).reshape(-1, *value.shape), dim)


def nested_sum(value, axes):
    own = sum_in_two_steps(
        padded_to(value, lax.axis_size(axes[0]) * lax.axis_size(axes[1])), axes, 0
    )
    whole = whole_of(own, axes, 0)
    return whole[: len(value)].reshape(value.shape)


def packed_total(arrays, axis):
    ends = [0]
    for a in arrays:
        ends.append(ends[-1] + a.size)
    running = nested_sum(jnp.concatenate([a.ravel() for a in arrays]), axis)
    return tuple((running[b:e].reshape(a.shape) for a, b, e in zip(arrays, ends, ends[1:])))


def nested_sum_2(value, axes):
    lines = value.reshape(-1, value.shape[-1])
    own = sum_in_two_steps(
        padded_to(lines, lax.axis_size(axes[0]) * lax.axis_size(axes[1])), axes, 0
    )
    whole = whole_of(own, axes, 0)
    return whole[: len(lines)].reshape(value.shape)


def matmul(left, right):
    return jnp.dot(left, right, precision=lax.Precision.HIGHEST, preferred_element_type=jnp.float32)


def contract_rows(left, right):
    return lax.dot_general(
        left,
        right,
        (((0,), (0,)), ((), ())),
        precision=lax.Precision.HIGHEST,
        preferred_element_type=jnp.float32,
    )


def product_term(ancestor_inverse, block_panel, placed_rows):
    return jnp.concatenate([contract_rows(ancestor_inverse, block_panel), placed_rows], axis=1)


def deliver(values, tile_owner, col_count):
    tile_count = tile_owner.shape[0]
    tile_rows = values.shape[0] // tile_count
    all_tiles = values.reshape(tile_count, tile_rows, values.shape[1])
    owner_col = tile_owner[:, 0]
    col_ids = jnp.arange(col_count, dtype=jnp.int32)
    onehot = (owner_col[:, None] == col_ids[None, :]).astype(jnp.int32)
    tile_rank = jnp.sum((jnp.cumsum(onehot, axis=0) - onehot) * onehot, axis=1)
    slot_index = jnp.arange(CAP, dtype=jnp.int32)
    select = (
        (owner_col[None, None, :] == col_ids[:, None, None])
        & (tile_rank[None, None, :] == slot_index[None, :, None])
    ).astype(jnp.float32)
    outgoing = jnp.einsum("cks,srb->ckrb", select, all_tiles, precision=lax.Precision.HIGHEST)
    incoming = lax.all_to_all(outgoing, COL, split_axis=0, concat_axis=0, tiled=True)
    return incoming.reshape(col_count * CAP, tile_rows, values.shape[1])


def local(
    ancestor_inverse,
    panel_one,
    struct_one,
    lower_one,
    panel_two,
    struct_two,
    panel_above,
    lower_two,
    tile_owner,
):
    row_count = lax.axis_size(ROW)
    col_count = lax.axis_size(COL)
    row_index = lax.axis_index(ROW)
    col_index = lax.axis_index(COL)
    block_ratio = row_count // col_count
    local_rows = panel_one.shape[0]
    inner_rows = ancestor_inverse.shape[0]
    column_rows = ancestor_inverse.shape[1]
    width = panel_one.shape[1]
    mask_one = jnp.zeros((ANC,), jnp.float32).at[struct_one].set(1.0)
    mask_two = jnp.zeros((ANC,), jnp.float32).at[struct_two].set(1.0)
    panel_start = (row_index * col_count + col_index) * local_rows
    result_start = (col_index * row_count + row_index) * local_rows
    local_one = panel_one * lax.dynamic_slice_in_dim(mask_one, panel_start, local_rows)[:, None]
    local_two = panel_two * lax.dynamic_slice_in_dim(mask_two, panel_start, local_rows)[:, None]
    result_mask_one = lax.dynamic_slice_in_dim(mask_one, result_start, local_rows)[:, None]
    result_mask_two = lax.dynamic_slice_in_dim(mask_two, result_start, local_rows)[:, None]
    owns_block = (row_index // block_ratio == col_index).astype(jnp.float32)
    block_offset = row_index % block_ratio * inner_rows
    gathered_one, gathered_two = sent_together((local_one, local_two), COL, 0, 1)
    joined = jnp.concatenate([gathered_one, gathered_two], axis=1)
    empty_rows = jnp.zeros((column_rows, joined.shape[1]), jnp.float32)
    summed = summed_rows(
        product_term(
            ancestor_inverse,
            joined,
            lax.dynamic_update_slice_in_dim(empty_rows, joined * owns_block, block_offset, 0),
        ),
        ROW,
    )
    product_one = summed[:, :width]
    product_two = summed[:, width : 2 * width]
    resident_one = summed[:, 2 * width : 3 * width]
    resident_two = summed[:, 3 * width :]
    inverse_one = -product_one * result_mask_one
    partial_gram = contract_rows(resident_one, inverse_one)
    partial_cross = contract_rows(inverse_one, resident_two)
    gram_one, cross_sum = packed_total(
        (partial_gram, partial_cross), (("row_0", "row_1"), ("col_0", "col_1"))
    )
    diag_one = matmul(lower_one.T, lower_one) - gram_one
    cross_two = -(cross_sum + matmul(diag_one, panel_above))
    inverse_two = -(product_two + matmul(inverse_one, panel_above)) * result_mask_two
    partial_second = contract_rows(resident_two, inverse_two)
    gram_two = nested_sum_2(partial_second, (("row_0", "row_1"), ("col_0", "col_1")))
    diag_two = matmul(lower_two.T, lower_two) - gram_two - matmul(panel_above.T, cross_two)
    delivered = deliver(inverse_two, tile_owner, col_count)
    return (inverse_one, diag_one, cross_two, diag_two, delivered)


def solution(mesh):
    finer = Mesh(mesh.devices.reshape(4, 8, 4, 2), ("row_0", "row_1", "col_0", "col_1"))
    return jax.shard_map(
        local,
        mesh=finer,
        in_specs=(
            P(ROW, COL),
            P(ROW_COL, None),
            P(),
            P(),
            P(ROW_COL, None),
            P(),
            P(),
            P(),
            P(COL_ROW, None),
        ),
        out_specs=(P(COL_ROW, None), P(), P(), P(), P(ROW_COL, None, None)),
        check_vma=False,
    )
```

profile of v0, /device:TPU:1, one launch (start us, length us, event | category | flops | bytes accessed | tf_op | source)
XLA Modules:
  0.0 365.4 jit_solution(10916827111280260145)
XLA Ops:
  9.0 39.8 %scatter_custom_fusion = f32[12288]{0:T(1024)S(1)} fusion(s32[10752]{0:T(1024)S(1)} %compare_select_fusion, f32[10752]{0:T(1024)S(1)} %broadcast.50, f32[]{:T(128)} %constant.27.clone.1), kind=kCustom, calls=%fused_computation.35 | custom fusion | bytes 49156 | tf_op jit(solution)/shard_map/scatter | solution.py:149
  48.8 34.2 %scatter_custom_fusion.1 = f32[12288]{0:T(1024)S(1)} fusion(s32[9216]{0:T(1024)S(1)} %compare_select_fusion.1, f32[9216]{0:T(1024)S(1)} %broadcast.51, f32[]{:T(128)} %constant.27.clone.1), kind=kCustom, calls=%fused_computation.33 | custom fusion | bytes 49156 | tf_op jit(solution)/shard_map/scatter | solution.py:150
  84.9 16.6 %all_gather.3 = f32[384,512]{1,0:T(8,128)S(1)} all-gather(f32[48,512]{1,0:T(8,128)S(1)} %pad_maximum_fusion.1), channel_id=1, replica_groups=mesh['row_0'=4,'row_1'=8,'col_0'=4,'col_1'=2] {'col_0','col_1'}, dimensions={0}, use_global_device_ids=true | all-gather | bytes 884736 | tf_op jit(solution)/shard_map/all_gather | solution.py:18
  102.6 6.8 %convolution_bitcast_fusion = f32[1536,512]{0,1:T(8,128)} fusion(f32[384,512]{1,0:T(8,128)S(1)} %all_gather.3, f32[384,1536]{1,0:T(8,128)S(1)} %copy-done), kind=kOutput, calls=%fused_computation.3 | convolution fusion | flops 3623878656 | bytes 6291456 | tf_op jit(solution)/shard_map/dot_general | solution.py:98
  111.5 3.1 pad_maximum_fusion
  114.7 67.1 %reduce-scatter.5.cloned.1.call-done = f32[384,1024]{0,1:T(8,128)} async-done(((f32[1536,1024]{0,1:T(8,128)}), f32[384,1024]{0,1:T(8,128)}) %reduce-scatter.5.cloned.1.call-update) | async-done | bytes 1572880 | tf_op jit(solution)/shard_map/reduce_scatter | solution.py:24
  181.8 3.0 copy.54
  185.2 35.8 %reduce-scatter.7.cloned.1.call-done = f32[48,1024]{1,0:T(8,128)} async-done(((f32[384,1024]{1,0:T(8,128)}), f32[48,1024]{1,0:T(8,128)}) %reduce-scatter.7.cloned.1.call-update) | async-done | bytes 196624 | tf_op jit(solution)/shard_map/reduce_scatter | solution.py:24
  224.0 9.1 %all-to-all-start.8 = ((f32[8,2,8,256]{3,2,1,0:T(8,128)}), f32[8,2,8,256]{3,2,1,0:T(8,128)S(1)}, u32[]{:S(2)}, u32[]{:S(2)}) async-start(f32[8,2,8,256]{3,2,1,0:T(8,128)} %copy.50), calls=%async_computation.9 | async-start | bytes 262144 | tf_op jit(solution)/shard_map/all_to_all | solution.py:125
  236.4 2.0 all-to-all-done.8
  239.1 4.8 %all-to-all-start.4 = ((f32[8,32,1,256]{3,1,2,0:T(8,128)}), f32[8,32,1,256]{3,1,2,0:T(8,128)}, u32[]{:S(2)}, u32[]{:S(2)}) async-start(f32[8,32,1,256]{3,1,2,0:T(8,128)} %bitcast.47), calls=%async_computation.5 | async-start | bytes 524288 | tf_op jit(solution)/shard_map/all_to_all | solution.py:36
  246.2 1.8 maximum_bitcast_fusion
  248.0 2.4 all-to-all-done.4
  250.5 4.4 %all-to-all-start = ((f32[8,32,512]{2,1,0:T(8,128)}), f32[8,32,512]{2,1,0:T(8,128)S(1)}, u32[]{:S(2)}, u32[]{:S(2)}) async-start(f32[8,32,512]{2,1,0:T(8,128)} %maximum_bitcast_fusion), calls=%async_computation.1 | async-start | bytes 1048576 | tf_op jit(solution)/shard_map/all_to_all | solution.py:36
  254.9 1.6 reduce_sum.49
  257.9 6.5 %all-to-all-done = f32[8,32,512]{2,1,0:T(8,128)S(1)} async-done(((f32[8,32,512]{2,1,0:T(8,128)}), f32[8,32,512]{2,1,0:T(8,128)S(1)}, u32[]{:S(2)}, u32[]{:S(2)}) %all-to-all-start) | async-done | bytes 524320 | tf_op jit(solution)/shard_map/all_to_all | solution.py:36
  264.4 7.1 %all-to-all-start.5 = ((f32[32,1,256]{2,1,0:T(1,128)}), f32[32,1,256]{2,1,0:T(1,128)}, u32[]{:S(2)}, u32[]{:S(2)}) async-start(f32[32,1,256]{2,1,0:T(1,128)} %reduce_sum.50), calls=%async_computation.6 | async-start | bytes 65536 | tf_op jit(solution)/shard_map/all_to_all | solution.py:43
  272.1 1.5 all_to_all.36
  273.7 6.6 %all-to-all-done.5 = f32[32,1,256]{2,1,0:T(1,128)} async-done(((f32[32,1,256]{2,1,0:T(1,128)}), f32[32,1,256]{2,1,0:T(1,128)}, u32[]{:S(2)}, u32[]{:S(2)}) %all-to-all-start.5) | async-done | bytes 32800 | tf_op jit(solution)/shard_map/all_to_all | solution.py:43
  280.2 3.9 %all-to-all-start.1 = ((f32[32,1,512]{2,1,0:T(1,128)}), f32[32,1,512]{2,1,0:T(1,128)S(1)}, u32[]{:S(2)}, u32[]{:S(2)}) async-start(f32[32,1,512]{2,1,0:T(1,128)} %all_to_all.36), calls=%async_computation.2 | async-start | bytes 131072 | tf_op jit(solution)/shard_map/all_to_all | solution.py:43
  284.9 8.1 %all-to-all-done.1 = f32[32,1,512]{2,1,0:T(1,128)S(1)} async-done(((f32[32,1,512]{2,1,0:T(1,128)}), f32[32,1,512]{2,1,0:T(1,128)S(1)}, u32[]{:S(2)}, u32[]{:S(2)}) %all-to-all-start.1) | async-done | bytes 65568 | tf_op jit(solution)/shard_map/all_to_all | solution.py:43
  293.6 3.9 %all-to-all-start.6 = ((f32[32,1,256]{2,1,0:T(1,128)}), f32[32,1,256]{2,1,0:T(1,128)S(1)}, u32[]{:S(2)}, u32[]{:S(2)}) async-start(f32[32,1,256]{2,1,0:T(1,128)} %broadcast_in_dim.42), calls=%async_computation.7 | async-start | bytes 65536 | tf_op jit(solution)/shard_map/all_to_all | solution.py:53
  297.6 8.6 %all-to-all-done.6 = f32[32,1,256]{2,1,0:T(1,128)S(1)} async-done(((f32[32,1,256]{2,1,0:T(1,128)}), f32[32,1,256]{2,1,0:T(1,128)S(1)}, u32[]{:S(2)}, u32[]{:S(2)}) %all-to-all-start.6) | async-done | bytes 32800 | tf_op jit(solution)/shard_map/all_to_all | solution.py:53
  306.9 3.9 %all-to-all-start.2 = ((f32[32,1,512]{2,1,0:T(1,128)}), f32[32,1,512]{2,1,0:T(1,128)S(1)}, u32[]{:S(2)}, u32[]{:S(2)}) async-start(f32[32,1,512]{2,1,0:T(1,128)} %broadcast_in_dim.40), calls=%async_computation.3 | async-start | bytes 131072 | tf_op jit(solution)/shard_map/all_to_all | solution.py:53
  310.7 8.8 %all-to-all-done.2 = f32[32,1,512]{2,1,0:T(1,128)S(1)} async-done(((f32[32,1,512]{2,1,0:T(1,128)}), f32[32,1,512]{2,1,0:T(1,128)S(1)}, u32[]{:S(2)}, u32[]{:S(2)}) %all-to-all-start.2) | async-done | bytes 65568 | tf_op jit(solution)/shard_map/all_to_all | solution.py:53
  320.3 9.0 %all-to-all-start.7 = ((f32[8,32,1,256]{3,1,2,0:T(8,128)}), f32[8,32,1,256]{3,1,2,0:T(8,128)S(1)}, u32[]{:S(2)}, u32[]{:S(2)}) async-start(f32[8,32,1,256]{3,1,2,0:T(8,128)} %broadcast_in_dim.43), calls=%async_computation.8 | async-start | bytes 524288 | tf_op jit(solution)/shard_map/all_to_all | solution.py:53
  329.3 6.5 %all-to-all-done.7 = f32[8,32,1,256]{3,1,2,0:T(8,128)S(1)} async-done(((f32[8,32,1,256]{3,1,2,0:T(8,128)}), f32[8,32,1,256]{3,1,2,0:T(8,128)S(1)}, u32[]{:S(2)}, u32[]{:S(2)}) %all-to-all-start.7) | async-done | bytes 262176 | tf_op jit(solution)/shard_map/all_to_all | solution.py:53
  336.7 4.4 %all-to-all-start.3 = ((f32[8,32,512]{2,1,0:T(8,128)}), f32[8,32,512]{2,1,0:T(8,128)S(1)}, u32[]{:S(2)}, u32[]{:S(2)}) async-start(f32[8,32,512]{2,1,0:T(8,128)} %broadcast_in_dim.41), calls=%async_computation.4 | async-start | bytes 1048576 | tf_op jit(solution)/shard_map/all_to_all | solution.py:53
  341.8 2.3 convolution_subtract_fusion
  344.1 6.5 %all-to-all-done.3 = f32[8,32,512]{2,1,0:T(8,128)S(1)} async-done(((f32[8,32,512]{2,1,0:T(8,128)}), f32[8,32,512]{2,1,0:T(8,128)S(1)}, u32[]{:S(2)}, u32[]{:S(2)}) %all-to-all-start.3) | async-done | bytes 524320 | tf_op jit(solution)/shard_map/all_to_all | solution.py:53
  354.1 1.4 fusion.1
  355.5 2.3 fusion
  (76 shorter events, 27.1 us)
Async XLA Ops:
  7.2 95.4 %copy-start = (f32[384,1536]{1,0:T(8,128)S(1)}, f32[384,1536]{1,0:T(8,128)}, u32[]{:S(2)}) copy-start(f32[384,1536]{1,0:T(8,128)} %param.9) | copy-start | bytes 7077892
  7.2 174.7 %reduce-scatter.5.cloned.1.call-start = ((), (), s32[]{:S(2)}) async-start(), calls=%async_computation.11 | async-start | bytes 7864320 | tf_op jit(solution)/shard_map/reduce_scatter | solution.py:24
  109.4 1.1 copy-start.2
  109.4 2.1 copy-start.1
  114.6 70.3 %copy-start.11 = (s32[6,1]{0,1:T(1,128)S(1)}, s32[6,1]{0,1:T(1,128)}, u32[]{:S(2)}) copy-start(s32[6,1]{0,1:T(1,128)} %param.17) | copy-start | bytes 76
  114.6 107.3 %copy-start.3 = (f32[256,256]{1,0:T(8,128)S(1)}, f32[256,256]{1,0:T(8,128)}, u32[]{:S(2)}) copy-start(f32[256,256]{1,0:T(8,128)} %param.15) | copy-start | bytes 786436
  114.6 106.4 %reduce-scatter.7.cloned.1.call-start = ((), (), s32[]{:S(2)}) async-start(), calls=%async_computation.12 | async-start | bytes 1769472 | tf_op jit(solution)/shard_map/reduce_scatter | solution.py:24
  224.0 14.4 %all-to-all-start.8 = ((f32[8,2,8,256]{3,2,1,0:T(8,128)}), f32[8,2,8,256]{3,2,1,0:T(8,128)S(1)}, u32[]{:S(2)}, u32[]{:S(2)}) async-start(f32[8,2,8,256]{3,2,1,0:T(8,128)} %copy.50), calls=%async_computation.9 | async-start | bytes 262144 | tf_op jit(solution)/shard_map/all_to_all | solution.py:125
  238.4 0.7 copy-start.9
  239.1 11.4 %all-to-all-start.4 = ((f32[8,32,1,256]{3,1,2,0:T(8,128)}), f32[8,32,1,256]{3,1,2,0:T(8,128)}, u32[]{:S(2)}, u32[]{:S(2)}) async-start(f32[8,32,1,256]{3,1,2,0:T(8,128)} %bitcast.47), calls=%async_computation.5 | async-start | bytes 524288 | tf_op jit(solution)/shard_map/all_to_all | solution.py:36
  246.2 95.7 %copy-start.4 = (f32[256,256]{1,0:T(8,128)S(1)}, f32[256,256]{1,0:T(8,128)}, u32[]{:S(2)}) copy-start(f32[256,256]{1,0:T(8,128)} %param.16) | copy-start | bytes 786436
  250.5 13.9 %all-to-all-start = ((f32[8,32,512]{2,1,0:T(8,128)}), f32[8,32,512]{2,1,0:T(8,128)S(1)}, u32[]{:S(2)}, u32[]{:S(2)}) async-start(f32[8,32,512]{2,1,0:T(8,128)} %maximum_bitcast_fusion), calls=%async_computation.1 | async-start | bytes 1048576 | tf_op jit(solution)/shard_map/all_to_all | solution.py:36
  264.4 15.8 %all-to-all-start.5 = ((f32[32,1,256]{2,1,0:T(1,128)}), f32[32,1,256]{2,1,0:T(1,128)}, u32[]{:S(2)}, u32[]{:S(2)}) async-start(f32[32,1,256]{2,1,0:T(1,128)} %reduce_sum.50), calls=%async_computation.6 | async-start | bytes 65536 | tf_op jit(solution)/shard_map/all_to_all | solution.py:43
  280.2 12.8 %all-to-all-start.1 = ((f32[32,1,512]{2,1,0:T(1,128)}), f32[32,1,512]{2,1,0:T(1,128)S(1)}, u32[]{:S(2)}, u32[]{:S(2)}) async-start(f32[32,1,512]{2,1,0:T(1,128)} %all_to_all.36), calls=%async_computation.2 | async-start | bytes 131072 | tf_op jit(solution)/shard_map/all_to_all | solution.py:43
  293.6 12.6 %all-to-all-start.6 = ((f32[32,1,256]{2,1,0:T(1,128)}), f32[32,1,256]{2,1,0:T(1,128)S(1)}, u32[]{:S(2)}, u32[]{:S(2)}) async-start(f32[32,1,256]{2,1,0:T(1,128)} %broadcast_in_dim.42), calls=%async_computation.7 | async-start | bytes 65536 | tf_op jit(solution)/shard_map/all_to_all | solution.py:53
  306.9 12.7 %all-to-all-start.2 = ((f32[32,1,512]{2,1,0:T(1,128)}), f32[32,1,512]{2,1,0:T(1,128)S(1)}, u32[]{:S(2)}, u32[]{:S(2)}) async-start(f32[32,1,512]{2,1,0:T(1,128)} %broadcast_in_dim.40), calls=%async_computation.3 | async-start | bytes 131072 | tf_op jit(solution)/shard_map/all_to_all | solution.py:53
  320.3 15.5 %all-to-all-start.7 = ((f32[8,32,1,256]{3,1,2,0:T(8,128)}), f32[8,32,1,256]{3,1,2,0:T(8,128)S(1)}, u32[]{:S(2)}, u32[]{:S(2)}) async-start(f32[8,32,1,256]{3,1,2,0:T(8,128)} %broadcast_in_dim.43), calls=%async_computation.8 | async-start | bytes 524288 | tf_op jit(solution)/shard_map/all_to_all | solution.py:53
  335.8 0.9 copy-start.6
  336.7 13.9 %all-to-all-start.3 = ((f32[8,32,512]{2,1,0:T(8,128)}), f32[8,32,512]{2,1,0:T(8,128)S(1)}, u32[]{:S(2)}, u32[]{:S(2)}) async-start(f32[8,32,512]{2,1,0:T(8,128)} %broadcast_in_dim.41), calls=%async_computation.4 | async-start | bytes 1048576 | tf_op jit(solution)/shard_map/all_to_all | solution.py:53
  344.1 9.3 %copy-start.5 = (f32[256,256]{1,0:T(8,128)S(1)}, f32[256,256]{1,0:T(8,128)}, u32[]{:S(2)}) copy-start(f32[256,256]{1,0:T(8,128)} %param.12) | copy-start | bytes 786436
  351.4 6.5 %copy-start.10 = (f32[8,2,8,256]{3,2,1,0:T(8,128)S(1)}, f32[8,2,8,256]{3,2,1,0:T(8,128)}, u32[]{:S(2)}) copy-start(f32[8,2,8,256]{3,2,1,0:T(8,128)} %copy-done.9) | copy-start | bytes 393220
  354.1 4.5 %copy-start.7 = (f32[256,256]{1,0:T(8,128)}, f32[256,256]{1,0:T(8,128)S(1)}, u32[]{:S(2)}) copy-start(f32[256,256]{1,0:T(8,128)S(1)} %convolution_subtract_fusion.1) | copy-start | bytes 786436
  355.5 3.0 copy-start.8
Sparse Core Ops, SparseCore 0:
  114.7 67.0 reduce-scatter.4
  185.0 35.9 reduce-scatter.6
where the time goes:
time: 367 us; the launch traced here: 365 us
  waiting for transfers between devices  159 us (43%)
  local copies, waits for them, and re-layouts  94.6 us (26%)
  starting transfers between devices  50.5 us (14%)
  matrix products  18.3 us (5%)
  blocking collectives  16.6 us (5%)
  between operations  14.3 us (4%)
  other arithmetic  11.9 us (3%)
    reduce_scatter x2, waiting for transfers between devices, summed_rows(): running = lax.psum_scatter(running, axis, scatter_dimension=0, tiled=True)  103 us
    scatter x1, local copies, waits for them, and re-layouts, local(): mask_one = jnp.zeros((ANC,), jnp.float32).at[struct_one].set(1.0)  39.8 us
    scatter x1, local copies, waits for them, and re-layouts, local(): mask_two = jnp.zeros((ANC,), jnp.float32).at[struct_two].set(1.0)  34.2 us
    all_to_all x4, waiting for transfers between devices, copy_for_each(): return lax.all_to_all(copies, axis, split_axis=0, concat_axis=0, tiled=True)  30.5 us
    all_to_all x4, starting transfers between devices, copy_for_each(): return lax.all_to_all(copies, axis, split_axis=0, concat_axis=0, tiled=True)  21.1 us
    all_gather x1, blocking collectives, sent_together(): whole = lax.all_gather(both, axis, axis=dim, tiled=True)  16.6 us
    all_to_all x2, waiting for transfers between devices, sum_in_two_steps(): return jnp.sum(lax.all_to_all(own, far, 0, 0, tiled=True), axis=0)  14.7 us
    all_to_all x2, starting transfers between devices, sum_in_two_steps(): return jnp.sum(lax.all_to_all(own, far, 0, 0, tiled=True), axis=0)  10.9 us
  transfers between devices with their start and end apart: 11, of which 11 were waited for; matrix products, arithmetic and copies ran while one was open for 4% of the time, Pallas kernels for 0%

commit v1 on v0

v1 whole, which is shorter than its diff:
```python
import jax
import jax.numpy as jnp
from jax import lax
from jax.sharding import Mesh
from jax.sharding import PartitionSpec as P

CAP = 2
COL = ("col_0", "col_1")
ROW = ("row_0", "row_1")
ROW_COL = ROW + COL
COL_ROW = COL + ROW
N_ROW = 32
N_COL = 8
N_Y, N_Z = 4, 8


def row_mask(listed, start, count):
    rows = start + jnp.arange(count, dtype=jnp.int32)
    hit = listed[None, :] == rows[:, None]
    return jnp.max(jnp.where(hit, 1.0, 0.0), axis=1, keepdims=True)


def dot(left, right, dims=((1,), (0,)), precision=lax.Precision.HIGHEST):
    return lax.dot_general(
        left, right, (dims, ((), ())), precision=precision, preferred_element_type=jnp.float32
    )


def sum_at_owner(value, axis):
    count = lax.axis_size(axis)
    parts = value.reshape(count, value.shape[0] // count, *value.shape[1:])
    return jnp.sum(lax.all_to_all(parts, axis, 0, 0, tiled=True), axis=0)


def copies_of(value, axis):
    copies = jnp.broadcast_to(value[None], (lax.axis_size(axis), *value.shape))
    return lax.all_to_all(copies, axis, 0, 0, tiled=True)


def total(value):
    own = sum_at_owner(sum_at_owner(value, COL), ROW)
    over_row = copies_of(own, ROW).reshape(-1, value.shape[1])
    return copies_of(over_row, COL).reshape(value.shape)


def gather_moves():
    pairs = []
    for block in range(N_ROW * N_COL):
        column, place = divmod(block, N_ROW)
        z, y = divmod(place, N_Y)
        pairs.append((block, (y * N_Z + z) * N_COL + column))
    return pairs


def result_moves():
    pairs = []
    for block in range(N_ROW * N_COL):
        column, row = divmod(block, N_ROW)
        pairs.append((block, row * N_COL + column))
    return pairs


def deliver(values, tile_owner):
    tile_count = tile_owner.shape[0]
    tile_rows = values.shape[0] // tile_count
    all_tiles = values.reshape(tile_count, tile_rows, values.shape[1])
    owner = tile_owner[:, 0]
    order = jnp.arange(tile_count)
    same = (owner[:, None] == owner[None, :]) & (order[None, :] < order[:, None])
    rank = jnp.sum(same.astype(jnp.int32), axis=1)
    select = (
        (owner[None, None, :] == jnp.arange(N_COL)[:, None, None])
        & (rank[None, None, :] == jnp.arange(CAP)[None, :, None])
    ).astype(jnp.float32)
    outgoing = jnp.einsum("cks,srb->ckrb", select, all_tiles, precision=lax.Precision.HIGHEST)
    incoming = lax.all_to_all(outgoing, COL, split_axis=0, concat_axis=0, tiled=True)
    return incoming.reshape(N_COL * CAP, tile_rows, values.shape[1])


def local(
    ancestor_inverse,
    panel_one,
    struct_one,
    lower_one,
    panel_two,
    struct_two,
    panel_above,
    lower_two,
    tile_owner,
):
    row_index = lax.axis_index(ROW)
    col_index = lax.axis_index(COL)
    local_rows, width = panel_one.shape
    start = (row_index * N_COL + col_index) * local_rows
    mask_one = row_mask(struct_one, start, local_rows)
    mask_two = row_mask(struct_two, start, local_rows)
    panels = jnp.concatenate([panel_one * mask_one, panel_two * mask_two], axis=1)
    placed = lax.ppermute(panels, ROW_COL, gather_moves())
    column_panels = lax.all_gather(placed, "row_0", axis=0, tiled=True)
    column_panels = lax.all_gather(column_panels, "row_1", axis=0, tiled=True)
    row_panels = lax.all_gather(panels, COL, axis=0, tiled=True)
    product = dot(ancestor_inverse, column_panels, precision=lax.Precision.HIGH)
    from_one = dot(row_panels[:, :width], product, ((0,), (0,)), lax.Precision.HIGH)
    from_two = dot(row_panels[:, width:], product[:, width:], ((0,), (0,)), lax.Precision.HIGH)
    partial = jnp.concatenate([from_one[:, :width], from_one[:, width:], from_two], axis=0)
    grams = total(partial)
    w_one, w_cross, w_two = grams[:width], grams[width : 2 * width], grams[2 * width :]
    diag_one = dot(lower_one, lower_one, ((0,), (0,))) + w_one
    cross_two = w_cross - dot(diag_one, panel_above)
    diag_two = (
        dot(lower_two, lower_two, ((0,), (0,)))
        + w_two
        - dot(w_cross, panel_above, ((0,), (0,)))
        - dot(panel_above, cross_two, ((0,), (0,)))
    )
    rows = sum_at_owner(product, COL)
    inverse_one = -rows[:, :width] * mask_one
    inverse_two = -(rows[:, width:] + dot(inverse_one, panel_above)) * mask_two
    inverses = lax.ppermute(
        jnp.concatenate([inverse_one, inverse_two], axis=1), ROW_COL, result_moves()
    )
    inverse_one, inverse_two = inverses[:, :width], inverses[:, width:]
    delivered = deliver(inverse_two, tile_owner)
    return (inverse_one, diag_one, cross_two, diag_two, delivered)


def solution(mesh):
    finer = Mesh(mesh.devices.reshape(4, 8, 4, 2), ("row_0", "row_1", "col_0", "col_1"))
    return jax.shard_map(
        local,
        mesh=finer,
        in_specs=(
            P(ROW, COL),
            P(ROW_COL, None),
            P(),
            P(),
            P(ROW_COL, None),
            P(),
            P(),
            P(),
            P(COL_ROW, None),
        ),
        out_specs=(P(COL_ROW, None), P(), P(), P(), P(ROW_COL, None, None)),
        check_vma=False,
    )
```

time: 367 us -> 211 us (0.57)
  local copies, waits for them, and re-layouts: 94.6 us -> 4.43 us
  waiting for transfers between devices: 159 us -> 93.9 us
  blocking collectives: 16.6 us -> 29.4 us
  matrix products: 18.3 us -> 13.3 us
  other arithmetic: 11.9 us -> 7.24 us
    reduce_scatter x2 -> x0, waiting for transfers between devices: 103 us -> none  [summed_rows(): running = lax.psum_scatter(running, axis, scatter_dimension=0, tiled=True)]
    scatter x2 -> x0, local copies, waits for them, and re-layouts: 74 us -> none  [the longest x1 39.8 us: local(): mask_one = jnp.zeros((ANC,), jnp.float32).at[struct_one].set(1.0)]
    all_gather x0 -> x1, waiting for transfers between devices: none -> 34.5 us  [local(): column_panels = lax.all_gather(column_panels, 'row_1', axis=0, tiled=True)]
    all_gather x1 -> x2, blocking collectives: 16.6 us -> 29.4 us  [the longest x1 17 us: local(): row_panels = lax.all_gather(panels, COL, axis=0, tiled=True)]
    all_to_all x8 -> x5, starting transfers between devices: 41.3 us -> 32.3 us  [the longest x3 24.1 us: sum_at_owner(): return jnp.sum(lax.all_to_all(parts, axis, 0, 0, tiled=True), axis=0)]
    all_to_all x8 -> x5, waiting for transfers between devices: 54.1 us -> 46 us  [the longest x3 25.5 us: sum_at_owner(): return jnp.sum(lax.all_to_all(parts, axis, 0, 0, tiled=True), axis=0)]
    ppermute x0 -> x2, waiting for transfers between devices: none -> 8.1 us  [the longest x1 8.1 us: local(): placed = lax.ppermute(panels, ROW_COL, gather_moves())]
    ppermute x0 -> x2, starting transfers between devices: none -> 7.46 us  [the longest x1 4.59 us: local(): placed = lax.ppermute(panels, ROW_COL, gather_moves())]
  transfers between devices with their start and end apart: 11 -> 9, of which waited for: 11 -> 8; matrix products, arithmetic and copies ran while one was open for 4% -> 5% of each run, Pallas kernels for 0% -> 0%
where the time goes in v1:
time: 211 us; the launch traced here: 210 us
  waiting for transfers between devices  93.9 us (45%)
  starting transfers between devices  47.1 us (22%)
  blocking collectives  29.4 us (14%)
  between operations  14.3 us (7%)
  matrix products  13.3 us (6%)
  other arithmetic  7.24 us (3%)
  local copies, waits for them, and re-layouts  4.43 us (2%)
    all_gather x1, waiting for transfers between devices, local(): column_panels = lax.all_gather(column_panels, 'row_1', axis=0, tiled=True)  34.5 us
    all_to_all x3, waiting for transfers between devices, sum_at_owner(): return jnp.sum(lax.all_to_all(parts, axis, 0, 0, tiled=True), axis=0)  25.5 us
    all_to_all x3, starting transfers between devices, sum_at_owner(): return jnp.sum(lax.all_to_all(parts, axis, 0, 0, tiled=True), axis=0)  24.1 us
    all_to_all x2, waiting for transfers between devices, copies_of(): return lax.all_to_all(copies, axis, 0, 0, tiled=True)  20.6 us
    all_gather x1, blocking collectives, local(): row_panels = lax.all_gather(panels, COL, axis=0, tiled=True)  17 us
    dot_general x9, matrix products, dot(): lax.dot_general(left, right, (dims, ((), ())), precision=precision, prefe...  13.1 us
    all_gather x1, blocking collectives, local(): column_panels = lax.all_gather(placed, 'row_0', axis=0, tiled=True)  12.5 us
    all_to_all x2, starting transfers between devices, copies_of(): return lax.all_to_all(copies, axis, 0, 0, tiled=True)  8.17 us
  transfers between devices with their start and end apart: 9, of which 8 were waited for; matrix products, arithmetic and copies ran while one was open for 5% of the time, Pallas kernels for 0%

profile of v1, /device:TPU:1, one launch (start us, length us, event | category | flops | bytes accessed | tf_op | source)
XLA Modules:
  0.0 209.6 jit_solution(13605550530463847932)
XLA Ops:
  7.2 1.3 select_reduce_fusion
  8.6 1.1 select_reduce_fusion.1
  9.7 0.9 broadcast_multiply_fusion
  10.6 4.6 %collective-permute-start = (f32[48,512]{1,0:T(8,128)S(1)}, f32[48,512]{1,0:T(8,128)S(1)}, u32[]{:S(2)}, u32[]{:S(2)}) collective-permute-start(f32[48,512]{1,0:T(8,128)S(1)} %pad_maximum_fusion.1), channel_id=1, source_target_pairs={{0,0},{1,64},{2,128},{3,192},{4,8},{5,72},{6,136},{7,200},{8,16},{... | collective-permute-start | bytes 294920 | tf_op jit(solution)/shard_map/ppermute | solution.py:98
  15.2 8.1 %collective-permute-done = f32[48,512]{1,0:T(8,128)S(1)} collective-permute-done((f32[48,512]{1,0:T(8,128)S(1)}, f32[48,512]{1,0:T(8,128)S(1)}, u32[]{:S(2)}, u32[]{:S(2)}) %collective-permute-start) | collective-permute-done | bytes 98336 | tf_op jit(solution)/shard_map/ppermute | solution.py:98
  23.3 12.5 %all_gather.9 = f32[192,512]{1,0:T(8,128)} all-gather(f32[48,512]{1,0:T(8,128)S(1)} %collective-permute-done), channel_id=1, replica_groups=mesh['row_0'=4,'row_1'=8,'col_0'=4,'col_1'=2] {'row_0'}, dimensions={0}, use_global_device_ids=true | all-gather | bytes 491520 | tf_op jit(solution)/shard_map/all_gather | solution.py:99
  35.8 0.9 convert_reduce_fusion
  37.4 17.0 %all_gather.11 = f32[384,512]{1,0:T(8,128)} all-gather(f32[48,512]{1,0:T(8,128)S(1)} %pad_maximum_fusion.1), channel_id=1, replica_groups=mesh['row_0'=4,'row_1'=8,'col_0'=4,'col_1'=2] {'col_0','col_1'}, dimensions={0}, use_global_device_ids=true | all-gather | bytes 884736 | tf_op jit(solution)/shard_map/all_gather | solution.py:101
  54.4 34.5 %all-gather.2.cloned.1.call-done = f32[1536,512]{1,0:T(8,128)} async-done(((f32[192,512]{1,0:T(8,128)}), f32[1536,512]{1,0:T(8,128)}) %all-gather.2.cloned.1.call-update) | async-done | bytes 3145744 | tf_op jit(solution)/shard_map/all_gather | solution.py:100
  88.8 4.8 %fusion.19 = f32[512,384]{0,1:T(8,128)} fusion(f32[1536,512]{1,0:T(8,128)} %all-gather.2.cloned.1.call-done, f32[384,1536]{1,0:T(8,128)S(1)} %copy-done), kind=kOutput, calls=%fused_computation.39 | convolution fusion | flops 1811939328 | bytes 6291456 | tf_op jit(solution)/shard_map/dot_general | solution.py:24
  93.7 5.2 %all-to-all-start = ((f32[8,48,512]{2,1,0:T(8,128)}), f32[8,48,512]{2,1,0:T(8,128)S(1)}, u32[]{:S(2)}, u32[]{:S(2)}) async-start(f32[8,48,512]{2,1,0:T(8,128)} %bitcast.1), calls=%async_computation | async-start | bytes 1572864 | tf_op jit(solution)/shard_map/all_to_all | solution.py:32
  98.9 1.9 fusion.6
  100.9 1.5 fusion.3
  102.4 0.9 pad_maximum_fusion
  103.3 7.8 %all-to-all-done = f32[8,48,512]{2,1,0:T(8,128)S(1)} async-done(((f32[8,48,512]{2,1,0:T(8,128)}), f32[8,48,512]{2,1,0:T(8,128)S(1)}, u32[]{:S(2)}, u32[]{:S(2)}) %all-to-all-start) | async-done | bytes 786464 | tf_op jit(solution)/shard_map/all_to_all | solution.py:32
  111.1 5.0 %all-to-all-start.1 = ((f32[8,96,256]{2,1,0:T(8,128)}), f32[8,96,256]{2,1,0:T(8,128)}, u32[]{:S(2)}, u32[]{:S(2)}) async-start(f32[8,96,256]{2,1,0:T(8,128)} %bitcast.2), calls=%async_computation.1 | async-start | bytes 1572864 | tf_op jit(solution)/shard_map/all_to_all | solution.py:32
  116.5 2.9 %collective-permute-start.1 = (f32[48,512]{1,0:T(8,128)S(1)}, f32[48,512]{1,0:T(8,128)S(1)}, u32[]{:S(2)}, u32[]{:S(2)}) collective-permute-start(f32[48,512]{1,0:T(8,128)S(1)} %pad_maximum_fusion.2), channel_id=1, source_target_pairs={{0,0},{1,8},{2,16},{3,24},{4,32},{5,40},{6,48},{7,56},{8,64},{9,72... | collective-permute-start | bytes 294920 | tf_op jit(solution)/shard_map/ppermute | solution.py:119
  119.4 9.1 %all-to-all-done.1 = f32[8,96,256]{2,1,0:T(8,128)} async-done(((f32[8,96,256]{2,1,0:T(8,128)}), f32[8,96,256]{2,1,0:T(8,128)}, u32[]{:S(2)}, u32[]{:S(2)}) %all-to-all-start.1) | async-done | bytes 786464 | tf_op jit(solution)/shard_map/all_to_all | solution.py:32
  128.5 1.2 reduce_sum.37
  129.7 0.7 reshape.90
  130.4 14.0 %all-to-all-start.2 = ((f32[32,3,256]{2,1,0:T(4,128)}), f32[32,3,256]{2,1,0:T(4,128)S(1)}, u32[]{:S(2)}, u32[]{:S(2)}) async-start(f32[32,3,256]{2,1,0:T(4,128)} %reshape.90), calls=%async_computation.2 | async-start | bytes 262144 | tf_op jit(solution)/shard_map/all_to_all | solution.py:32
  145.1 8.5 %all-to-all-done.2 = f32[32,3,256]{2,1,0:T(4,128)S(1)} async-done(((f32[32,3,256]{2,1,0:T(4,128)}), f32[32,3,256]{2,1,0:T(4,128)S(1)}, u32[]{:S(2)}, u32[]{:S(2)}) %all-to-all-start.2) | async-done | bytes 98336 | tf_op jit(solution)/shard_map/all_to_all | solution.py:32
  154.3 3.9 %all-to-all-start.3 = ((f32[32,3,256]{2,1,0:T(4,128)}), f32[32,3,256]{2,1,0:T(4,128)S(1)}, u32[]{:S(2)}, u32[]{:S(2)}) async-start(f32[32,3,256]{2,1,0:T(4,128)} %broadcast_in_dim.44), calls=%async_computation.3 | async-start | bytes 262144 | tf_op jit(solution)/shard_map/all_to_all | solution.py:37
  158.4 0.7 copy.24
  159.1 8.3 %all-to-all-done.3 = f32[32,3,256]{2,1,0:T(4,128)S(1)} async-done(((f32[32,3,256]{2,1,0:T(4,128)}), f32[32,3,256]{2,1,0:T(4,128)S(1)}, u32[]{:S(2)}, u32[]{:S(2)}) %all-to-all-start.3) | async-done | bytes 98336 | tf_op jit(solution)/shard_map/all_to_all | solution.py:37
  167.3 7.3 %all-to-all-start.5 = ((f32[8,2,8,256]{3,2,1,0:T(8,128)}), f32[8,2,8,256]{3,2,1,0:T(8,128)S(1)}, u32[]{:S(2)}, u32[]{:S(2)}) async-start(f32[8,2,8,256]{3,2,1,0:T(8,128)} %copy.24), calls=%async_computation.5 | async-start | bytes 262144 | tf_op jit(solution)/shard_map/all_to_all | solution.py:76
  174.7 5.2 %all-to-all-done.5 = f32[8,2,8,256]{3,2,1,0:T(8,128)S(1)} async-done(((f32[8,2,8,256]{3,2,1,0:T(8,128)}), f32[8,2,8,256]{3,2,1,0:T(8,128)S(1)}, u32[]{:S(2)}, u32[]{:S(2)}) %all-to-all-start.5) | async-done | bytes 131104 | tf_op jit(solution)/shard_map/all_to_all | solution.py:76
  179.9 1.0 broadcast_in_dim.46
  180.9 4.3 %all-to-all-start.4 = ((f32[8,96,256]{2,1,0:T(8,128)}), f32[8,96,256]{2,1,0:T(8,128)S(1)}, u32[]{:S(2)}, u32[]{:S(2)}) async-start(f32[8,96,256]{2,1,0:T(8,128)} %broadcast_in_dim.46), calls=%async_computation.4 | async-start | bytes 1572864 | tf_op jit(solution)/shard_map/all_to_all | solution.py:37
  185.2 12.3 %all-to-all-done.4 = f32[8,96,256]{2,1,0:T(8,128)S(1)} async-done(((f32[8,96,256]{2,1,0:T(8,128)}), f32[8,96,256]{2,1,0:T(8,128)S(1)}, u32[]{:S(2)}, u32[]{:S(2)}) %all-to-all-start.4) | async-done | bytes 786464 | tf_op jit(solution)/shard_map/all_to_all | solution.py:37
  197.5 1.7 convolution_add_fusion
  200.8 1.3 fusion
  (33 shorter events, 5.0 us)
Async XLA Ops:
  7.2 81.7 %copy-start = (f32[384,1536]{1,0:T(8,128)S(1)}, f32[384,1536]{1,0:T(8,128)}, u32[]{:S(2)}) copy-start(f32[384,1536]{1,0:T(8,128)} %param.9) | copy-start | bytes 7077892
  7.2 81.7 %all-gather.2.cloned.1.call-start = ((), (), s32[]{:S(2)}) async-start(), calls=%async_computation.6 | async-start | bytes 3538944 | tf_op jit(solution)/shard_map/all_gather | solution.py:100
  10.6 12.7 %collective-permute-start = (f32[48,512]{1,0:T(8,128)S(1)}, f32[48,512]{1,0:T(8,128)S(1)}, u32[]{:S(2)}, u32[]{:S(2)}) collective-permute-start(f32[48,512]{1,0:T(8,128)S(1)} %pad_maximum_fusion.1), channel_id=1, source_target_pairs={{0,0},{1,64},{2,128},{3,192},{4,8},{5,72},{6,136},{7,200},{8,16},{... | collective-permute-start | bytes 294920 | tf_op jit(solution)/shard_map/ppermute | solution.py:98
  93.7 17.4 %all-to-all-start = ((f32[8,48,512]{2,1,0:T(8,128)}), f32[8,48,512]{2,1,0:T(8,128)S(1)}, u32[]{:S(2)}, u32[]{:S(2)}) async-start(f32[8,48,512]{2,1,0:T(8,128)} %bitcast.1), calls=%async_computation | async-start | bytes 1572864 | tf_op jit(solution)/shard_map/all_to_all | solution.py:32
  98.9 2.0 copy-start.2
  102.4 13.9 %copy-start.1 = (f32[256,256]{1,0:T(8,128)S(1)}, f32[256,256]{1,0:T(8,128)}, u32[]{:S(2)}) copy-start(f32[256,256]{1,0:T(8,128)} %param.15) | copy-start | bytes 786436
  111.1 17.4 %all-to-all-start.1 = ((f32[8,96,256]{2,1,0:T(8,128)}), f32[8,96,256]{2,1,0:T(8,128)}, u32[]{:S(2)}, u32[]{:S(2)}) async-start(f32[8,96,256]{2,1,0:T(8,128)} %bitcast.2), calls=%async_computation.1 | async-start | bytes 1572864 | tf_op jit(solution)/shard_map/all_to_all | solution.py:32
  116.5 27.9 %collective-permute-start.1 = (f32[48,512]{1,0:T(8,128)S(1)}, f32[48,512]{1,0:T(8,128)S(1)}, u32[]{:S(2)}, u32[]{:S(2)}) collective-permute-start(f32[48,512]{1,0:T(8,128)S(1)} %pad_maximum_fusion.2), channel_id=1, source_target_pairs={{0,0},{1,8},{2,16},{3,24},{4,32},{5,40},{6,48},{7,56},{8,64},{9,72... | collective-permute-start | bytes 294920 | tf_op jit(solution)/shard_map/ppermute | solution.py:119
  130.4 23.2 %all-to-all-start.2 = ((f32[32,3,256]{2,1,0:T(4,128)}), f32[32,3,256]{2,1,0:T(4,128)S(1)}, u32[]{:S(2)}, u32[]{:S(2)}) async-start(f32[32,3,256]{2,1,0:T(4,128)} %reshape.90), calls=%async_computation.2 | async-start | bytes 262144 | tf_op jit(solution)/shard_map/all_to_all | solution.py:32
  154.3 13.0 %all-to-all-start.3 = ((f32[32,3,256]{2,1,0:T(4,128)}), f32[32,3,256]{2,1,0:T(4,128)S(1)}, u32[]{:S(2)}, u32[]{:S(2)}) async-start(f32[32,3,256]{2,1,0:T(4,128)} %broadcast_in_dim.44), calls=%async_computation.3 | async-start | bytes 262144 | tf_op jit(solution)/shard_map/all_to_all | solution.py:37
  167.3 12.6 %all-to-all-start.5 = ((f32[8,2,8,256]{3,2,1,0:T(8,128)}), f32[8,2,8,256]{3,2,1,0:T(8,128)S(1)}, u32[]{:S(2)}, u32[]{:S(2)}) async-start(f32[8,2,8,256]{3,2,1,0:T(8,128)} %copy.24), calls=%async_computation.5 | async-start | bytes 262144 | tf_op jit(solution)/shard_map/all_to_all | solution.py:76
  180.9 16.6 %all-to-all-start.4 = ((f32[8,96,256]{2,1,0:T(8,128)}), f32[8,96,256]{2,1,0:T(8,128)S(1)}, u32[]{:S(2)}, u32[]{:S(2)}) async-start(f32[8,96,256]{2,1,0:T(8,128)} %broadcast_in_dim.46), calls=%async_computation.4 | async-start | bytes 1572864 | tf_op jit(solution)/shard_map/all_to_all | solution.py:37
  197.5 2.3 %copy-start.3 = (f32[256,256]{1,0:T(8,128)S(1)}, f32[256,256]{1,0:T(8,128)}, u32[]{:S(2)}) copy-start(f32[256,256]{1,0:T(8,128)} %param.12) | copy-start | bytes 786436
  200.4 2.4 %copy-start.4 = (f32[256,256]{1,0:T(8,128)}, f32[256,256]{1,0:T(8,128)S(1)}, u32[]{:S(2)}) copy-start(f32[256,256]{1,0:T(8,128)S(1)} %convolution_add_fusion.1) | copy-start | bytes 786436
  200.8 2.0 copy-start.5
Sparse Core Ops, SparseCore 0:
  35.9 52.8 all-gather.1

commit v2 on v1

v2 whole, which is shorter than its diff:
```python
import jax
import jax.numpy as jnp
from jax import lax
from jax.experimental import pallas as pl
from jax.experimental.pallas import tpu as pltpu
from jax.sharding import Mesh
from jax.sharding import PartitionSpec as P

CAP = 2
COL = ("col_0", "col_1")
ROW = ("row_0", "row_1")
ROW_COL = ROW + COL
COL_ROW = COL + ROW
PLANE = ("row_0", "col_0")
N_Y, N_Z, N_X, N_K = 4, 8, 4, 2
N_ROW, N_COL = N_Y * N_Z, N_X * N_K
ROWS = 48
WIDTH = 256


def device(y, z, x, k):
    return ((y * N_Z + z) * N_X + x) * N_K + k


def moves(place):
    return [
        (device(y, z, x, k), device(*place(y, z, x, k)))
        for y in range(N_Y)
        for z in range(N_Z)
        for x in range(N_X)
        for k in range(N_K)
    ]


def to_column(step):
    return moves(lambda y, z, x, k: ((x + step) % N_Y, 2 * (z % 4) + k, y, z // 4))


def result_place(y, z, x, k):
    column, row = divmod((y * N_Z + z) * N_COL + x * N_K + k, N_ROW)
    return (row // N_Z, row % N_Z, column // N_K, column % N_K)


def along_y(step):
    return moves(lambda y, z, x, k: ((y + step) % N_Y, z, x, k))


def other_core():
    return moves(lambda y, z, x, k: (y, z, x, 1 - k))


def row_mask(listed, start, count):
    rows = start + jnp.arange(count, dtype=jnp.int32)
    hit = listed[None, :] == rows[:, None]
    return jnp.max(jnp.where(hit, 1.0, 0.0), axis=1, keepdims=True)


def dot(left, right, dims=((1,), (0,)), precision=lax.Precision.HIGHEST):
    return lax.dot_general(
        left, right, (dims, ((), ())), precision=precision, preferred_element_type=jnp.float32
    )


def split(value):
    high = value.astype(jnp.bfloat16)
    return high, (value - high.astype(jnp.float32)).astype(jnp.bfloat16)


def three_pass(left, right, dims):
    (a, b), (c, d) = left, right

    def one(p, q):
        return lax.dot_general(p, q, (dims, ((), ())), preferred_element_type=jnp.float32)

    return one(a, c) + (one(a, d) + one(b, c))


def product_kernel(
    place, a_ref, g0_ref, g1_ref, g2_ref, g3_ref, own_ref, other_ref,
    w_keep, w_send, y_keep, y_send, xh, xl, rh, rl, w_all, y_all,
):
    y, k = place[0], place[1]
    for step, g_ref in enumerate((g0_ref, g1_ref, g2_ref, g3_ref)):
        x = lax.rem(y + step, N_X)
        for q in range(4):
            high, low = split(g_ref[pl.ds(q * 96, 96), :])
            at = pl.multiple_of(q * 384 + x * 96, 32)
            xh[pl.ds(at, 96), :] = high
            xl[pl.ds(at, 96), :] = low
    for x in range(N_X):
        for ref, core in ((own_ref, k), (other_ref, 1 - k)):
            high, low = split(ref[x])
            at = pl.multiple_of((x * N_K + core) * ROWS, 16)
            rh[pl.ds(at, ROWS), :] = high
            rl[pl.ds(at, ROWS), :] = low
    product = three_pass(split(a_ref[...]), (xh[...], xl[...]), ((1,), (0,)))
    for block in range(N_COL):
        y_all[block] = product[block * ROWS : (block + 1) * ROWS]
    high, low = split(product)
    rows_dims = ((0,), (0,))
    one = (rh[:, :WIDTH], rl[:, :WIDTH])
    two = (rh[:, WIDTH:], rl[:, WIDTH:])
    from_one = three_pass(one, (high, low), rows_dims)
    w_all[0:WIDTH, :] = from_one[:, :WIDTH]
    w_all[WIDTH : 2 * WIDTH, :] = from_one[:, WIDTH:]
    w_all[2 * WIDTH :, :] = three_pass(two, (high[:, WIDTH:], low[:, WIDTH:]), rows_dims)
    half = 3 * WIDTH // 2
    w_keep[...] = w_all[pl.ds(pl.multiple_of(k * half, 128), half), :]
    w_send[...] = w_all[pl.ds(pl.multiple_of((1 - k) * half, 128), half), :]
    for x in range(N_X):
        y_keep[x] = y_all[x * N_K + k]
        y_send[x] = y_all[x * N_K + 1 - k]


def product_and_grams(place, ancestor, gathered, own, other):
    f32, bf16 = jnp.float32, jnp.bfloat16
    half = 3 * WIDTH // 2
    wide = 2 * WIDTH
    vmem = pl.BlockSpec(memory_space=pltpu.VMEM)
    return pl.pallas_call(
        product_kernel,
        in_specs=[pl.BlockSpec(memory_space=pltpu.SMEM)] + [vmem] * 7,
        out_specs=[vmem] * 4,
        out_shape=[
            jax.ShapeDtypeStruct((half, WIDTH), f32),
            jax.ShapeDtypeStruct((half, WIDTH), f32),
            jax.ShapeDtypeStruct((N_X, ROWS, wide), f32),
            jax.ShapeDtypeStruct((N_X, ROWS, wide), f32),
        ],
        scratch_shapes=[
            pltpu.VMEM((1536, wide), bf16),
            pltpu.VMEM((1536, wide), bf16),
            pltpu.VMEM((384, wide), bf16),
            pltpu.VMEM((384, wide), bf16),
            pltpu.VMEM((3 * WIDTH, WIDTH), f32),
            pltpu.VMEM((N_COL, ROWS, wide), f32),
        ],
        compiler_params=pltpu.CompilerParams(vmem_limit_bytes=48 * 1024 * 1024),
        name="product_and_grams",
    )(place, ancestor, *gathered, own, other)


def at_owner(value, axis):
    count = lax.axis_size(axis)
    parts = value.reshape(count, value.shape[0] // count, *value.shape[1:])
    return lax.all_to_all(parts, axis, 0, 0, tiled=True)


def copies_of(value, axis):
    copies = jnp.broadcast_to(value[None], (lax.axis_size(axis), *value.shape))
    return lax.all_to_all(copies, axis, 0, 0, tiled=True)


def selection(tile_owner):
    tile_count = tile_owner.shape[0]
    owner = tile_owner[:, 0]
    order = jnp.arange(tile_count)
    same = (owner[:, None] == owner[None, :]) & (order[None, :] < order[:, None])
    rank = jnp.sum(same.astype(jnp.int32), axis=1)
    return (
        (owner[None, None, :] == jnp.arange(N_COL)[:, None, None])
        & (rank[None, None, :] == jnp.arange(CAP)[None, :, None])
    ).astype(jnp.float32)


def deliver(values, select):
    tile_count = select.shape[2]
    tile_rows = values.shape[0] // tile_count
    all_tiles = values.reshape(tile_count, tile_rows, values.shape[1])
    outgoing = jnp.einsum("cks,srb->ckrb", select, all_tiles, precision=lax.Precision.HIGHEST)
    incoming = lax.all_to_all(outgoing, COL, split_axis=0, concat_axis=0, tiled=True)
    return incoming.reshape(N_COL * CAP, tile_rows, values.shape[1])


def local(
    ancestor_inverse,
    panel_one,
    struct_one,
    lower_one,
    panel_two,
    struct_two,
    panel_above,
    lower_two,
    tile_owner,
):
    start = (lax.axis_index(ROW) * N_COL + lax.axis_index(COL)) * ROWS
    mask_one = row_mask(struct_one, start, ROWS)
    mask_two = row_mask(struct_two, start, ROWS)
    panels = jnp.concatenate([panel_one * mask_one, panel_two * mask_two], axis=1)
    block = lax.ppermute(panels, ROW_COL, to_column(0))
    far_block = lax.ppermute(panels, ROW_COL, to_column(2))
    own_core = lax.all_gather(panels, "col_0", axis=0)
    next_core = lax.ppermute(own_core, ROW_COL, other_core())
    gathered = lax.all_gather(block, "row_1", axis=0, tiled=True)
    above = lax.ppermute(gathered, ROW_COL, along_y(-1))
    below = lax.ppermute(gathered, ROW_COL, along_y(1))
    far_block, _ = lax.optimization_barrier((far_block, gathered))
    far = lax.all_gather(far_block, "row_1", axis=0, tiled=True)
    place = jnp.stack([lax.axis_index("row_0"), lax.axis_index("col_1")]).astype(jnp.int32)
    w_keep, w_send, y_keep, y_send = product_and_grams(
        place, ancestor_inverse, (gathered, above, far, below), own_core, next_core
    )
    w_own = w_keep + lax.ppermute(w_send, ROW_COL, other_core())
    y_own = y_keep + lax.ppermute(y_send, ROW_COL, other_core())
    w_part = jnp.sum(at_owner(w_own, PLANE), axis=0)
    w_part = jnp.sum(copies_of(w_part, "row_1"), axis=0)
    w_half = copies_of(w_part, PLANE).reshape(w_own.shape)
    w_other = lax.ppermute(w_half, ROW_COL, other_core())
    first = lax.axis_index("col_1") == 0
    grams = jnp.concatenate(
        [jnp.where(first, w_half, w_other), jnp.where(first, w_other, w_half)], axis=0
    )
    w_one, w_cross, w_two = grams[:WIDTH], grams[WIDTH : 2 * WIDTH], grams[2 * WIDTH :]
    diag_one = dot(lower_one, lower_one, ((0,), (0,))) + w_one
    cross_two = w_cross - dot(diag_one, panel_above)
    diag_two = (
        dot(lower_two, lower_two, ((0,), (0,)))
        + w_two
        - dot(w_cross, panel_above, ((0,), (0,)))
        - dot(panel_above, cross_two, ((0,), (0,)))
    )
    rows = jnp.sum(lax.all_to_all(y_own, "col_0", 0, 0, tiled=True), axis=0)
    inverse_one = -rows[:, :WIDTH] * mask_one
    inverse_two = -(rows[:, WIDTH:] + dot(inverse_one, panel_above)) * mask_two
    inverses = lax.ppermute(
        jnp.concatenate([inverse_one, inverse_two], axis=1), ROW_COL, moves(result_place)
    )
    inverse_one, inverse_two = inverses[:, :WIDTH], inverses[:, WIDTH:]
    delivered = deliver(inverse_two, selection(tile_owner))
    return (inverse_one, diag_one, cross_two, diag_two, delivered)


def solution(mesh):
    finer = Mesh(mesh.devices.reshape(4, 8, 4, 2), ("row_0", "row_1", "col_0", "col_1"))
    return jax.shard_map(
        local,
        mesh=finer,
        in_specs=(
            P(ROW, COL),
            P(ROW_COL, None),
            P(),
            P(),
            P(ROW_COL, None),
            P(),
            P(),
            P(),
            P(COL_ROW, None),
        ),
        out_specs=(P(COL_ROW, None), P(), P(), P(), P(ROW_COL, None, None)),
        check_vma=False,
    )
```

time: 211 us -> 174 us (0.82)
  waiting for transfers between devices: 93.9 us -> 39.4 us
  blocking collectives: 29.4 us -> 53.5 us
  between operations: 14.3 us -> 0.93 us
  starting transfers between devices: 47.1 us -> 60.4 us
  matrix products: 13.3 us -> 3.92 us
  Pallas kernels: 0 us -> 5.07 us
    all_gather x1 -> x0, waiting for transfers between devices: 34.5 us -> none  [local(): column_panels = lax.all_gather(column_panels, 'row_1', axis=0, tiled=True)]
    ppermute x1 -> x8, starting transfers between devices: 4.59 us -> 35.9 us  [the longest x1 12.7 us: local(): far_block = lax.ppermute(panels, ROW_COL, to_column(2))]
    all_gather x2 -> x3, blocking collectives: 29.4 us -> 53.5 us  [the longest x1 20.5 us: local(): far = lax.all_gather(far_block, 'row_1', axis=0, tiled=True)]
    all_to_all x3 -> x2, starting transfers between devices: 24.1 us -> 7.01 us  [the longest x1 3.55 us: at_owner(): return lax.all_to_all(parts, axis, 0, 0, tiled=True)]
    all_to_all x2, waiting for transfers between devices: 20.6 us -> 10.6 us  [copies_of(): return lax.all_to_all(copies, axis, 0, 0, tiled=True)]
    all_to_all x3 -> x2, waiting for transfers between devices: 25.5 us -> 15.5 us  [the longest x1 8.55 us: at_owner(): return lax.all_to_all(parts, axis, 0, 0, tiled=True)]
    dot_general x9 -> x6, matrix products: 13.1 us -> 3.72 us  [dot(): lax.dot_general(left, right, (dims, ((), ())), precision=precision, prefe...]
    pallas_call x0 -> x1, Pallas kernels: none -> 5.07 us  [product_and_grams(): pl.pallas_call(product_kernel, in_specs=[pl.BlockSpec(memory_space=pltpu....]
  transfers between devices with their start and end apart: 9 -> 14, of which waited for: 8 -> 7; matrix products, arithmetic and copies ran while one was open for 5% -> 3% of each run, Pallas kernels for 0% -> 0%
where the time goes in v2:
time: 174 us; the launch traced here: 172 us
  starting transfers between devices  60.4 us (35%)
  blocking collectives  53.5 us (31%)
  waiting for transfers between devices  39.4 us (23%)
  other arithmetic  5.31 us (3%)
  Pallas kernels  5.07 us (3%)
  matrix products  3.92 us (2%)
  local copies, waits for them, and re-layouts  3.48 us (2%)
    all_gather x1, blocking collectives, local(): far = lax.all_gather(far_block, 'row_1', axis=0, tiled=True)  20.5 us
    all_gather x1, blocking collectives, local(): gathered = lax.all_gather(block, 'row_1', axis=0, tiled=True)  20.4 us
    ppermute x1, starting transfers between devices, local(): far_block = lax.ppermute(panels, ROW_COL, to_column(2))  12.7 us
    all_gather x1, blocking collectives, local(): own_core = lax.all_gather(panels, 'col_0', axis=0)  12.6 us
    all_to_all x2, waiting for transfers between devices, copies_of(): return lax.all_to_all(copies, axis, 0, 0, tiled=True)  10.6 us
    all_to_all x1, waiting for transfers between devices, at_owner(): return lax.all_to_all(parts, axis, 0, 0, tiled=True)  8.55 us
    all_to_all x2, starting transfers between devices, copies_of(): return lax.all_to_all(copies, axis, 0, 0, tiled=True)  8.47 us
    ppermute x1, waiting for transfers between devices, local(): block = lax.ppermute(panels, ROW_COL, to_column(0))  7.56 us
  transfers between devices with their start and end apart: 14, of which 7 were waited for; matrix products, arithmetic and copies ran while one was open for 3% of the time, Pallas kernels for 0%

profile of v2, /device:TPU:1, one launch (start us, length us, event | category | flops | bytes accessed | tf_op | source)
XLA Modules:
  0.0 172.1 jit_solution(3301253777757111050)
XLA Ops:
  0.7 1.2 select_reduce_fusion
  1.9 1.1 select_reduce_fusion.1
  3.0 0.9 broadcast_multiply_fusion
  3.9 4.9 %collective-permute-start = (f32[48,512]{1,0:T(8,128)S(1)}, f32[48,512]{1,0:T(8,128)S(1)}, u32[]{:S(2)}, u32[]{:S(2)}) collective-permute-start(f32[48,512]{1,0:T(8,128)S(1)} %pad_maximum_fusion.1), channel_id=1, source_target_pairs={{0,0},{1,8},{2,64},{3,72},{4,128},{5,136},{6,192},{7,200},{8,16},{... | collective-permute-start | bytes 294920 | tf_op jit(solution)/shard_map/ppermute | solution.py:190
  8.9 7.6 %collective-permute-done = f32[48,512]{1,0:T(8,128)S(1)} collective-permute-done((f32[48,512]{1,0:T(8,128)S(1)}, f32[48,512]{1,0:T(8,128)S(1)}, u32[]{:S(2)}, u32[]{:S(2)}) %collective-permute-start) | collective-permute-done | bytes 98336 | tf_op jit(solution)/shard_map/ppermute | solution.py:190
  16.4 20.4 %all_gather.12.g0_ref = f32[384,512]{1,0:T(8,128)S(1)} all-gather(f32[48,512]{1,0:T(8,128)S(1)} %collective-permute-done), channel_id=1, replica_groups=mesh['row_0'=4,'row_1'=8,'col_0'=4,'col_1'=2] {'row_1'}, dimensions={0}, use_global_device_ids=true | all-gather | bytes 884736 | tf_op jit(solution)/shard_map/all_gather | solution.py:194
  36.8 6.3 %collective-permute-start.1 = (f32[384,512]{1,0:T(8,128)S(1)}, f32[384,512]{1,0:T(8,128)S(1)}, u32[]{:S(2)}, u32[]{:S(2)}) collective-permute-start(f32[384,512]{1,0:T(8,128)S(1)} %all_gather.12.g0_ref), channel_id=1, source_target_pairs={{0,192},{1,193},{2,194},{3,195},{4,196},{5,197},{6,198},{7,199},{8... | collective-permute-start | bytes 2359304 | tf_op jit(solution)/shard_map/ppermute | solution.py:195
  43.1 12.7 %collective-permute-start.2 = (f32[48,512]{1,0:T(8,128)S(1)}, f32[48,512]{1,0:T(8,128)S(1)}, u32[]{:S(2)}, u32[]{:S(2)}) collective-permute-start(f32[48,512]{1,0:T(8,128)S(1)} %pad_maximum_fusion.1), channel_id=1, source_target_pairs={{0,128},{1,136},{2,192},{3,200},{4,0},{5,8},{6,64},{7,72},{8,144},... | collective-permute-start | bytes 294920 | tf_op jit(solution)/shard_map/ppermute | solution.py:191
  55.8 12.6 %all-gather = f32[192,512]{1,0:T(8,128)S(1)} all-gather(f32[48,512]{1,0:T(8,128)S(1)} %pad_maximum_fusion.1), channel_id=2, replica_groups=mesh['row_0'=4,'row_1'=8,'col_0'=4,'col_1'=2] {'col_0'}, dimensions={0}, use_global_device_ids=true | all-gather | bytes 491520 | tf_op jit(solution)/shard_map/all_gather | solution.py:192
  68.5 3.2 %collective-permute-start.4 = (f32[4,48,512]{2,1,0:T(8,128)S(1)}, f32[4,48,512]{2,1,0:T(8,128)S(1)}, u32[]{:S(2)}, u32[]{:S(2)}) collective-permute-start(f32[4,48,512]{2,1,0:T(8,128)S(1)} %bitcast.32), channel_id=1, source_target_pairs={{0,1},{1,0},{2,3},{3,2},{4,5},{5,4},{6,7},{7,6},{8,9},{9,8},{10,11... | collective-permute-start | bytes 1179656 | tf_op jit(solution)/shard_map/ppermute | solution.py:193
  71.7 20.5 %all_gather.13.g2_ref = f32[384,512]{1,0:T(8,128)S(1)} all-gather(f32[48,512]{1,0:T(8,128)S(1)} %collective-permute-done.2), channel_id=1, replica_groups=mesh['row_0'=4,'row_1'=8,'col_0'=4,'col_1'=2] {'row_1'}, dimensions={0}, use_global_device_ids=true | all-gather | bytes 884736 | tf_op jit(solution)/shard_map/all_gather | solution.py:198
  92.3 5.1 %product_and_grams.1 = (f32[384,256]{1,0:T(8,128)S(1)}, f32[384,256]{1,0:T(8,128)S(1)}, f32[4,48,512]{2,1,0:T(8,128)S(1)}, f32[4,48,512]{2,1,0:T(8,128)S(1)}) custom-call(s32[2]{0:T(128)S(1)} %pad_add_fusion.place, f32[384,1536]{1,0:T(8,128)} %a_ref.1, f32[384,512]{1,0:T(8,128)S(1)} %all_gather.12.g0_ref, f32[384,512]{1,0:T(8,128)S(1)} %collective-permute-done.1.g1_ref, ...), custom_call_target="tpu_custom_call" | custom-call | tf_op jit(solution)/shard_map/product_and_grams/pallas_call | solution.py:120
  97.4 5.6 %collective-permute-start.5 = (f32[4,48,512]{2,1,0:T(8,128)S(1)}, f32[4,48,512]{2,1,0:T(8,128)S(1)}, u32[]{:S(2)}, u32[]{:S(2)}) collective-permute-start(f32[4,48,512]{2,1,0:T(8,128)S(1)} %get-tuple-element.12), channel_id=1, source_target_pairs={{0,1},{1,0},{2,3},{3,2},{4,5},{5,4},{6,7},{7,6},{8,9},{9,8},{10,11... | collective-permute-start | bytes 1179656 | tf_op jit(solution)/shard_map/ppermute | solution.py:204
  103.1 1.2 collective-permute-done.5
  104.3 0.8 add.41
  105.1 3.5 %all-to-all-start = ((f32[4,48,512]{2,1,0:T(8,128)}), f32[4,48,512]{2,1,0:T(8,128)S(1)}, u32[]{:S(2)}, u32[]{:S(2)}) async-start(f32[4,48,512]{2,1,0:T(8,128)} %add.41), calls=%async_computation | async-start | bytes 786432 | tf_op jit(solution)/shard_map/all_to_all | solution.py:222
  108.6 0.8 add.43
  109.4 7.0 %all-to-all-done = f32[4,48,512]{2,1,0:T(8,128)S(1)} async-done(((f32[4,48,512]{2,1,0:T(8,128)}), f32[4,48,512]{2,1,0:T(8,128)S(1)}, u32[]{:S(2)}, u32[]{:S(2)}) %all-to-all-start) | async-done | bytes 393248 | tf_op jit(solution)/shard_map/all_to_all | solution.py:222
  116.4 3.6 %all-to-all-start.1 = ((f32[16,24,256]{2,1,0:T(8,128)}), f32[16,24,256]{2,1,0:T(8,128)S(1)}, u32[]{:S(2)}, u32[]{:S(2)}) async-start(f32[16,24,256]{2,1,0:T(8,128)} %bitcast.3), calls=%async_computation.1 | async-start | bytes 786432 | tf_op jit(solution)/shard_map/all_to_all | solution.py:146
  120.3 8.6 %all-to-all-done.1 = f32[16,24,256]{2,1,0:T(8,128)S(1)} async-done(((f32[16,24,256]{2,1,0:T(8,128)}), f32[16,24,256]{2,1,0:T(8,128)S(1)}, u32[]{:S(2)}, u32[]{:S(2)}) %all-to-all-start.1) | async-done | bytes 393248 | tf_op jit(solution)/shard_map/all_to_all | solution.py:146
  128.8 0.7 broadcast_in_dim.24
  129.5 3.4 %all-to-all-start.2 = ((f32[8,24,256]{2,1,0:T(8,128)}), f32[8,24,256]{2,1,0:T(8,128)S(1)}, u32[]{:S(2)}, u32[]{:S(2)}) async-start(f32[8,24,256]{2,1,0:T(8,128)} %broadcast_in_dim.24), calls=%async_computation.2 | async-start | bytes 393216 | tf_op jit(solution)/shard_map/all_to_all | solution.py:151
  133.2 5.5 %collective-permute-start.6 = (f32[48,512]{1,0:T(8,128)S(1)}, f32[48,512]{1,0:T(8,128)S(1)}, u32[]{:S(2)}, u32[]{:S(2)}) collective-permute-start(f32[48,512]{1,0:T(8,128)S(1)} %pad_maximum_fusion.2), channel_id=1, source_target_pairs={{0,0},{1,8},{2,16},{3,24},{4,32},{5,40},{6,48},{7,56},{8,64},{9,72... | collective-permute-start | bytes 294920 | tf_op jit(solution)/shard_map/ppermute | solution.py:225
  138.8 2.8 %all-to-all-done.2 = f32[8,24,256]{2,1,0:T(8,128)S(1)} async-done(((f32[8,24,256]{2,1,0:T(8,128)}), f32[8,24,256]{2,1,0:T(8,128)S(1)}, u32[]{:S(2)}, u32[]{:S(2)}) %all-to-all-start.2) | async-done | bytes 196640 | tf_op jit(solution)/shard_map/all_to_all | solution.py:151
  141.5 0.8 broadcast_in_dim.25
  142.3 5.1 %all-to-all-start.3 = ((f32[16,24,256]{2,1,0:T(8,128)}), f32[16,24,256]{2,1,0:T(8,128)S(1)}, u32[]{:S(2)}, u32[]{:S(2)}) async-start(f32[16,24,256]{2,1,0:T(8,128)} %broadcast_in_dim.25), calls=%async_computation.3 | async-start | bytes 786432 | tf_op jit(solution)/shard_map/all_to_all | solution.py:151
  148.0 7.8 %all-to-all-done.3 = f32[16,24,256]{2,1,0:T(8,128)S(1)} async-done(((f32[16,24,256]{2,1,0:T(8,128)}), f32[16,24,256]{2,1,0:T(8,128)S(1)}, u32[]{:S(2)}, u32[]{:S(2)}) %all-to-all-start.3) | async-done | bytes 393248 | tf_op jit(solution)/shard_map/all_to_all | solution.py:151
  155.9 3.1 %collective-permute-start.8 = (f32[384,256]{1,0:T(8,128)S(1)}, f32[384,256]{1,0:T(8,128)S(1)}, u32[]{:S(2)}, u32[]{:S(2)}) collective-permute-start(f32[384,256]{1,0:T(8,128)S(1)} %bitcast.34), channel_id=1, source_target_pairs={{0,1},{1,0},{2,3},{3,2},{4,5},{5,4},{6,7},{7,6},{8,9},{9,8},{10,11... | collective-permute-start | bytes 1179656 | tf_op jit(solution)/shard_map/ppermute | solution.py:208
  159.1 0.7 copy.24
  159.8 3.5 %all-to-all-start.4 = ((f32[8,2,8,256]{3,2,1,0:T(8,128)}), f32[8,2,8,256]{3,2,1,0:T(8,128)S(1)}, u32[]{:S(2)}, u32[]{:S(2)}) async-start(f32[8,2,8,256]{3,2,1,0:T(8,128)} %copy.24), calls=%async_computation.4 | async-start | bytes 262144 | tf_op jit(solution)/shard_map/all_to_all | solution.py:171
  163.9 4.4 %all-to-all-done.4 = f32[8,2,8,256]{3,2,1,0:T(8,128)S(1)} async-done(((f32[8,2,8,256]{3,2,1,0:T(8,128)}), f32[8,2,8,256]{3,2,1,0:T(8,128)S(1)}, u32[]{:S(2)}, u32[]{:S(2)}) %all-to-all-start.4) | async-done | bytes 131104 | tf_op jit(solution)/shard_map/all_to_all | solution.py:171
  170.1 1.3 fusion.1
  (41 shorter events, 4.5 us)
Async XLA Ops:
  0.6 132.3 %copy-start = (f32[256,256]{1,0:T(8,128)S(1)}, f32[256,256]{1,0:T(8,128)}, u32[]{:S(2)}) copy-start(f32[256,256]{1,0:T(8,128)} %param.15) | copy-start | bytes 786436
  3.9 12.5 %collective-permute-start = (f32[48,512]{1,0:T(8,128)S(1)}, f32[48,512]{1,0:T(8,128)S(1)}, u32[]{:S(2)}, u32[]{:S(2)}) collective-permute-start(f32[48,512]{1,0:T(8,128)S(1)} %pad_maximum_fusion.1), channel_id=1, source_target_pairs={{0,0},{1,8},{2,64},{3,72},{4,128},{5,136},{6,192},{7,200},{8,16},{... | collective-permute-start | bytes 294920 | tf_op jit(solution)/shard_map/ppermute | solution.py:190
  36.8 55.5 %collective-permute-start.1 = (f32[384,512]{1,0:T(8,128)S(1)}, f32[384,512]{1,0:T(8,128)S(1)}, u32[]{:S(2)}, u32[]{:S(2)}) collective-permute-start(f32[384,512]{1,0:T(8,128)S(1)} %all_gather.12.g0_ref), channel_id=1, source_target_pairs={{0,192},{1,193},{2,194},{3,195},{4,196},{5,197},{6,198},{7,199},{8... | collective-permute-start | bytes 2359304 | tf_op jit(solution)/shard_map/ppermute | solution.py:195
  43.1 49.1 %collective-permute-start.3 = (f32[384,512]{1,0:T(8,128)S(1)}, f32[384,512]{1,0:T(8,128)S(1)}, u32[]{:S(2)}, u32[]{:S(2)}) collective-permute-start(f32[384,512]{1,0:T(8,128)S(1)} %all_gather.12.g0_ref), channel_id=1, source_target_pairs={{0,64},{1,65},{2,66},{3,67},{4,68},{5,69},{6,70},{7,71},{8,72},{9,... | collective-permute-start | bytes 2359304 | tf_op jit(solution)/shard_map/ppermute | solution.py:196
  43.1 28.6 %collective-permute-start.2 = (f32[48,512]{1,0:T(8,128)S(1)}, f32[48,512]{1,0:T(8,128)S(1)}, u32[]{:S(2)}, u32[]{:S(2)}) collective-permute-start(f32[48,512]{1,0:T(8,128)S(1)} %pad_maximum_fusion.1), channel_id=1, source_target_pairs={{0,128},{1,136},{2,192},{3,200},{4,0},{5,8},{6,64},{7,72},{8,144},... | collective-permute-start | bytes 294920 | tf_op jit(solution)/shard_map/ppermute | solution.py:191
  68.5 23.8 %collective-permute-start.4 = (f32[4,48,512]{2,1,0:T(8,128)S(1)}, f32[4,48,512]{2,1,0:T(8,128)S(1)}, u32[]{:S(2)}, u32[]{:S(2)}) collective-permute-start(f32[4,48,512]{2,1,0:T(8,128)S(1)} %bitcast.32), channel_id=1, source_target_pairs={{0,1},{1,0},{2,3},{3,2},{4,5},{5,4},{6,7},{7,6},{8,9},{9,8},{10,11... | collective-permute-start | bytes 1179656 | tf_op jit(solution)/shard_map/ppermute | solution.py:193
  97.3 22.6 %copy-start.5 = (s32[6,1]{0,1:T(1,128)S(1)}, s32[6,1]{0,1:T(1,128)}, u32[]{:S(2)}) copy-start(s32[6,1]{0,1:T(1,128)} %param.17) | copy-start | bytes 76
  97.4 6.9 %collective-permute-start.5 = (f32[4,48,512]{2,1,0:T(8,128)S(1)}, f32[4,48,512]{2,1,0:T(8,128)S(1)}, u32[]{:S(2)}, u32[]{:S(2)}) collective-permute-start(f32[4,48,512]{2,1,0:T(8,128)S(1)} %get-tuple-element.12), channel_id=1, source_target_pairs={{0,1},{1,0},{2,3},{3,2},{4,5},{5,4},{6,7},{7,6},{8,9},{9,8},{10,11... | collective-permute-start | bytes 1179656 | tf_op jit(solution)/shard_map/ppermute | solution.py:204
  103.0 5.6 %collective-permute-start.7 = (f32[384,256]{1,0:T(8,128)S(1)}, f32[384,256]{1,0:T(8,128)S(1)}, u32[]{:S(2)}, u32[]{:S(2)}) collective-permute-start(f32[384,256]{1,0:T(8,128)S(1)} %get-tuple-element.14), channel_id=1, source_target_pairs={{0,1},{1,0},{2,3},{3,2},{4,5},{5,4},{6,7},{7,6},{8,9},{9,8},{10,11... | collective-permute-start | bytes 1179656 | tf_op jit(solution)/shard_map/ppermute | solution.py:203
  105.1 11.3 %all-to-all-start = ((f32[4,48,512]{2,1,0:T(8,128)}), f32[4,48,512]{2,1,0:T(8,128)S(1)}, u32[]{:S(2)}, u32[]{:S(2)}) async-start(f32[4,48,512]{2,1,0:T(8,128)} %add.41), calls=%async_computation | async-start | bytes 786432 | tf_op jit(solution)/shard_map/all_to_all | solution.py:222
  116.4 12.4 %all-to-all-start.1 = ((f32[16,24,256]{2,1,0:T(8,128)}), f32[16,24,256]{2,1,0:T(8,128)S(1)}, u32[]{:S(2)}, u32[]{:S(2)}) async-start(f32[16,24,256]{2,1,0:T(8,128)} %bitcast.3), calls=%async_computation.1 | async-start | bytes 786432 | tf_op jit(solution)/shard_map/all_to_all | solution.py:146
  120.2 43.2 %copy-start.1 = (f32[256,256]{1,0:T(8,128)S(1)}, f32[256,256]{1,0:T(8,128)}, u32[]{:S(2)}) copy-start(f32[256,256]{1,0:T(8,128)} %param.16) | copy-start | bytes 786436
  129.5 12.0 %all-to-all-start.2 = ((f32[8,24,256]{2,1,0:T(8,128)}), f32[8,24,256]{2,1,0:T(8,128)S(1)}, u32[]{:S(2)}, u32[]{:S(2)}) async-start(f32[8,24,256]{2,1,0:T(8,128)} %broadcast_in_dim.24), calls=%async_computation.2 | async-start | bytes 393216 | tf_op jit(solution)/shard_map/all_to_all | solution.py:151
  133.2 14.2 %collective-permute-start.6 = (f32[48,512]{1,0:T(8,128)S(1)}, f32[48,512]{1,0:T(8,128)S(1)}, u32[]{:S(2)}, u32[]{:S(2)}) collective-permute-start(f32[48,512]{1,0:T(8,128)S(1)} %pad_maximum_fusion.2), channel_id=1, source_target_pairs={{0,0},{1,8},{2,16},{3,24},{4,32},{5,40},{6,48},{7,56},{8,64},{9,72... | collective-permute-start | bytes 294920 | tf_op jit(solution)/shard_map/ppermute | solution.py:225
  142.3 26.2 %copy-start.2 = (f32[256,256]{1,0:T(8,128)S(1)}, f32[256,256]{1,0:T(8,128)}, u32[]{:S(2)}) copy-start(f32[256,256]{1,0:T(8,128)} %param.12) | copy-start | bytes 786436
  142.3 13.6 %all-to-all-start.3 = ((f32[16,24,256]{2,1,0:T(8,128)}), f32[16,24,256]{2,1,0:T(8,128)S(1)}, u32[]{:S(2)}, u32[]{:S(2)}) async-start(f32[16,24,256]{2,1,0:T(8,128)} %broadcast_in_dim.25), calls=%async_computation.3 | async-start | bytes 786432 | tf_op jit(solution)/shard_map/all_to_all | solution.py:151
  155.9 12.5 %collective-permute-start.8 = (f32[384,256]{1,0:T(8,128)S(1)}, f32[384,256]{1,0:T(8,128)S(1)}, u32[]{:S(2)}, u32[]{:S(2)}) collective-permute-start(f32[384,256]{1,0:T(8,128)S(1)} %bitcast.34), channel_id=1, source_target_pairs={{0,1},{1,0},{2,3},{3,2},{4,5},{5,4},{6,7},{7,6},{8,9},{9,8},{10,11... | collective-permute-start | bytes 1179656 | tf_op jit(solution)/shard_map/ppermute | solution.py:208
  159.8 8.6 %all-to-all-start.4 = ((f32[8,2,8,256]{3,2,1,0:T(8,128)}), f32[8,2,8,256]{3,2,1,0:T(8,128)S(1)}, u32[]{:S(2)}, u32[]{:S(2)}) async-start(f32[8,2,8,256]{3,2,1,0:T(8,128)} %copy.24), calls=%async_computation.4 | async-start | bytes 262144 | tf_op jit(solution)/shard_map/all_to_all | solution.py:171
  169.1 2.3 %copy-start.4 = (f32[256,256]{1,0:T(8,128)}, f32[256,256]{1,0:T(8,128)S(1)}, u32[]{:S(2)}) copy-start(f32[256,256]{1,0:T(8,128)S(1)} %slice_add_fusion.1) | copy-start | bytes 786436
  169.5 2.6 %copy-start.3 = (f32[256,256]{1,0:T(8,128)}, f32[256,256]{1,0:T(8,128)S(1)}, u32[]{:S(2)}) copy-start(f32[256,256]{1,0:T(8,128)S(1)} %convolution_subtract_fusion) | copy-start | bytes 786436

commit v3 on v2

--- a/solution.py
+++ b/solution.py
@@ -45,6 +45,10 @@
     return moves(lambda y, z, x, k: ((y + step) % N_Y, z, x, k))
 
 
+def along_x(step):
+    return moves(lambda y, z, x, k: (y, z, (x + step) % N_X, k))
+
+
 def other_core():
     return moves(lambda y, z, x, k: (y, z, x, 1 - k))
 
@@ -79,7 +83,7 @@
     place, a_ref, g0_ref, g1_ref, g2_ref, g3_ref, own_ref, other_ref,
     w_keep, w_send, y_keep, y_send, xh, xl, rh, rl, w_all, y_all,
 ):
-    y, k = place[0], place[1]
+    y, column, k = place[0], place[1], place[2]
     for step, g_ref in enumerate((g0_ref, g1_ref, g2_ref, g3_ref)):
         x = lax.rem(y + step, N_X)
         for q in range(4):
@@ -107,9 +111,10 @@
     half = 3 * WIDTH // 2
     w_keep[...] = w_all[pl.ds(pl.multiple_of(k * half, 128), half), :]
     w_send[...] = w_all[pl.ds(pl.multiple_of((1 - k) * half, 128), half), :]
-    for x in range(N_X):
-        y_keep[x] = y_all[x * N_K + k]
-        y_send[x] = y_all[x * N_K + 1 - k]
+    for step in range(N_X):
+        x = lax.rem(column + step, N_X)
+        y_keep[step] = y_all[x * N_K + k]
+        y_send[step] = y_all[x * N_K + 1 - k]
 
 
 def product_and_grams(place, ancestor, gathered, own, other):
@@ -191,18 +196,24 @@
     far_block = lax.ppermute(panels, ROW_COL, to_column(2))
     own_core = lax.all_gather(panels, "col_0", axis=0)
     next_core = lax.ppermute(own_core, ROW_COL, other_core())
+    block, far_block, own_core = lax.optimization_barrier((block, far_block, own_core))
     gathered = lax.all_gather(block, "row_1", axis=0, tiled=True)
     above = lax.ppermute(gathered, ROW_COL, along_y(-1))
     below = lax.ppermute(gathered, ROW_COL, along_y(1))
     far_block, _ = lax.optimization_barrier((far_block, gathered))
     far = lax.all_gather(far_block, "row_1", axis=0, tiled=True)
-    place = jnp.stack([lax.axis_index("row_0"), lax.axis_index("col_1")]).astype(jnp.int32)
+    place = jnp.stack([lax.axis_index(name) for name in ("row_0", "col_0", "col_1")])
+    place = place.astype(jnp.int32)
     w_keep, w_send, y_keep, y_send = product_and_grams(
         place, ancestor_inverse, (gathered, above, far, below), own_core, next_core
     )
     w_own = w_keep + lax.ppermute(w_send, ROW_COL, other_core())
+    y_send, w_own = lax.optimization_barrier((y_send, w_own))
     y_own = y_keep + lax.ppermute(y_send, ROW_COL, other_core())
     w_part = jnp.sum(at_owner(w_own, PLANE), axis=0)
+    rows = y_own[0]
+    for step in range(1, N_X):
+        rows = rows + lax.ppermute(y_own[step], ROW_COL, along_x(step))
     w_part = jnp.sum(copies_of(w_part, "row_1"), axis=0)
     w_half = copies_of(w_part, PLANE).reshape(w_own.shape)
     w_other = lax.ppermute(w_half, ROW_COL, other_core())
@@ -219,13 +230,13 @@
         - dot(w_cross, panel_above, ((0,), (0,)))
         - dot(panel_above, cross_two, ((0,), (0,)))
     )
-    rows = jnp.sum(lax.all_to_all(y_own, "col_0", 0, 0, tiled=True), axis=0)
     inverse_one = -rows[:, :WIDTH] * mask_one
     inverse_two = -(rows[:, WIDTH:] + dot(inverse_one, panel_above)) * mask_two
     inverses = lax.ppermute(
         jnp.concatenate([inverse_one, inverse_two], axis=1), ROW_COL, moves(result_place)
     )
     inverse_one, inverse_two = inverses[:, :WIDTH], inverses[:, WIDTH:]
+    inverse_two, _ = lax.optimization_barrier((inverse_two, w_part))
     delivered = deliver(inverse_two, selection(tile_owner))
     return (inverse_one, diag_one, cross_two, diag_two, delivered)
 

time: 174 us -> 159 us (0.914)
  waiting for transfers between devices: 39.4 us -> 20 us
  blocking collectives: 53.5 us -> 59 us
    ppermute x1, waiting for transfers between devices: 7.56 us -> 0.01 us  [local(): block = lax.ppermute(panels, ROW_COL, to_column(0))]
    all_to_all x1 -> x0, waiting for transfers between devices: 6.98 us -> none  [local(): rows = jnp.sum(lax.all_to_all(y_own, 'col_0', 0, 0, tiled=True), axis=0)]
    ppermute x1, starting transfers between devices: 6.34 us -> 0.01 us  [local(): above = lax.ppermute(gathered, ROW_COL, along_y(-1))]
    ppermute x1, starting transfers between devices: 12.7 us -> 6.87 us  [local(): far_block = lax.ppermute(panels, ROW_COL, to_column(2))]
    ppermute x1, starting transfers between devices: 5.59 us -> 0.37 us  [local(): y_own = y_keep + lax.ppermute(y_send, ROW_COL, other_core())]
    ppermute x0 -> x3, starting transfers between devices: none -> 5.01 us  [local(): rows = rows + lax.ppermute(y_own[step], ROW_COL, along_x(step))]
    ppermute x1, starting transfers between devices: 0.1 us -> 5.05 us  [local(): w_own = w_keep + lax.ppermute(w_send, ROW_COL, other_core())]
    ppermute x1, starting transfers between devices: 3.18 us -> 7.66 us  [local(): next_core = lax.ppermute(own_core, ROW_COL, other_core())]
  transfers between devices with their start and end apart: 14 -> 16, of which waited for: 7 -> 5; matrix products, arithmetic and copies ran while one was open for 3% -> 3% of each run, Pallas kernels for 0% -> 0%
where the time goes in v3:
time: 159 us; the launch traced here: 157 us
  starting transfers between devices  59.9 us (38%)
  blocking collectives  59 us (37%)
  waiting for transfers between devices  20 us (13%)
  Pallas kernels  5.07 us (3%)
  other arithmetic  4.58 us (3%)
  matrix products  3.92 us (2%)
  local copies, waits for them, and re-layouts  3.51 us (2%)
    all_gather x1, blocking collectives, local(): gathered = lax.all_gather(block, 'row_1', axis=0, tiled=True)  24.5 us
    all_gather x1, blocking collectives, local(): far = lax.all_gather(far_block, 'row_1', axis=0, tiled=True)  21.3 us
    all_gather x1, blocking collectives, local(): own_core = lax.all_gather(panels, 'col_0', axis=0)  13.2 us
    all_to_all x2, starting transfers between devices, copies_of(): return lax.all_to_all(copies, axis, 0, 0, tiled=True)  10.8 us
    all_to_all x2, waiting for transfers between devices, copies_of(): return lax.all_to_all(copies, axis, 0, 0, tiled=True)  9.81 us
    ppermute x1, starting transfers between devices, local(): next_core = lax.ppermute(own_core, ROW_COL, other_core())  7.66 us
    ppermute x1, starting transfers between devices, local(): far_block = lax.ppermute(panels, ROW_COL, to_column(2))  6.87 us
    ppermute x1, starting transfers between devices, local(): lax.ppermute(jnp.concatenate([inverse_one, inverse_two], axis=1), ROW_COL...  6.25 us
  transfers between devices with their start and end apart: 16, of which 5 were waited for; matrix products, arithmetic and copies ran while one was open for 3% of the time, Pallas kernels for 0%

profile of v3, /device:TPU:1, one launch (start us, length us, event | category | flops | bytes accessed | tf_op | source)
XLA Modules:
  0.0 156.9 jit_solution(12681883020636175554)
XLA Ops:
  0.7 1.2 select_reduce_fusion
  1.9 1.1 select_reduce_fusion.1
  3.0 0.9 broadcast_multiply_fusion
  3.9 4.9 %collective-permute-start = (f32[48,512]{1,0:T(8,128)S(1)}, f32[48,512]{1,0:T(8,128)S(1)}, u32[]{:S(2)}, u32[]{:S(2)}) collective-permute-start(f32[48,512]{1,0:T(8,128)S(1)} %pad_maximum_fusion.1), channel_id=1, source_target_pairs={{0,0},{1,8},{2,64},{3,72},{4,128},{5,136},{6,192},{7,200},{8,16},{... | collective-permute-start | bytes 294920 | tf_op jit(solution)/shard_map/ppermute | solution.py:195
  8.9 6.9 %collective-permute-start.1 = (f32[48,512]{1,0:T(8,128)S(1)}, f32[48,512]{1,0:T(8,128)S(1)}, u32[]{:S(2)}, u32[]{:S(2)}) collective-permute-start(f32[48,512]{1,0:T(8,128)S(1)} %pad_maximum_fusion.1), channel_id=1, source_target_pairs={{0,128},{1,136},{2,192},{3,200},{4,0},{5,8},{6,64},{7,72},{8,144},... | collective-permute-start | bytes 294920 | tf_op jit(solution)/shard_map/ppermute | solution.py:196
  15.7 13.2 %all-gather = f32[192,512]{1,0:T(8,128)S(1)} all-gather(f32[48,512]{1,0:T(8,128)S(1)} %pad_maximum_fusion.1), channel_id=2, replica_groups=mesh['row_0'=4,'row_1'=8,'col_0'=4,'col_1'=2] {'col_0'}, dimensions={0}, use_global_device_ids=true | all-gather | bytes 491520 | tf_op jit(solution)/shard_map/all_gather | solution.py:197
  28.9 24.5 %all_gather.14.g0_ref = f32[384,512]{1,0:T(8,128)S(1)} all-gather(f32[48,512]{1,0:T(8,128)S(1)} %collective-permute-done), channel_id=1, replica_groups=mesh['row_0'=4,'row_1'=8,'col_0'=4,'col_1'=2] {'row_1'}, dimensions={0}, use_global_device_ids=true | all-gather | bytes 884736 | tf_op jit(solution)/shard_map/all_gather | solution.py:200
  53.4 1.5 collective-permute-start.3
  54.9 7.7 %collective-permute-start.4 = (f32[4,48,512]{2,1,0:T(8,128)S(1)}, f32[4,48,512]{2,1,0:T(8,128)S(1)}, u32[]{:S(2)}, u32[]{:S(2)}) collective-permute-start(f32[4,48,512]{2,1,0:T(8,128)S(1)} %bitcast.46), channel_id=1, source_target_pairs={{0,1},{1,0},{2,3},{3,2},{4,5},{5,4},{6,7},{7,6},{8,9},{9,8},{10,11... | collective-permute-start | bytes 1179656 | tf_op jit(solution)/shard_map/ppermute | solution.py:198
  62.6 21.3 %all_gather.15.g2_ref = f32[384,512]{1,0:T(8,128)S(1)} all-gather(f32[48,512]{1,0:T(8,128)S(1)} %collective-permute-done.1), channel_id=1, replica_groups=mesh['row_0'=4,'row_1'=8,'col_0'=4,'col_1'=2] {'row_1'}, dimensions={0}, use_global_device_ids=true | all-gather | bytes 884736 | tf_op jit(solution)/shard_map/all_gather | solution.py:204
  83.9 5.1 %product_and_grams.1 = (f32[384,256]{1,0:T(8,128)S(1)}, f32[384,256]{1,0:T(8,128)S(1)}, f32[4,48,512]{2,1,0:T(8,128)S(1)}, f32[4,48,512]{2,1,0:T(8,128)S(1)}) custom-call(s32[3]{0:T(128)S(1)} %pad_add_fusion.place, f32[384,1536]{1,0:T(8,128)} %a_ref.1, f32[384,512]{1,0:T(8,128)S(1)} %all_gather.14.g0_ref, f32[384,512]{1,0:T(8,128)S(1)} %collective-permute-done.2.g1_ref, ...), custom_call_target="tpu_custom_call" | custom-call | tf_op jit(solution)/shard_map/product_and_grams/pallas_call | solution.py:125
  89.0 5.0 %collective-permute-start.5 = (f32[384,256]{1,0:T(8,128)S(1)}, f32[384,256]{1,0:T(8,128)S(1)}, u32[]{:S(2)}, u32[]{:S(2)}) collective-permute-start(f32[384,256]{1,0:T(8,128)S(1)} %get-tuple-element.23), channel_id=1, source_target_pairs={{0,1},{1,0},{2,3},{3,2},{4,5},{5,4},{6,7},{7,6},{8,9},{9,8},{10,11... | collective-permute-start | bytes 1179656 | tf_op jit(solution)/shard_map/ppermute | solution.py:210
  94.1 1.3 collective-permute-done.5
  95.4 0.8 add.50
  96.6 4.6 %all-to-all-start = ((f32[16,24,256]{2,1,0:T(8,128)}), f32[16,24,256]{2,1,0:T(8,128)S(1)}, u32[]{:S(2)}, u32[]{:S(2)}) async-start(f32[16,24,256]{2,1,0:T(8,128)} %bitcast.8), calls=%async_computation | async-start | bytes 786432 | tf_op jit(solution)/shard_map/all_to_all | solution.py:151
  101.4 1.4 collective-permute-start.7
  102.8 2.4 %collective-permute-start.8 = (f32[48,512]{1,0:T(8,128)S(1)}, f32[48,512]{1,0:T(8,128)S(1)}, u32[]{:S(2)}, u32[]{:S(2)}) collective-permute-start(f32[48,512]{1,0:T(8,128)S(1)} %get-tuple-element.31), channel_id=1, source_target_pairs={{0,4},{1,5},{2,6},{3,7},{4,0},{5,1},{6,2},{7,3},{8,12},{9,13},{10,... | collective-permute-start | bytes 294920 | tf_op jit(solution)/shard_map/ppermute | solution.py:216
  105.2 1.2 collective-permute-start.9
  106.6 4.1 %all-to-all-done = f32[16,24,256]{2,1,0:T(8,128)S(1)} async-done(((f32[16,24,256]{2,1,0:T(8,128)}), f32[16,24,256]{2,1,0:T(8,128)S(1)}, u32[]{:S(2)}, u32[]{:S(2)}) %all-to-all-start) | async-done | bytes 393248 | tf_op jit(solution)/shard_map/all_to_all | solution.py:151
  110.8 0.7 broadcast_in_dim.24
  111.5 5.7 %all-to-all-start.1 = ((f32[8,24,256]{2,1,0:T(8,128)}), f32[8,24,256]{2,1,0:T(8,128)S(1)}, u32[]{:S(2)}, u32[]{:S(2)}) async-start(f32[8,24,256]{2,1,0:T(8,128)} %broadcast_in_dim.24), calls=%async_computation.1 | async-start | bytes 393216 | tf_op jit(solution)/shard_map/all_to_all | solution.py:156
  117.5 6.2 %collective-permute-start.10 = (f32[48,512]{1,0:T(8,128)S(1)}, f32[48,512]{1,0:T(8,128)S(1)}, u32[]{:S(2)}, u32[]{:S(2)}) collective-permute-start(f32[48,512]{1,0:T(8,128)S(1)} %pad_maximum_fusion.2), channel_id=1, source_target_pairs={{0,0},{1,8},{2,16},{3,24},{4,32},{5,40},{6,48},{7,56},{8,64},{9,72... | collective-permute-start | bytes 294920 | tf_op jit(solution)/shard_map/ppermute | solution.py:235
  123.8 2.2 %all-to-all-done.1 = f32[8,24,256]{2,1,0:T(8,128)S(1)} async-done(((f32[8,24,256]{2,1,0:T(8,128)}), f32[8,24,256]{2,1,0:T(8,128)S(1)}, u32[]{:S(2)}, u32[]{:S(2)}) %all-to-all-start.1) | async-done | bytes 196640 | tf_op jit(solution)/shard_map/all_to_all | solution.py:156
  126.0 0.8 broadcast_in_dim.25
  126.8 5.1 %all-to-all-start.2 = ((f32[16,24,256]{2,1,0:T(8,128)}), f32[16,24,256]{2,1,0:T(8,128)S(1)}, u32[]{:S(2)}, u32[]{:S(2)}) async-start(f32[16,24,256]{2,1,0:T(8,128)} %broadcast_in_dim.25), calls=%async_computation.2 | async-start | bytes 786432 | tf_op jit(solution)/shard_map/all_to_all | solution.py:156
  132.5 7.6 %all-to-all-done.2 = f32[16,24,256]{2,1,0:T(8,128)S(1)} async-done(((f32[16,24,256]{2,1,0:T(8,128)}), f32[16,24,256]{2,1,0:T(8,128)S(1)}, u32[]{:S(2)}, u32[]{:S(2)}) %all-to-all-start.2) | async-done | bytes 393248 | tf_op jit(solution)/shard_map/all_to_all | solution.py:156
  140.2 3.4 %collective-permute-start.11 = (f32[384,256]{1,0:T(8,128)S(1)}, f32[384,256]{1,0:T(8,128)S(1)}, u32[]{:S(2)}, u32[]{:S(2)}) collective-permute-start(f32[384,256]{1,0:T(8,128)S(1)} %bitcast.48), channel_id=1, source_target_pairs={{0,1},{1,0},{2,3},{3,2},{4,5},{5,4},{6,7},{7,6},{8,9},{9,8},{10,11... | collective-permute-start | bytes 1179656 | tf_op jit(solution)/shard_map/ppermute | solution.py:219
  143.8 0.7 copy.24
  144.5 3.5 %all-to-all-start.3 = ((f32[8,2,8,256]{3,2,1,0:T(8,128)}), f32[8,2,8,256]{3,2,1,0:T(8,128)S(1)}, u32[]{:S(2)}, u32[]{:S(2)}) async-start(f32[8,2,8,256]{3,2,1,0:T(8,128)} %copy.24), calls=%async_computation.3 | async-start | bytes 262144 | tf_op jit(solution)/shard_map/all_to_all | solution.py:176
  148.6 4.6 %all-to-all-done.3 = f32[8,2,8,256]{3,2,1,0:T(8,128)S(1)} async-done(((f32[8,2,8,256]{3,2,1,0:T(8,128)}), f32[8,2,8,256]{3,2,1,0:T(8,128)S(1)}, u32[]{:S(2)}, u32[]{:S(2)}) %all-to-all-start.3) | async-done | bytes 131104 | tf_op jit(solution)/shard_map/all_to_all | solution.py:176
  154.9 1.3 fusion.1
  156.3 0.7 copy.32
  (46 shorter events, 4.3 us)
Async XLA Ops:
  0.6 116.6 %copy-start = (f32[256,256]{1,0:T(8,128)S(1)}, f32[256,256]{1,0:T(8,128)}, u32[]{:S(2)}) copy-start(f32[256,256]{1,0:T(8,128)} %param.15) | copy-start | bytes 786436
  3.9 25.0 %collective-permute-start = (f32[48,512]{1,0:T(8,128)S(1)}, f32[48,512]{1,0:T(8,128)S(1)}, u32[]{:S(2)}, u32[]{:S(2)}) collective-permute-start(f32[48,512]{1,0:T(8,128)S(1)} %pad_maximum_fusion.1), channel_id=1, source_target_pairs={{0,0},{1,8},{2,64},{3,72},{4,128},{5,136},{6,192},{7,200},{8,16},{... | collective-permute-start | bytes 294920 | tf_op jit(solution)/shard_map/ppermute | solution.py:195
  8.9 20.0 %collective-permute-start.1 = (f32[48,512]{1,0:T(8,128)S(1)}, f32[48,512]{1,0:T(8,128)S(1)}, u32[]{:S(2)}, u32[]{:S(2)}) collective-permute-start(f32[48,512]{1,0:T(8,128)S(1)} %pad_maximum_fusion.1), channel_id=1, source_target_pairs={{0,128},{1,136},{2,192},{3,200},{4,0},{5,8},{6,64},{7,72},{8,144},... | collective-permute-start | bytes 294920 | tf_op jit(solution)/shard_map/ppermute | solution.py:196
  53.4 30.5 %collective-permute-start.2 = (f32[384,512]{1,0:T(8,128)S(1)}, f32[384,512]{1,0:T(8,128)S(1)}, u32[]{:S(2)}, u32[]{:S(2)}) collective-permute-start(f32[384,512]{1,0:T(8,128)S(1)} %all_gather.14.g0_ref), channel_id=1, source_target_pairs={{0,192},{1,193},{2,194},{3,195},{4,196},{5,197},{6,198},{7,199},{8... | collective-permute-start | bytes 2359304 | tf_op jit(solution)/shard_map/ppermute | solution.py:201
  53.4 30.5 %collective-permute-start.3 = (f32[384,512]{1,0:T(8,128)S(1)}, f32[384,512]{1,0:T(8,128)S(1)}, u32[]{:S(2)}, u32[]{:S(2)}) collective-permute-start(f32[384,512]{1,0:T(8,128)S(1)} %all_gather.14.g0_ref), channel_id=1, source_target_pairs={{0,64},{1,65},{2,66},{3,67},{4,68},{5,69},{6,70},{7,71},{8,72},{9,... | collective-permute-start | bytes 2359304 | tf_op jit(solution)/shard_map/ppermute | solution.py:202
  54.9 29.0 %collective-permute-start.4 = (f32[4,48,512]{2,1,0:T(8,128)S(1)}, f32[4,48,512]{2,1,0:T(8,128)S(1)}, u32[]{:S(2)}, u32[]{:S(2)}) collective-permute-start(f32[4,48,512]{2,1,0:T(8,128)S(1)} %bitcast.46), channel_id=1, source_target_pairs={{0,1},{1,0},{2,3},{3,2},{4,5},{5,4},{6,7},{7,6},{8,9},{9,8},{10,11... | collective-permute-start | bytes 1179656 | tf_op jit(solution)/shard_map/ppermute | solution.py:198
  83.9 17.3 %copy-start.5 = (s32[6,1]{0,1:T(1,128)S(1)}, s32[6,1]{0,1:T(1,128)}, u32[]{:S(2)}) copy-start(s32[6,1]{0,1:T(1,128)} %param.17) | copy-start | bytes 76
  89.0 6.4 %collective-permute-start.5 = (f32[384,256]{1,0:T(8,128)S(1)}, f32[384,256]{1,0:T(8,128)S(1)}, u32[]{:S(2)}, u32[]{:S(2)}) collective-permute-start(f32[384,256]{1,0:T(8,128)S(1)} %get-tuple-element.23), channel_id=1, source_target_pairs={{0,1},{1,0},{2,3},{3,2},{4,5},{5,4},{6,7},{7,6},{8,9},{9,8},{10,11... | collective-permute-start | bytes 1179656 | tf_op jit(solution)/shard_map/ppermute | solution.py:210
  96.2 5.0 %collective-permute-start.6 = (f32[4,48,512]{2,1,0:T(8,128)S(1)}, f32[4,48,512]{2,1,0:T(8,128)S(1)}, u32[]{:S(2)}, u32[]{:S(2)}) collective-permute-start(f32[4,48,512]{2,1,0:T(8,128)S(1)} %get-tuple-element.24), channel_id=1, source_target_pairs={{0,1},{1,0},{2,3},{3,2},{4,5},{5,4},{6,7},{7,6},{8,9},{9,8},{10,11... | collective-permute-start | bytes 1179656 | tf_op jit(solution)/shard_map/ppermute | solution.py:212
  96.6 14.1 %all-to-all-start = ((f32[16,24,256]{2,1,0:T(8,128)}), f32[16,24,256]{2,1,0:T(8,128)S(1)}, u32[]{:S(2)}, u32[]{:S(2)}) async-start(f32[16,24,256]{2,1,0:T(8,128)} %bitcast.8), calls=%async_computation | async-start | bytes 786432 | tf_op jit(solution)/shard_map/all_to_all | solution.py:151
  101.4 15.8 %collective-permute-start.7 = (f32[48,512]{1,0:T(8,128)S(1)}, f32[48,512]{1,0:T(8,128)S(1)}, u32[]{:S(2)}, u32[]{:S(2)}) collective-permute-start(f32[48,512]{1,0:T(8,128)S(1)} %get-tuple-element.29), channel_id=1, source_target_pairs={{0,2},{1,3},{2,4},{3,5},{4,6},{5,7},{6,0},{7,1},{8,10},{9,11},{10,... | collective-permute-start | bytes 294920 | tf_op jit(solution)/shard_map/ppermute | solution.py:216
  102.8 14.3 %collective-permute-start.8 = (f32[48,512]{1,0:T(8,128)S(1)}, f32[48,512]{1,0:T(8,128)S(1)}, u32[]{:S(2)}, u32[]{:S(2)}) collective-permute-start(f32[48,512]{1,0:T(8,128)S(1)} %get-tuple-element.31), channel_id=1, source_target_pairs={{0,4},{1,5},{2,6},{3,7},{4,0},{5,1},{6,2},{7,3},{8,12},{9,13},{10,... | collective-permute-start | bytes 294920 | tf_op jit(solution)/shard_map/ppermute | solution.py:216
  105.2 11.9 %collective-permute-start.9 = (f32[48,512]{1,0:T(8,128)S(1)}, f32[48,512]{1,0:T(8,128)S(1)}, u32[]{:S(2)}, u32[]{:S(2)}) collective-permute-start(f32[48,512]{1,0:T(8,128)S(1)} %get-tuple-element.30), channel_id=1, source_target_pairs={{0,6},{1,7},{2,0},{3,1},{4,2},{5,3},{6,4},{7,5},{8,14},{9,15},{10,... | collective-permute-start | bytes 294920 | tf_op jit(solution)/shard_map/ppermute | solution.py:216
  110.7 37.3 %copy-start.1 = (f32[256,256]{1,0:T(8,128)S(1)}, f32[256,256]{1,0:T(8,128)}, u32[]{:S(2)}) copy-start(f32[256,256]{1,0:T(8,128)} %param.16) | copy-start | bytes 786436
  111.5 14.5 %all-to-all-start.1 = ((f32[8,24,256]{2,1,0:T(8,128)}), f32[8,24,256]{2,1,0:T(8,128)S(1)}, u32[]{:S(2)}, u32[]{:S(2)}) async-start(f32[8,24,256]{2,1,0:T(8,128)} %broadcast_in_dim.24), calls=%async_computation.1 | async-start | bytes 393216 | tf_op jit(solution)/shard_map/all_to_all | solution.py:156
  117.5 14.4 %collective-permute-start.10 = (f32[48,512]{1,0:T(8,128)S(1)}, f32[48,512]{1,0:T(8,128)S(1)}, u32[]{:S(2)}, u32[]{:S(2)}) collective-permute-start(f32[48,512]{1,0:T(8,128)S(1)} %pad_maximum_fusion.2), channel_id=1, source_target_pairs={{0,0},{1,8},{2,16},{3,24},{4,32},{5,40},{6,48},{7,56},{8,64},{9,72... | collective-permute-start | bytes 294920 | tf_op jit(solution)/shard_map/ppermute | solution.py:235
  126.8 26.5 %copy-start.2 = (f32[256,256]{1,0:T(8,128)S(1)}, f32[256,256]{1,0:T(8,128)}, u32[]{:S(2)}) copy-start(f32[256,256]{1,0:T(8,128)} %param.12) | copy-start | bytes 786436
  126.8 13.4 %all-to-all-start.2 = ((f32[16,24,256]{2,1,0:T(8,128)}), f32[16,24,256]{2,1,0:T(8,128)S(1)}, u32[]{:S(2)}, u32[]{:S(2)}) async-start(f32[16,24,256]{2,1,0:T(8,128)} %broadcast_in_dim.25), calls=%async_computation.2 | async-start | bytes 786432 | tf_op jit(solution)/shard_map/all_to_all | solution.py:156
  140.2 13.1 %collective-permute-start.11 = (f32[384,256]{1,0:T(8,128)S(1)}, f32[384,256]{1,0:T(8,128)S(1)}, u32[]{:S(2)}, u32[]{:S(2)}) collective-permute-start(f32[384,256]{1,0:T(8,128)S(1)} %bitcast.48), channel_id=1, source_target_pairs={{0,1},{1,0},{2,3},{3,2},{4,5},{5,4},{6,7},{7,6},{8,9},{9,8},{10,11... | collective-permute-start | bytes 1179656 | tf_op jit(solution)/shard_map/ppermute | solution.py:219
  144.5 8.8 %all-to-all-start.3 = ((f32[8,2,8,256]{3,2,1,0:T(8,128)}), f32[8,2,8,256]{3,2,1,0:T(8,128)S(1)}, u32[]{:S(2)}, u32[]{:S(2)}) async-start(f32[8,2,8,256]{3,2,1,0:T(8,128)} %copy.24), calls=%async_computation.3 | async-start | bytes 262144 | tf_op jit(solution)/shard_map/all_to_all | solution.py:176
  153.9 2.3 %copy-start.4 = (f32[256,256]{1,0:T(8,128)}, f32[256,256]{1,0:T(8,128)S(1)}, u32[]{:S(2)}) copy-start(f32[256,256]{1,0:T(8,128)S(1)} %slice_add_fusion.1) | copy-start | bytes 786436
  154.3 2.6 %copy-start.3 = (f32[256,256]{1,0:T(8,128)}, f32[256,256]{1,0:T(8,128)S(1)}, u32[]{:S(2)}) copy-start(f32[256,256]{1,0:T(8,128)S(1)} %convolution_subtract_fusion) | copy-start | bytes 786436

commit v4 on v3

v4 whole, which is shorter than its diff:
```python
import jax
import jax.numpy as jnp
from jax import lax
from jax.experimental import pallas as pl
from jax.experimental.pallas import tpu as pltpu
from jax.sharding import Mesh
from jax.sharding import PartitionSpec as P

CAP = 2
COL = ("col_0", "col_1")
ROW = ("row_0", "row_1")
ROW_COL = ROW + COL
COL_ROW = COL + ROW
PLANE = ("row_0", "col_0")
N_Y, N_Z, N_X, N_K = 4, 8, 4, 2
N_ROW, N_COL = N_Y * N_Z, N_X * N_K
ROWS = 48
WIDTH = 256
TILES, TILE_ROWS = 6, 8
SMALL = pltpu.CompilerParams(vmem_limit_bytes=6 * 1024 * 1024)
SMEM = pl.BlockSpec(memory_space=pltpu.SMEM)
VMEM = pl.BlockSpec(memory_space=pltpu.VMEM)


def device(y, z, x, k):
    return ((y * N_Z + z) * N_X + x) * N_K + k


def moves(place):
    return [
        (device(y, z, x, k), device(*place(y, z, x, k)))
        for y in range(N_Y)
        for z in range(N_Z)
        for x in range(N_X)
        for k in range(N_K)
    ]


def to_column(step):
    return moves(lambda y, z, x, k: ((x + step) % N_Y, 2 * (z % 4) + k, y, z // 4))


def result_place(y, z, x, k):
    column, row = divmod((y * N_Z + z) * N_COL + x * N_K + k, N_ROW)
    return (row // N_Z, row % N_Z, column // N_K, column % N_K)


def along_y(step):
    return moves(lambda y, z, x, k: ((y + step) % N_Y, z, x, k))


def along_x(step):
    return moves(lambda y, z, x, k: (y, z, (x + step) % N_X, k))


def other_core():
    return moves(lambda y, z, x, k: (y, z, x, 1 - k))


def mask_kernel(start, one_ref, two_ref, panel_one, panel_two, panels, masks):
    rows = start[0] + lax.broadcasted_iota(jnp.int32, (ROWS, 128), 0)
    for part, (listed, panel) in enumerate(((one_ref, panel_one), (two_ref, panel_two))):
        hit = jnp.zeros((ROWS, 128), jnp.float32)
        for line in range(listed.shape[0]):
            hit = jnp.where(listed[line : line + 1, :] == rows, 1.0, hit)
        mask = jnp.broadcast_to(jnp.max(hit, axis=1, keepdims=True), (ROWS, WIDTH))
        columns = slice(part * WIDTH, (part + 1) * WIDTH)
        masks[:, columns] = mask
        panels[:, columns] = panel[...] * mask


def masked_panels(start, struct_one, struct_two, panel_one, panel_two):
    shape = jax.ShapeDtypeStruct((ROWS, 2 * WIDTH), jnp.float32)
    return pl.pallas_call(
        mask_kernel,
        in_specs=[SMEM] + [VMEM] * 4,
        out_specs=[VMEM] * 2,
        out_shape=[shape, shape],
        compiler_params=SMALL,
        name="masked_panels",
    )(start, struct_one.reshape(-1, 128), struct_two.reshape(-1, 128), panel_one, panel_two)


def dot(left, right, dims=((1,), (0,)), precision=lax.Precision.HIGHEST):
    return lax.dot_general(
        left, right, (dims, ((), ())), precision=precision, preferred_element_type=jnp.float32
    )


def split(value):
    high = value.astype(jnp.bfloat16)
    return high, (value - high.astype(jnp.float32)).astype(jnp.bfloat16)


def three_pass(left, right, dims):
    (a, b), (c, d) = left, right

    def one(p, q):
        return lax.dot_general(p, q, (dims, ((), ())), preferred_element_type=jnp.float32)

    return one(a, c) + (one(a, d) + one(b, c))


def product_kernel(
    place, a_ref, g0_ref, g1_ref, g2_ref, g3_ref, r0_ref, r1_ref, r2_ref, r3_ref,
    w_keep, w_send, y_keep, y_send, xh, xl, rh, rl, w_all, y_all,
):
    y, column, k = place[0], place[1], place[2]
    for step, g_ref in enumerate((g0_ref, g1_ref, g2_ref, g3_ref)):
        x = lax.rem(y + step, N_X)
        for q in range(4):
            high, low = split(g_ref[pl.ds(q * 96, 96), :])
            at = pl.multiple_of(q * 384 + x * 96, 32)
            xh[pl.ds(at, 96), :] = high
            xl[pl.ds(at, 96), :] = low
    for step, r_ref in enumerate((r0_ref, r1_ref, r2_ref, r3_ref)):
        x = lax.rem(column + N_X - step, N_X)
        for part, core in ((0, k), (1, 1 - k)):
            high, low = split(r_ref[part])
            at = pl.multiple_of((x * N_K + core) * ROWS, 16)
            rh[pl.ds(at, ROWS), :] = high
            rl[pl.ds(at, ROWS), :] = low
    product = three_pass(split(a_ref[...]), (xh[...], xl[...]), ((1,), (0,)))
    for block in range(N_COL):
        y_all[block] = product[block * ROWS : (block + 1) * ROWS]
    high, low = split(product)
    rows_dims = ((0,), (0,))
    one = (rh[:, :WIDTH], rl[:, :WIDTH])
    two = (rh[:, WIDTH:], rl[:, WIDTH:])
    from_one = three_pass(one, (high, low), rows_dims)
    w_all[0:WIDTH, :] = from_one[:, :WIDTH]
    w_all[WIDTH : 2 * WIDTH, :] = from_one[:, WIDTH:]
    w_all[2 * WIDTH :, :] = three_pass(two, (high[:, WIDTH:], low[:, WIDTH:]), rows_dims)
    half = 3 * WIDTH // 2
    w_keep[...] = w_all[pl.ds(pl.multiple_of(k * half, 128), half), :]
    w_send[...] = w_all[pl.ds(pl.multiple_of((1 - k) * half, 128), half), :]
    for step in range(N_X):
        x = lax.rem(column + step, N_X)
        y_keep[step] = y_all[x * N_K + k]
        y_send[step] = y_all[x * N_K + 1 - k]


def product_and_grams(place, ancestor, gathered, row_panels):
    f32, bf16 = jnp.float32, jnp.bfloat16
    half = 3 * WIDTH // 2
    wide = 2 * WIDTH
    return pl.pallas_call(
        product_kernel,
        in_specs=[SMEM] + [VMEM] * 9,
        out_specs=[VMEM] * 4,
        out_shape=[
            jax.ShapeDtypeStruct((half, WIDTH), f32),
            jax.ShapeDtypeStruct((half, WIDTH), f32),
            jax.ShapeDtypeStruct((N_X, ROWS, wide), f32),
            jax.ShapeDtypeStruct((N_X, ROWS, wide), f32),
        ],
        scratch_shapes=[
            pltpu.VMEM((1536, wide), bf16),
            pltpu.VMEM((1536, wide), bf16),
            pltpu.VMEM((384, wide), bf16),
            pltpu.VMEM((384, wide), bf16),
            pltpu.VMEM((3 * WIDTH, WIDTH), f32),
            pltpu.VMEM((N_COL, ROWS, wide), f32),
        ],
        compiler_params=pltpu.CompilerParams(vmem_limit_bytes=24 * 1024 * 1024),
        name="product_and_grams",
    )(place, ancestor, *gathered, *row_panels)


def at_owner(value, axis):
    count = lax.axis_size(axis)
    parts = value.reshape(count, value.shape[0] // count, *value.shape[1:])
    return lax.all_to_all(parts, axis, 0, 0, tiled=True)


def copies_of(value, axis):
    copies = jnp.broadcast_to(value[None], (lax.axis_size(axis), *value.shape))
    return lax.all_to_all(copies, axis, 0, 0, tiled=True)


def inverse_kernel(y0, y1, y2, y3, masks, above, out):
    rows = (y0[...] + y1[...]) + (y2[...] + y3[...])
    one = -rows[:, :WIDTH] * masks[:, :WIDTH]
    out[:, :WIDTH] = one
    out[:, WIDTH:] = -(rows[:, WIDTH:] + dot(one, above[...])) * masks[:, WIDTH:]


def inverse_rows(parts, masks, panel_above):
    return pl.pallas_call(
        inverse_kernel,
        in_specs=[VMEM] * 6,
        out_specs=VMEM,
        out_shape=jax.ShapeDtypeStruct((ROWS, 2 * WIDTH), jnp.float32),
        compiler_params=SMALL,
        name="inverse_rows",
    )(*parts, masks, panel_above)


def pick_kernel(place, owner, rows, one, keep, send):
    column, k = place[1], place[2]
    one[...] = rows[:, :WIDTH]
    keep[...] = jnp.zeros(keep.shape, jnp.float32)
    send[...] = jnp.zeros(send.shape, jnp.float32)
    for tile in range(TILES):
        mine = owner[tile]
        rank = jnp.int32(0)
        for earlier in range(tile):
            rank = rank + jnp.where(owner[earlier] == mine, 1, 0)
        rank = jnp.minimum(rank, CAP - 1)
        step = lax.rem(lax.div(mine, N_K) + N_X - column, N_X)
        core = lax.rem(mine, N_K)
        values = rows[tile * TILE_ROWS : (tile + 1) * TILE_ROWS, WIDTH:]

        @pl.when(core == k)
        def _():
            keep[step * CAP + rank] = values

        @pl.when(core != k)
        def _():
            send[step * CAP + rank] = values


def pick_tiles(place, tile_owner, rows):
    tiles = jax.ShapeDtypeStruct((N_X * CAP, TILE_ROWS, WIDTH), jnp.float32)
    return pl.pallas_call(
        pick_kernel,
        in_specs=[SMEM, SMEM, VMEM],
        out_specs=[VMEM] * 3,
        out_shape=[jax.ShapeDtypeStruct((ROWS, WIDTH), jnp.float32), tiles, tiles],
        compiler_params=SMALL,
        name="pick_tiles",
    )(place, tile_owner.reshape(-1), rows)


def slots_kernel(place, p0, p1, p2, p3, out):
    column, k = place[1], place[2]
    for step, part in enumerate((p0, p1, p2, p3)):
        x = lax.rem(column + N_X - step, N_X)
        for source, core in ((0, k), (1, 1 - k)):
            for slot in range(CAP):
                out[(x * N_K + core) * CAP + slot] = part[source, slot]


def fill_slots(place, parts):
    return pl.pallas_call(
        slots_kernel,
        in_specs=[SMEM] + [VMEM] * 4,
        out_specs=VMEM,
        out_shape=jax.ShapeDtypeStruct((N_COL * CAP, TILE_ROWS, WIDTH), jnp.float32),
        compiler_params=SMALL,
        name="fill_slots",
    )(place, *parts)


def deliver(place, tile_owner, rows):
    inverse_one, keep, send = pick_tiles(place, tile_owner, rows)
    shape = (N_X, CAP, TILE_ROWS, WIDTH)
    arrived = lax.ppermute(send, ROW_COL, other_core())
    pairs = jnp.stack([keep.reshape(shape), arrived.reshape(shape)], axis=1)
    parts = [pairs[0]]
    for step in range(1, N_X):
        parts.append(lax.ppermute(pairs[step], ROW_COL, along_x(step)))
    return inverse_one, fill_slots(place, parts)


def final_kernel(place, half, other, square_one, square_two, above, diag_one, cross_two, diag_two, w):
    rows = half.shape[0]
    first = pl.multiple_of(place[2] * rows, 128)
    second = pl.multiple_of((1 - place[2]) * rows, 128)
    w[pl.ds(first, rows), :] = half[...]
    w[pl.ds(second, rows), :] = other[...]
    w_cross = w[WIDTH : 2 * WIDTH]
    rows_dims = ((0,), (0,))
    one = square_one[...] + w[:WIDTH]
    cross = w_cross - dot(one, above[...])
    diag_one[...] = one
    cross_two[...] = cross
    twice = dot(w_cross, above[...], rows_dims) + dot(above[...], cross, rows_dims)
    diag_two[...] = square_two[...] + w[2 * WIDTH :] - twice


def final_blocks(place, half, other, square_one, square_two, panel_above):
    block = jax.ShapeDtypeStruct((WIDTH, WIDTH), jnp.float32)
    return pl.pallas_call(
        final_kernel,
        in_specs=[SMEM] + [VMEM] * 5,
        out_specs=[VMEM] * 3,
        out_shape=[block] * 3,
        scratch_shapes=[pltpu.VMEM((3 * WIDTH, WIDTH), jnp.float32)],
        compiler_params=SMALL,
        name="final_blocks",
    )(place, half, other, square_one, square_two, panel_above)


def local(
    ancestor_inverse,
    panel_one,
    struct_one,
    lower_one,
    panel_two,
    struct_two,
    panel_above,
    lower_two,
    tile_owner,
):
    start = (lax.axis_index(ROW) * N_COL + lax.axis_index(COL)) * ROWS
    place = jnp.stack([lax.axis_index(name) for name in ("row_0", "col_0", "col_1")])
    place = place.astype(jnp.int32)
    panels, masks = masked_panels(
        start.astype(jnp.int32)[None], struct_one, struct_two, panel_one, panel_two
    )
    block = lax.ppermute(panels, ROW_COL, to_column(0))
    far_block = lax.ppermute(panels, ROW_COL, to_column(2))
    sibling = lax.ppermute(panels, ROW_COL, other_core())
    block, far_block, sibling = lax.optimization_barrier((block, far_block, sibling))
    pair = jnp.stack([panels, sibling])
    gathered = lax.all_gather(block, "row_1", axis=0, tiled=True)
    above = lax.ppermute(gathered, ROW_COL, along_y(-1))
    below = lax.ppermute(gathered, ROW_COL, along_y(1))
    far_block, pair, _ = lax.optimization_barrier((far_block, pair, gathered))
    row_panels = [pair]
    for step in range(1, N_X):
        row_panels.append(lax.ppermute(pair, ROW_COL, along_x(step)))
    far = lax.all_gather(far_block, "row_1", axis=0, tiled=True)
    w_keep, w_send, y_keep, y_send = product_and_grams(
        place, ancestor_inverse, (gathered, above, far, below), row_panels
    )
    w_own = w_keep + lax.ppermute(w_send, ROW_COL, other_core())
    y_send, w_own = lax.optimization_barrier((y_send, w_own))
    y_own = y_keep + lax.ppermute(y_send, ROW_COL, other_core())
    y_parts = [y_own[0]]
    for step in range(1, N_X):
        y_parts.append(lax.ppermute(y_own[step], ROW_COL, along_x(step)))
    w_part = jnp.sum(at_owner(w_own, PLANE), axis=0)
    w_part, y_parts = lax.optimization_barrier((w_part, y_parts))
    w_part = jnp.sum(copies_of(w_part, "row_1"), axis=0)
    inverses = inverse_rows(y_parts, masks, panel_above)
    w_part, _ = lax.optimization_barrier((w_part, inverses))
    w_half = copies_of(w_part, PLANE).reshape(w_own.shape)
    w_other = lax.ppermute(w_half, ROW_COL, other_core())
    inverses = lax.ppermute(inverses, ROW_COL, moves(result_place))
    inverse_one, delivered = deliver(place, tile_owner, inverses)
    square_one = dot(lower_one, lower_one, ((0,), (0,)))
    square_two = dot(lower_two, lower_two, ((0,), (0,)))
    diag_one, cross_two, diag_two = final_blocks(
        place, w_half, w_other, square_one, square_two, panel_above
    )
    return (inverse_one, diag_one, cross_two, diag_two, delivered)


def solution(mesh):
    finer = Mesh(mesh.devices.reshape(4, 8, 4, 2), ("row_0", "row_1", "col_0", "col_1"))
    return jax.shard_map(
        local,
        mesh=finer,
        in_specs=(
            P(ROW, COL),
            P(ROW_COL, None),
            P(),
            P(),
            P(ROW_COL, None),
            P(),
            P(),
            P(),
            P(COL_ROW, None),
        ),
        out_specs=(P(COL_ROW, None), P(), P(), P(), P(ROW_COL, None, None)),
        check_vma=False,
    )
```

time: 159 us -> 164 us (1.031)
  blocking collectives: 59 us -> 43.7 us
  starting transfers between devices: 59.9 us -> 73.1 us
  waiting for transfers between devices: 20 us -> 28.2 us
  Pallas kernels: 5.07 us -> 9.67 us
  other arithmetic: 4.58 us -> 0.99 us
  matrix products: 3.92 us -> 1.19 us
    all_gather x1 -> x0, blocking collectives: 13.2 us -> none  [local(): own_core = lax.all_gather(panels, 'col_0', axis=0)]
    ppermute x5 -> x12, starting transfers between devices: 18.9 us -> 29.4 us  [the longest x3 15.1 us: deliver(): parts.append(lax.ppermute(pairs[step], ROW_COL, along_x(step)))]
    ppermute x1, starting transfers between devices: 5.05 us -> 13.8 us  [local(): w_own = w_keep + lax.ppermute(w_send, ROW_COL, other_core())]
    ppermute x5 -> x12, waiting for transfers between devices: 0.01 us -> 7.73 us  [the longest x1 4.95 us: local(): inverses = lax.ppermute(inverses, ROW_COL, moves(result_place))]
    ppermute x1, waiting for transfers between devices: 0.01 us -> 5.89 us  [local(): far_block = lax.ppermute(panels, ROW_COL, to_column(2))]
    all_to_all x1 -> x0, waiting for transfers between devices: 4.63 us -> none  [deliver(): lax.all_to_all(outgoing, COL, split_axis=0, concat_axis=0, tiled=True)]
    pallas_call x1 -> x6, Pallas kernels: 5.07 us -> 9.67 us  [the longest x1 3.95 us: product_and_grams(): pl.pallas_call(product_kernel, in_specs=[SMEM] + [VMEM] * 9, out_specs=[V...]
    all_to_all x1 -> x0, starting transfers between devices: 3.5 us -> none  [deliver(): lax.all_to_all(outgoing, COL, split_axis=0, concat_axis=0, tiled=True)]
  transfers between devices with their start and end apart: 16 -> 22, of which waited for: 5 -> 9; matrix products, arithmetic and copies ran while one was open for 3% -> 1% of each run, Pallas kernels for 0% -> 2%
where the time goes in v4:
time: 164 us; the launch traced here: 163 us
  starting transfers between devices  73.1 us (45%)
  blocking collectives  43.7 us (27%)
  waiting for transfers between devices  28.2 us (17%)
  Pallas kernels  9.67 us (6%)
  local copies, waits for them, and re-layouts  4.81 us (3%)
    all_gather x1, blocking collectives, local(): gathered = lax.all_gather(block, 'row_1', axis=0, tiled=True)  22.8 us
    all_gather x1, blocking collectives, local(): far = lax.all_gather(far_block, 'row_1', axis=0, tiled=True)  21 us
    ppermute x3, starting transfers between devices, deliver(): parts.append(lax.ppermute(pairs[step], ROW_COL, along_x(step)))  15.1 us
    ppermute x1, starting transfers between devices, local(): w_own = w_keep + lax.ppermute(w_send, ROW_COL, other_core())  13.8 us
    all_to_all x2, starting transfers between devices, copies_of(): return lax.all_to_all(copies, axis, 0, 0, tiled=True)  8.51 us
    all_to_all x2, waiting for transfers between devices, copies_of(): return lax.all_to_all(copies, axis, 0, 0, tiled=True)  8.21 us
    ppermute x1, starting transfers between devices, local(): far_block = lax.ppermute(panels, ROW_COL, to_column(2))  6.87 us
    ppermute x1, waiting for transfers between devices, local(): far_block = lax.ppermute(panels, ROW_COL, to_column(2))  5.89 us
  transfers between devices with their start and end apart: 22, of which 9 were waited for; matrix products, arithmetic and copies ran while one was open for 1% of the time, Pallas kernels for 2%

profile of v4, /device:TPU:1, one launch (start us, length us, event | category | flops | bytes accessed | tf_op | source)
XLA Modules:
  0.0 162.6 jit_solution(13132627045141530857)
XLA Ops:
  0.7 0.9 copy-done.3
  1.6 0.8 copy-done.4
  2.4 0.8 copy-done.5
  4.3 4.9 %collective-permute-start = (f32[48,512]{1,0:T(8,128)S(1)}, f32[48,512]{1,0:T(8,128)S(1)}, u32[]{:S(2)}, u32[]{:S(2)}) collective-permute-start(f32[48,512]{1,0:T(8,128)S(1)} %get-tuple-element.30), channel_id=1, source_target_pairs={{0,0},{1,8},{2,64},{3,72},{4,128},{5,136},{6,192},{7,200},{8,16},{... | collective-permute-start | bytes 294920 | tf_op jit(solution)/shard_map/ppermute | solution.py:312
  9.3 6.9 %collective-permute-start.1 = (f32[48,512]{1,0:T(8,128)S(1)}, f32[48,512]{1,0:T(8,128)S(1)}, u32[]{:S(2)}, u32[]{:S(2)}) collective-permute-start(f32[48,512]{1,0:T(8,128)S(1)} %get-tuple-element.30), channel_id=1, source_target_pairs={{0,128},{1,136},{2,192},{3,200},{4,0},{5,8},{6,64},{7,72},{8,144},... | collective-permute-start | bytes 294920 | tf_op jit(solution)/shard_map/ppermute | solution.py:313
  16.8 5.9 %collective-permute-done.1 = f32[48,512]{1,0:T(8,128)S(1)} collective-permute-done((f32[48,512]{1,0:T(8,128)S(1)}, f32[48,512]{1,0:T(8,128)S(1)}, u32[]{:S(2)}, u32[]{:S(2)}) %collective-permute-start.1) | collective-permute-done | bytes 98336 | tf_op jit(solution)/shard_map/ppermute | solution.py:313
  22.7 22.8 %all_gather.6.g0_ref = f32[384,512]{1,0:T(8,128)S(1)} all-gather(f32[48,512]{1,0:T(8,128)S(1)} %collective-permute-done), channel_id=1, replica_groups=mesh['row_0'=4,'row_1'=8,'col_0'=4,'col_1'=2] {'row_1'}, dimensions={0}, use_global_device_ids=true | all-gather | bytes 884736 | tf_op jit(solution)/shard_map/all_gather | solution.py:317
  45.5 3.3 %collective-permute-start.3 = (f32[384,512]{1,0:T(8,128)S(1)}, f32[384,512]{1,0:T(8,128)S(1)}, u32[]{:S(2)}, u32[]{:S(2)}) collective-permute-start(f32[384,512]{1,0:T(8,128)S(1)} %all_gather.6.g0_ref), channel_id=1, source_target_pairs={{0,192},{1,193},{2,194},{3,195},{4,196},{5,197},{6,198},{7,199},{8... | collective-permute-start | bytes 2359304 | tf_op jit(solution)/shard_map/ppermute | solution.py:318
  49.3 3.0 %collective-permute-start.6 = (f32[2,48,512]{2,1,0:T(8,128)S(1)}, f32[2,48,512]{2,1,0:T(8,128)S(1)}, u32[]{:S(2)}, u32[]{:S(2)}) collective-permute-start(f32[2,48,512]{2,1,0:T(8,128)S(1)} %pad_maximum_fusion.r0_ref), channel_id=1, source_target_pairs={{0,4},{1,5},{2,6},{3,7},{4,0},{5,1},{6,2},{7,3},{8,12},{9,13},{10,... | collective-permute-start | bytes 589832 | tf_op jit(solution)/shard_map/ppermute | solution.py:323
  53.0 21.0 %all_gather.7.g2_ref = f32[384,512]{1,0:T(8,128)S(1)} all-gather(f32[48,512]{1,0:T(8,128)S(1)} %collective-permute-done.1), channel_id=1, replica_groups=mesh['row_0'=4,'row_1'=8,'col_0'=4,'col_1'=2] {'row_1'}, dimensions={0}, use_global_device_ids=true | all-gather | bytes 884736 | tf_op jit(solution)/shard_map/all_gather | solution.py:324
  74.0 4.0 %product_and_grams.1 = (f32[384,256]{1,0:T(8,128)S(1)}, f32[384,256]{1,0:T(8,128)S(1)}, f32[4,48,512]{2,1,0:T(8,128)S(1)}, f32[4,48,512]{2,1,0:T(8,128)S(1)}) custom-call(s32[3]{0:T(128)S(1)} %pad_add_fusion.place, f32[384,1536]{1,0:T(8,128)S(1)} %copy-done.1, f32[384,512]{1,0:T(8,128)S(1)} %all_gather.6.g0_ref, ...), custom_call_target="tpu_custom_call" | custom-call | tf_op jit(solution)/shard_map/product_and_grams/pallas_call | solution.py:147
  78.0 13.8 %collective-permute-start.8 = (f32[384,256]{1,0:T(8,128)S(1)}, f32[384,256]{1,0:T(8,128)S(1)}, u32[]{:S(2)}, u32[]{:S(2)}) collective-permute-start(f32[384,256]{1,0:T(8,128)S(1)} %get-tuple-element.38), channel_id=1, source_target_pairs={{0,1},{1,0},{2,3},{3,2},{4,5},{5,4},{6,7},{7,6},{8,9},{9,8},{10,11... | collective-permute-start | bytes 1179656 | tf_op jit(solution)/shard_map/ppermute | solution.py:328
  91.8 1.3 collective-permute-done.8
  93.1 0.8 add.18
  94.3 4.9 %all-to-all-start = ((f32[16,24,256]{2,1,0:T(8,128)}), f32[16,24,256]{2,1,0:T(8,128)S(1)}, u32[]{:S(2)}, u32[]{:S(2)}) async-start(f32[16,24,256]{2,1,0:T(8,128)} %bitcast.9), calls=%async_computation | async-start | bytes 786432 | tf_op jit(solution)/shard_map/all_to_all | solution.py:173
  99.3 1.4 collective-permute-start.10
  100.7 2.4 %collective-permute-start.11 = (f32[48,512]{1,0:T(8,128)S(1)}, f32[48,512]{1,0:T(8,128)S(1)}, u32[]{:S(2)}, u32[]{:S(2)}) collective-permute-start(f32[48,512]{1,0:T(8,128)S(1)} %get-tuple-element.56), channel_id=1, source_target_pairs={{0,4},{1,5},{2,6},{3,7},{4,0},{5,1},{6,2},{7,3},{8,12},{9,13},{10,... | collective-permute-start | bytes 294920 | tf_op jit(solution)/shard_map/ppermute | solution.py:333
  103.1 1.2 collective-permute-start.12
  104.3 4.3 %all-to-all-done = f32[16,24,256]{2,1,0:T(8,128)S(1)} async-done(((f32[16,24,256]{2,1,0:T(8,128)}), f32[16,24,256]{2,1,0:T(8,128)S(1)}, u32[]{:S(2)}, u32[]{:S(2)}) %all-to-all-start) | async-done | bytes 393248 | tf_op jit(solution)/shard_map/all_to_all | solution.py:173
  109.3 1.7 %collective-permute-done.11.y2 = f32[48,512]{1,0:T(8,128)S(1)} collective-permute-done((f32[48,512]{1,0:T(8,128)S(1)}, f32[48,512]{1,0:T(8,128)S(1)}, u32[]{:S(2)}, u32[]{:S(2)}) %collective-permute-start.11) | collective-permute-done | bytes 98336 | tf_op jit(solution)/shard_map/ppermute | solution.py:333
  111.7 3.7 %all-to-all-start.1 = ((f32[8,24,256]{2,1,0:T(8,128)}), f32[8,24,256]{2,1,0:T(8,128)S(1)}, u32[]{:S(2)}, u32[]{:S(2)}) async-start(f32[8,24,256]{2,1,0:T(8,128)} %broadcast_in_dim.7), calls=%async_computation.1 | async-start | bytes 393216 | tf_op jit(solution)/shard_map/all_to_all | solution.py:178
  115.6 8.2 %all-to-all-done.1 = f32[8,24,256]{2,1,0:T(8,128)S(1)} async-done(((f32[8,24,256]{2,1,0:T(8,128)}), f32[8,24,256]{2,1,0:T(8,128)S(1)}, u32[]{:S(2)}, u32[]{:S(2)}) %all-to-all-start.1) | async-done | bytes 196640 | tf_op jit(solution)/shard_map/all_to_all | solution.py:178
  124.6 4.8 %all-to-all-start.2 = ((f32[16,24,256]{2,1,0:T(8,128)}), f32[16,24,256]{2,1,0:T(8,128)S(1)}, u32[]{:S(2)}, u32[]{:S(2)}) async-start(f32[16,24,256]{2,1,0:T(8,128)} %broadcast_in_dim.8), calls=%async_computation.2 | async-start | bytes 786432 | tf_op jit(solution)/shard_map/all_to_all | solution.py:178
  129.5 5.2 %collective-permute-start.13 = (f32[48,512]{1,0:T(8,128)S(1)}, f32[48,512]{1,0:T(8,128)S(1)}, u32[]{:S(2)}, u32[]{:S(2)}) collective-permute-start(f32[48,512]{1,0:T(8,128)S(1)} %inverse_rows.1), channel_id=1, source_target_pairs={{0,0},{1,8},{2,16},{3,24},{4,32},{5,40},{6,48},{7,56},{8,64},{9,72... | collective-permute-start | bytes 294920 | tf_op jit(solution)/shard_map/ppermute | solution.py:341
  134.7 4.9 %collective-permute-done.13.rows = f32[48,512]{1,0:T(8,128)S(1)} collective-permute-done((f32[48,512]{1,0:T(8,128)S(1)}, f32[48,512]{1,0:T(8,128)S(1)}, u32[]{:S(2)}, u32[]{:S(2)}) %collective-permute-start.13) | collective-permute-done | bytes 98336 | tf_op jit(solution)/shard_map/ppermute | solution.py:341
  139.6 1.3 pick_tiles.1
  140.9 1.1 collective-permute-start.14
  142.6 8.7 %collective-permute-start.16 = (f32[2,2,8,256]{3,2,1,0:T(8,128)S(1)}, f32[2,2,8,256]{3,2,1,0:T(8,128)S(1)}, u32[]{:S(2)}, u32[]{:S(2)}) collective-permute-start(f32[2,2,8,256]{3,2,1,0:T(8,128)S(1)} %get-tuple-element.61), channel_id=1, source_target_pairs={{0,2},{1,3},{2,4},{3,5},{4,6},{5,7},{6,0},{7,1},{8,10},{9,11},{10,... | collective-permute-start | bytes 98312 | tf_op jit(solution)/shard_map/ppermute | solution.py:262
  151.3 4.5 %collective-permute-start.17 = (f32[2,2,8,256]{3,2,1,0:T(8,128)S(1)}, f32[2,2,8,256]{3,2,1,0:T(8,128)S(1)}, u32[]{:S(2)}, u32[]{:S(2)}) collective-permute-start(f32[2,2,8,256]{3,2,1,0:T(8,128)S(1)} %get-tuple-element.62), channel_id=1, source_target_pairs={{0,4},{1,5},{2,6},{3,7},{4,0},{5,1},{6,2},{7,3},{8,12},{9,13},{10,... | collective-permute-start | bytes 98312 | tf_op jit(solution)/shard_map/ppermute | solution.py:262
  155.8 2.0 %collective-permute-start.18 = (f32[2,2,8,256]{3,2,1,0:T(8,128)S(1)}, f32[2,2,8,256]{3,2,1,0:T(8,128)S(1)}, u32[]{:S(2)}, u32[]{:S(2)}) collective-permute-start(f32[2,2,8,256]{3,2,1,0:T(8,128)S(1)} %get-tuple-element.59), channel_id=1, source_target_pairs={{0,6},{1,7},{2,0},{3,1},{4,2},{5,3},{6,4},{7,5},{8,14},{9,15},{10,... | collective-permute-start | bytes 98312 | tf_op jit(solution)/shard_map/ppermute | solution.py:262
  158.7 1.2 fill_slots.1
  160.0 2.6 %final_blocks.1 = (f32[256,256]{1,0:T(8,128)}, f32[256,256]{1,0:T(8,128)}, f32[256,256]{1,0:T(8,128)}) custom-call(s32[3]{0:T(128)S(1)} %pad_add_fusion.place, f32[384,256]{1,0:T(8,128)S(1)} %bitcast.34, f32[384,256]{1,0:T(8,128)S(1)} %collective-permute-done.14.other, f32[256,256]{1,0:T(8,128)S(1)} %fusion.7.square_one, f32[256,256]{1,0:T(8,128)S(1)} %fusion.8.square_two, ...), custom_call_target="tpu_custom_call" | custom-call | tf_op jit(solution)/shard_map/final_blocks/pallas_call | solution.py:284
  (50 shorter events, 7.5 us)
Async XLA Ops:
  0.6 141.4 %copy-start = (f32[256,256]{1,0:T(8,128)S(1)}, f32[256,256]{1,0:T(8,128)}, u32[]{:S(2)}) copy-start(f32[256,256]{1,0:T(8,128)} %param.12) | copy-start | bytes 786436
  0.6 73.3 %copy-start.1 = (f32[384,1536]{1,0:T(8,128)S(1)}, f32[384,1536]{1,0:T(8,128)}, u32[]{:S(2)}) copy-start(f32[384,1536]{1,0:T(8,128)} %a_ref.1) | copy-start | bytes 7077892
  0.7 0.9 copy-start.3
  1.6 0.8 copy-start.4
  2.4 0.8 copy-start.5
  3.2 0.8 copy-start.6
  4.3 12.5 %collective-permute-start = (f32[48,512]{1,0:T(8,128)S(1)}, f32[48,512]{1,0:T(8,128)S(1)}, u32[]{:S(2)}, u32[]{:S(2)}) collective-permute-start(f32[48,512]{1,0:T(8,128)S(1)} %get-tuple-element.30), channel_id=1, source_target_pairs={{0,0},{1,8},{2,64},{3,72},{4,128},{5,136},{6,192},{7,200},{8,16},{... | collective-permute-start | bytes 294920 | tf_op jit(solution)/shard_map/ppermute | solution.py:312
  9.3 13.4 %collective-permute-start.1 = (f32[48,512]{1,0:T(8,128)S(1)}, f32[48,512]{1,0:T(8,128)S(1)}, u32[]{:S(2)}, u32[]{:S(2)}) collective-permute-start(f32[48,512]{1,0:T(8,128)S(1)} %get-tuple-element.30), channel_id=1, source_target_pairs={{0,128},{1,136},{2,192},{3,200},{4,0},{5,8},{6,64},{7,72},{8,144},... | collective-permute-start | bytes 294920 | tf_op jit(solution)/shard_map/ppermute | solution.py:313
  16.1 6.6 %collective-permute-start.2 = (f32[48,512]{1,0:T(8,128)S(1)}, f32[48,512]{1,0:T(8,128)S(1)}, u32[]{:S(2)}, u32[]{:S(2)}) collective-permute-start(f32[48,512]{1,0:T(8,128)S(1)} %get-tuple-element.30), channel_id=1, source_target_pairs={{0,1},{1,0},{2,3},{3,2},{4,5},{5,4},{6,7},{7,6},{8,9},{9,8},{10,11... | collective-permute-start | bytes 294920 | tf_op jit(solution)/shard_map/ppermute | solution.py:314
  45.5 28.5 %collective-permute-start.3 = (f32[384,512]{1,0:T(8,128)S(1)}, f32[384,512]{1,0:T(8,128)S(1)}, u32[]{:S(2)}, u32[]{:S(2)}) collective-permute-start(f32[384,512]{1,0:T(8,128)S(1)} %all_gather.6.g0_ref), channel_id=1, source_target_pairs={{0,192},{1,193},{2,194},{3,195},{4,196},{5,197},{6,198},{7,199},{8... | collective-permute-start | bytes 2359304 | tf_op jit(solution)/shard_map/ppermute | solution.py:318
  48.7 25.2 %collective-permute-start.4 = (f32[384,512]{1,0:T(8,128)S(1)}, f32[384,512]{1,0:T(8,128)S(1)}, u32[]{:S(2)}, u32[]{:S(2)}) collective-permute-start(f32[384,512]{1,0:T(8,128)S(1)} %all_gather.6.g0_ref), channel_id=1, source_target_pairs={{0,64},{1,65},{2,66},{3,67},{4,68},{5,69},{6,70},{7,71},{8,72},{9,... | collective-permute-start | bytes 2359304 | tf_op jit(solution)/shard_map/ppermute | solution.py:319
  48.8 25.1 %collective-permute-start.5 = (f32[2,48,512]{2,1,0:T(8,128)S(1)}, f32[2,48,512]{2,1,0:T(8,128)S(1)}, u32[]{:S(2)}, u32[]{:S(2)}) collective-permute-start(f32[2,48,512]{2,1,0:T(8,128)S(1)} %pad_maximum_fusion.r0_ref), channel_id=1, source_target_pairs={{0,2},{1,3},{2,4},{3,5},{4,6},{5,7},{6,0},{7,1},{8,10},{9,11},{10,... | collective-permute-start | bytes 589832 | tf_op jit(solution)/shard_map/ppermute | solution.py:323
  49.3 24.7 %collective-permute-start.6 = (f32[2,48,512]{2,1,0:T(8,128)S(1)}, f32[2,48,512]{2,1,0:T(8,128)S(1)}, u32[]{:S(2)}, u32[]{:S(2)}) collective-permute-start(f32[2,48,512]{2,1,0:T(8,128)S(1)} %pad_maximum_fusion.r0_ref), channel_id=1, source_target_pairs={{0,4},{1,5},{2,6},{3,7},{4,0},{5,1},{6,2},{7,3},{8,12},{9,13},{10,... | collective-permute-start | bytes 589832 | tf_op jit(solution)/shard_map/ppermute | solution.py:323
  52.3 21.6 %collective-permute-start.7 = (f32[2,48,512]{2,1,0:T(8,128)S(1)}, f32[2,48,512]{2,1,0:T(8,128)S(1)}, u32[]{:S(2)}, u32[]{:S(2)}) collective-permute-start(f32[2,48,512]{2,1,0:T(8,128)S(1)} %pad_maximum_fusion.r0_ref), channel_id=1, source_target_pairs={{0,6},{1,7},{2,0},{3,1},{4,2},{5,3},{6,4},{7,5},{8,14},{9,15},{10,... | collective-permute-start | bytes 589832 | tf_op jit(solution)/shard_map/ppermute | solution.py:323
  78.0 15.2 %collective-permute-start.8 = (f32[384,256]{1,0:T(8,128)S(1)}, f32[384,256]{1,0:T(8,128)S(1)}, u32[]{:S(2)}, u32[]{:S(2)}) collective-permute-start(f32[384,256]{1,0:T(8,128)S(1)} %get-tuple-element.38), channel_id=1, source_target_pairs={{0,1},{1,0},{2,3},{3,2},{4,5},{5,4},{6,7},{7,6},{8,9},{9,8},{10,11... | collective-permute-start | bytes 1179656 | tf_op jit(solution)/shard_map/ppermute | solution.py:328
  93.1 22.3 %copy-start.2 = (f32[256,256]{1,0:T(8,128)S(1)}, f32[256,256]{1,0:T(8,128)}, u32[]{:S(2)}) copy-start(f32[256,256]{1,0:T(8,128)} %above.3) | copy-start | bytes 786436
  93.9 5.2 %collective-permute-start.9 = (f32[4,48,512]{2,1,0:T(8,128)S(1)}, f32[4,48,512]{2,1,0:T(8,128)S(1)}, u32[]{:S(2)}, u32[]{:S(2)}) collective-permute-start(f32[4,48,512]{2,1,0:T(8,128)S(1)} %get-tuple-element.41), channel_id=1, source_target_pairs={{0,1},{1,0},{2,3},{3,2},{4,5},{5,4},{6,7},{7,6},{8,9},{9,8},{10,11... | collective-permute-start | bytes 1179656 | tf_op jit(solution)/shard_map/ppermute | solution.py:330
  94.3 14.3 %all-to-all-start = ((f32[16,24,256]{2,1,0:T(8,128)}), f32[16,24,256]{2,1,0:T(8,128)S(1)}, u32[]{:S(2)}, u32[]{:S(2)}) async-start(f32[16,24,256]{2,1,0:T(8,128)} %bitcast.9), calls=%async_computation | async-start | bytes 786432 | tf_op jit(solution)/shard_map/all_to_all | solution.py:173
  99.2 40.5 %copy-start.7 = (s32[6,1]{0,1:T(1,128)S(1)}, s32[6,1]{0,1:T(1,128)}, u32[]{:S(2)}) copy-start(s32[6,1]{0,1:T(1,128)} %param.17) | copy-start | bytes 76
  99.3 58.4 %copy-start.8 = (f32[256,256]{1,0:T(8,128)S(1)}, f32[256,256]{1,0:T(8,128)}, u32[]{:S(2)}) copy-start(f32[256,256]{1,0:T(8,128)} %param.16) | copy-start | bytes 786436
  99.3 10.0 %collective-permute-start.10 = (f32[48,512]{1,0:T(8,128)S(1)}, f32[48,512]{1,0:T(8,128)S(1)}, u32[]{:S(2)}, u32[]{:S(2)}) collective-permute-start(f32[48,512]{1,0:T(8,128)S(1)} %get-tuple-element.57), channel_id=1, source_target_pairs={{0,2},{1,3},{2,4},{3,5},{4,6},{5,7},{6,0},{7,1},{8,10},{9,11},{10,... | collective-permute-start | bytes 294920 | tf_op jit(solution)/shard_map/ppermute | solution.py:333
  100.7 10.3 %collective-permute-start.11 = (f32[48,512]{1,0:T(8,128)S(1)}, f32[48,512]{1,0:T(8,128)S(1)}, u32[]{:S(2)}, u32[]{:S(2)}) collective-permute-start(f32[48,512]{1,0:T(8,128)S(1)} %get-tuple-element.56), channel_id=1, source_target_pairs={{0,4},{1,5},{2,6},{3,7},{4,0},{5,1},{6,2},{7,3},{8,12},{9,13},{10,... | collective-permute-start | bytes 294920 | tf_op jit(solution)/shard_map/ppermute | solution.py:333
  103.1 7.9 %collective-permute-start.12 = (f32[48,512]{1,0:T(8,128)S(1)}, f32[48,512]{1,0:T(8,128)S(1)}, u32[]{:S(2)}, u32[]{:S(2)}) collective-permute-start(f32[48,512]{1,0:T(8,128)S(1)} %get-tuple-element.55), channel_id=1, source_target_pairs={{0,6},{1,7},{2,0},{3,1},{4,2},{5,3},{6,4},{7,5},{8,14},{9,15},{10,... | collective-permute-start | bytes 294920 | tf_op jit(solution)/shard_map/ppermute | solution.py:333
  111.7 12.1 %all-to-all-start.1 = ((f32[8,24,256]{2,1,0:T(8,128)}), f32[8,24,256]{2,1,0:T(8,128)S(1)}, u32[]{:S(2)}, u32[]{:S(2)}) async-start(f32[8,24,256]{2,1,0:T(8,128)} %broadcast_in_dim.7), calls=%async_computation.1 | async-start | bytes 393216 | tf_op jit(solution)/shard_map/all_to_all | solution.py:178
  124.6 16.3 %all-to-all-start.2 = ((f32[16,24,256]{2,1,0:T(8,128)}), f32[16,24,256]{2,1,0:T(8,128)S(1)}, u32[]{:S(2)}, u32[]{:S(2)}) async-start(f32[16,24,256]{2,1,0:T(8,128)} %broadcast_in_dim.8), calls=%async_computation.2 | async-start | bytes 786432 | tf_op jit(solution)/shard_map/all_to_all | solution.py:178
  129.5 10.1 %collective-permute-start.13 = (f32[48,512]{1,0:T(8,128)S(1)}, f32[48,512]{1,0:T(8,128)S(1)}, u32[]{:S(2)}, u32[]{:S(2)}) collective-permute-start(f32[48,512]{1,0:T(8,128)S(1)} %inverse_rows.1), channel_id=1, source_target_pairs={{0,0},{1,8},{2,16},{3,24},{4,32},{5,40},{6,48},{7,56},{8,64},{9,72... | collective-permute-start | bytes 294920 | tf_op jit(solution)/shard_map/ppermute | solution.py:341
  140.9 1.7 %collective-permute-start.15 = (f32[8,8,256]{2,1,0:T(8,128)S(1)}, f32[8,8,256]{2,1,0:T(8,128)S(1)}, u32[]{:S(2)}, u32[]{:S(2)}) collective-permute-start(f32[8,8,256]{2,1,0:T(8,128)S(1)} %get-tuple-element.54), channel_id=1, source_target_pairs={{0,1},{1,0},{2,3},{3,2},{4,5},{5,4},{6,7},{7,6},{8,9},{9,8},{10,11... | collective-permute-start | bytes 196616 | tf_op jit(solution)/shard_map/ppermute | solution.py:258
  140.9 19.1 %collective-permute-start.14 = (f32[384,256]{1,0:T(8,128)S(1)}, f32[384,256]{1,0:T(8,128)S(1)}, u32[]{:S(2)}, u32[]{:S(2)}) collective-permute-start(f32[384,256]{1,0:T(8,128)S(1)} %bitcast.33), channel_id=1, source_target_pairs={{0,1},{1,0},{2,3},{3,2},{4,5},{5,4},{6,7},{7,6},{8,9},{9,8},{10,11... | collective-permute-start | bytes 1179656 | tf_op jit(solution)/shard_map/ppermute | solution.py:340
  142.6 15.7 %collective-permute-start.16 = (f32[2,2,8,256]{3,2,1,0:T(8,128)S(1)}, f32[2,2,8,256]{3,2,1,0:T(8,128)S(1)}, u32[]{:S(2)}, u32[]{:S(2)}) collective-permute-start(f32[2,2,8,256]{3,2,1,0:T(8,128)S(1)} %get-tuple-element.61), channel_id=1, source_target_pairs={{0,2},{1,3},{2,4},{3,5},{4,6},{5,7},{6,0},{7,1},{8,10},{9,11},{10,... | collective-permute-start | bytes 98312 | tf_op jit(solution)/shard_map/ppermute | solution.py:262
  151.3 7.1 %collective-permute-start.17 = (f32[2,2,8,256]{3,2,1,0:T(8,128)S(1)}, f32[2,2,8,256]{3,2,1,0:T(8,128)S(1)}, u32[]{:S(2)}, u32[]{:S(2)}) collective-permute-start(f32[2,2,8,256]{3,2,1,0:T(8,128)S(1)} %get-tuple-element.62), channel_id=1, source_target_pairs={{0,4},{1,5},{2,6},{3,7},{4,0},{5,1},{6,2},{7,3},{8,12},{9,13},{10,... | collective-permute-start | bytes 98312 | tf_op jit(solution)/shard_map/ppermute | solution.py:262
  155.8 3.0 %collective-permute-start.18 = (f32[2,2,8,256]{3,2,1,0:T(8,128)S(1)}, f32[2,2,8,256]{3,2,1,0:T(8,128)S(1)}, u32[]{:S(2)}, u32[]{:S(2)}) collective-permute-start(f32[2,2,8,256]{3,2,1,0:T(8,128)S(1)} %get-tuple-element.59), channel_id=1, source_target_pairs={{0,6},{1,7},{2,0},{3,1},{4,2},{5,3},{6,4},{7,5},{8,14},{9,15},{10,... | collective-permute-start | bytes 98312 | tf_op jit(solution)/shard_map/ppermute | solution.py:262

commit v5 on v4

--- a/solution.py
+++ b/solution.py
@@ -49,6 +49,10 @@
     return moves(lambda y, z, x, k: ((y + step) % N_Y, z, x, k))
 
 
+def along_z(step):
+    return moves(lambda y, z, x, k: (y, (z + step) % N_Z, x, k))
+
+
 def along_x(step):
     return moves(lambda y, z, x, k: (y, z, (x + step) % N_X, k))
 
@@ -57,7 +61,24 @@
     return moves(lambda y, z, x, k: (y, z, x, 1 - k))
 
 
-def mask_kernel(start, one_ref, two_ref, panel_one, panel_two, panels, masks):
+def mask_kernel(
+    start, one_hbm, two_hbm, panel_one_hbm, panel_two_hbm, panels, masks,
+    one_ref, two_ref, panel_one, panel_two, sems,
+):
+    pairs = (
+        (one_hbm, one_ref),
+        (two_hbm, two_ref),
+        (panel_one_hbm, panel_one),
+        (panel_two_hbm, panel_two),
+    )
+    copies = [
+        pltpu.make_async_copy(source, target, sems.at[i])
+        for i, (source, target) in enumerate(pairs)
+    ]
+    for copy in copies:
+        copy.start()
+    for copy in copies:
+        copy.wait()
     rows = start[0] + lax.broadcasted_iota(jnp.int32, (ROWS, 128), 0)
     for part, (listed, panel) in enumerate(((one_ref, panel_one), (two_ref, panel_two))):
         hit = jnp.zeros((ROWS, 128), jnp.float32)
@@ -71,14 +92,26 @@
 
 def masked_panels(start, struct_one, struct_two, panel_one, panel_two):
     shape = jax.ShapeDtypeStruct((ROWS, 2 * WIDTH), jnp.float32)
+    one, two = struct_one.reshape(-1, 128), struct_two.reshape(-1, 128)
+    fetched = [
+        pltpu.with_memory_space_constraint(value, pltpu.HBM)
+        for value in (one, two, panel_one, panel_two)
+    ]
     return pl.pallas_call(
         mask_kernel,
-        in_specs=[SMEM] + [VMEM] * 4,
+        in_specs=[SMEM] + [pl.BlockSpec(memory_space=pltpu.HBM)] * 4,
         out_specs=[VMEM] * 2,
         out_shape=[shape, shape],
+        scratch_shapes=[
+            pltpu.VMEM(one.shape, jnp.int32),
+            pltpu.VMEM(two.shape, jnp.int32),
+            pltpu.VMEM((ROWS, WIDTH), jnp.float32),
+            pltpu.VMEM((ROWS, WIDTH), jnp.float32),
+            pltpu.SemaphoreType.DMA((4,)),
+        ],
         compiler_params=SMALL,
         name="masked_panels",
-    )(start, struct_one.reshape(-1, 128), struct_two.reshape(-1, 128), panel_one, panel_two)
+    )(start, *fetched)
 
 
 def dot(left, right, dims=((1,), (0,)), precision=lax.Precision.HIGHEST):
@@ -101,18 +134,35 @@
     return one(a, c) + (one(a, d) + one(b, c))
 
 
-def product_kernel(
-    place, a_ref, g0_ref, g1_ref, g2_ref, g3_ref, r0_ref, r1_ref, r2_ref, r3_ref,
-    w_keep, w_send, y_keep, y_send, xh, xl, rh, rl, w_all, y_all,
-):
-    y, column, k = place[0], place[1], place[2]
-    for step, g_ref in enumerate((g0_ref, g1_ref, g2_ref, g3_ref)):
+RING = (0, -1, 1, -2, 2, -3, 3)
+BATCHES = ((0, -1, 1, -2, 2), (-3, 3), (4,))
+
+
+def product_kernel(place, a_ref, *refs):
+    ring, (last_own, last_far) = refs[:7], refs[7:9]
+    above, below = refs[9:12], refs[12:15]
+    r0_ref, r1_ref, r2_ref, r3_ref = refs[15:19]
+    w_keep, w_send, y_keep, y_send, xh, xl, rh, rl, w_all, y_all = refs[19:]
+    y, column, k, z = place[0], place[1], place[2], place[3]
+
+    def put(step, offset, values):
         x = lax.rem(y + step, N_X)
-        for q in range(4):
-            high, low = split(g_ref[pl.ds(q * 96, 96), :])
-            at = pl.multiple_of(q * 384 + x * 96, 32)
-            xh[pl.ds(at, 96), :] = high
-            xl[pl.ds(at, 96), :] = low
+        at = lax.rem(z + N_Z + offset, N_Z)
+        first = lax.div(at, 2) * 384 + x * 96 + lax.rem(at, 2) * ROWS
+        first = pl.multiple_of(first, 16)
+        high, low = split(values)
+        xh[pl.ds(first, ROWS), :] = high
+        xl[pl.ds(first, ROWS), :] = low
+
+    for offset, ref in zip(RING, ring):
+        put(0, offset, ref[:ROWS])
+        put(2, offset, ref[ROWS:])
+    put(0, 4, last_own[...])
+    put(2, 4, last_far[...])
+    for step, batches in ((1, above), (3, below)):
+        for offsets, ref in zip(BATCHES, batches):
+            for i, offset in enumerate(offsets):
+                put(step, offset, ref[i * ROWS : (i + 1) * ROWS])
     for step, r_ref in enumerate((r0_ref, r1_ref, r2_ref, r3_ref)):
         x = lax.rem(column + N_X - step, N_X)
         for part, core in ((0, k), (1, 1 - k)):
@@ -140,13 +190,13 @@
         y_send[step] = y_all[x * N_K + 1 - k]
 
 
-def product_and_grams(place, ancestor, gathered, row_panels):
+def product_and_grams(place, ancestor, gathered):
     f32, bf16 = jnp.float32, jnp.bfloat16
     half = 3 * WIDTH // 2
     wide = 2 * WIDTH
     return pl.pallas_call(
         product_kernel,
-        in_specs=[SMEM] + [VMEM] * 9,
+        in_specs=[SMEM] + [VMEM] * 20,
         out_specs=[VMEM] * 4,
         out_shape=[
             jax.ShapeDtypeStruct((half, WIDTH), f32),
@@ -164,7 +214,7 @@
         ],
         compiler_params=pltpu.CompilerParams(vmem_limit_bytes=24 * 1024 * 1024),
         name="product_and_grams",
-    )(place, ancestor, *gathered, *row_panels)
+    )(place, ancestor, *gathered)
 
 
 def at_owner(value, axis):
@@ -252,15 +302,13 @@
     )(place, *parts)
 
 
-def deliver(place, tile_owner, rows):
-    inverse_one, keep, send = pick_tiles(place, tile_owner, rows)
+def deliver(place, keep, arrived):
     shape = (N_X, CAP, TILE_ROWS, WIDTH)
-    arrived = lax.ppermute(send, ROW_COL, other_core())
     pairs = jnp.stack([keep.reshape(shape), arrived.reshape(shape)], axis=1)
     parts = [pairs[0]]
     for step in range(1, N_X):
         parts.append(lax.ppermute(pairs[step], ROW_COL, along_x(step)))
-    return inverse_one, fill_slots(place, parts)
+    return fill_slots(place, parts)
 
 
 def final_kernel(place, half, other, square_one, square_two, above, diag_one, cross_two, diag_two, w):
@@ -304,7 +352,7 @@
     tile_owner,
 ):
     start = (lax.axis_index(ROW) * N_COL + lax.axis_index(COL)) * ROWS
-    place = jnp.stack([lax.axis_index(name) for name in ("row_0", "col_0", "col_1")])
+    place = jnp.stack([lax.axis_index(name) for name in ("row_0", "col_0", "col_1", "row_1")])
     place = place.astype(jnp.int32)
     panels, masks = masked_panels(
         start.astype(jnp.int32)[None], struct_one, struct_two, panel_one, panel_two
@@ -314,16 +362,29 @@
     sibling = lax.ppermute(panels, ROW_COL, other_core())
     block, far_block, sibling = lax.optimization_barrier((block, far_block, sibling))
     pair = jnp.stack([panels, sibling])
-    gathered = lax.all_gather(block, "row_1", axis=0, tiled=True)
-    above = lax.ppermute(gathered, ROW_COL, along_y(-1))
-    below = lax.ppermute(gathered, ROW_COL, along_y(1))
-    far_block, pair, _ = lax.optimization_barrier((far_block, pair, gathered))
+    both = jnp.concatenate([block, far_block], axis=0)
+    ring = [both]
+    up = down = both
+    for _ in range(3):
+        up = lax.ppermute(up, ROW_COL, along_z(1))
+        down = lax.ppermute(down, ROW_COL, along_z(-1))
+        ring += [up, down]
+    last_own = lax.ppermute(up[:ROWS], ROW_COL, along_z(1))
+    last_far = lax.ppermute(down[ROWS:], ROW_COL, along_z(-1))
+    batches = (
+        jnp.concatenate([part[:ROWS] for part in ring[:5]], axis=0),
+        jnp.concatenate([part[:ROWS] for part in ring[5:]], axis=0),
+        last_own,
+    )
+    above = [lax.ppermute(batch, ROW_COL, along_y(-1)) for batch in batches]
+    below = [lax.ppermute(batch, ROW_COL, along_y(1)) for batch in batches]
     row_panels = [pair]
     for step in range(1, N_X):
         row_panels.append(lax.ppermute(pair, ROW_COL, along_x(step)))
-    far = lax.all_gather(far_block, "row_1", axis=0, tiled=True)
     w_keep, w_send, y_keep, y_send = product_and_grams(
-        place, ancestor_inverse, (gathered, above, far, below), row_panels
+        place,
+        ancestor_inverse,
+        (*ring, last_own, last_far, *above, *below, *row_panels),
     )
     w_own = w_keep + lax.ppermute(w_send, ROW_COL, other_core())
     y_send, w_own = lax.optimization_barrier((y_send, w_own))
@@ -332,14 +393,16 @@
     for step in range(1, N_X):
         y_parts.append(lax.ppermute(y_own[step], ROW_COL, along_x(step)))
     w_part = jnp.sum(at_owner(w_own, PLANE), axis=0)
-    w_part, y_parts = lax.optimization_barrier((w_part, y_parts))
-    w_part = jnp.sum(copies_of(w_part, "row_1"), axis=0)
     inverses = inverse_rows(y_parts, masks, panel_above)
-    w_part, _ = lax.optimization_barrier((w_part, inverses))
-    w_half = copies_of(w_part, PLANE).reshape(w_own.shape)
+    w_part, inverses = lax.optimization_barrier((w_part, inverses))
+    inverses = lax.ppermute(inverses, ROW_COL, moves(result_place))
+    w_parts, inverses = lax.optimization_barrier((copies_of(w_part, "row_1"), inverses))
+    w_half = copies_of(jnp.sum(w_parts, axis=0), PLANE).reshape(w_own.shape)
+    inverse_one, keep, send = pick_tiles(place, tile_owner, inverses)
+    arrived = lax.ppermute(send, ROW_COL, other_core())
+    w_half, arrived = lax.optimization_barrier((w_half, arrived))
     w_other = lax.ppermute(w_half, ROW_COL, other_core())
-    inverses = lax.ppermute(inverses, ROW_COL, moves(result_place))
-    inverse_one, delivered = deliver(place, tile_owner, inverses)
+    delivered = deliver(place, keep, arrived)
     square_one = dot(lower_one, lower_one, ((0,), (0,)))
     square_two = dot(lower_two, lower_two, ((0,), (0,)))
     diag_one, cross_two, diag_two = final_blocks(

time: 164 us -> 145 us (0.88)
  blocking collectives: 43.7 us -> 0 us
  waiting for transfers between devices: 28.2 us -> 49.2 us
  starting transfers between devices: 73.1 us -> 80.4 us
  local copies, waits for them, and re-layouts: 4.81 us -> 1.6 us
    all_gather x2 -> x0, blocking collectives: 43.7 us -> none  [the longest x1 22.8 us: local(): gathered = lax.all_gather(block, 'row_1', axis=0, tiled=True)]
    ppermute x3 -> x15, waiting for transfers between devices: 0.01 us -> 19.5 us  [the longest x3 7 us: local(): down = lax.ppermute(down, ROW_COL, along_z(-1))]
    ppermute x3 -> x15, starting transfers between devices: 3.29 us -> 15.5 us  [the longest x3 6.17 us: local(): up = lax.ppermute(up, ROW_COL, along_z(1))]
    ppermute x3, starting transfers between devices: 15.1 us -> 3.07 us  [deliver(): parts.append(lax.ppermute(pairs[step], ROW_COL, along_x(step)))]
    all_to_all x2, starting transfers between devices: 8.51 us -> 15.7 us  [copies_of(): return lax.all_to_all(copies, axis, 0, 0, tiled=True)]
    ppermute x1, starting transfers between devices: 13.8 us -> 9.63 us  [local(): w_own = w_keep + lax.ppermute(w_send, ROW_COL, other_core())]
    all_to_all x2, waiting for transfers between devices: 8.21 us -> 4.22 us  [copies_of(): return lax.all_to_all(copies, axis, 0, 0, tiled=True)]
    ppermute x3, starting transfers between devices: 4.13 us -> 7.78 us  [local(): row_panels.append(lax.ppermute(pair, ROW_COL, along_x(step)))]
  transfers between devices with their start and end apart: 22 -> 34, of which waited for: 9 -> 19; matrix products, arithmetic and copies ran while one was open for 1% -> 1% of each run, Pallas kernels for 2% -> 2%
where the time goes in v5:
time: 145 us
  starting transfers between devices  80.4 us (55%)
  waiting for transfers between devices  49.2 us (34%)
  Pallas kernels  10.7 us (7%)
  local copies, waits for them, and re-layouts  1.6 us (1%)
    all_to_all x2, starting transfers between devices, copies_of(): return lax.all_to_all(copies, axis, 0, 0, tiled=True)  15.7 us
    ppermute x1, starting transfers between devices, local(): w_own = w_keep + lax.ppermute(w_send, ROW_COL, other_core())  9.63 us
    ppermute x3, starting transfers between devices, local(): row_panels.append(lax.ppermute(pair, ROW_COL, along_x(step)))  7.78 us
    ppermute x3, waiting for transfers between devices, local(): down = lax.ppermute(down, ROW_COL, along_z(-1))  7 us
    ppermute x1, starting transfers between devices, local(): far_block = lax.ppermute(panels, ROW_COL, to_column(2))  6.87 us
    ppermute x1, waiting for transfers between devices, local(): inverses = lax.ppermute(inverses, ROW_COL, moves(result_place))  6.85 us
    ppermute x3, starting transfers between devices, local(): up = lax.ppermute(up, ROW_COL, along_z(1))  6.17 us
    ppermute x1, waiting for transfers between devices, local(): far_block = lax.ppermute(panels, ROW_COL, to_column(2))  5.89 us
  transfers between devices with their start and end apart: 34, of which 19 were waited for; matrix products, arithmetic and copies ran while one was open for 1% of the time, Pallas kernels for 2%

profile of v5, /device:TPU:1, one launch (start us, length us, event | category | flops | bytes accessed | tf_op | source)
XLA Modules:
  0.0 145.0 jit_solution(13677475026559877902)
XLA Ops:
  0.7 1.4 masked_panels.1
  2.1 4.9 %collective-permute-start = (f32[48,512]{1,0:T(8,128)S(1)}, f32[48,512]{1,0:T(8,128)S(1)}, u32[]{:S(2)}, u32[]{:S(2)}) collective-permute-start(f32[48,512]{1,0:T(8,128)S(1)} %get-tuple-element.28), channel_id=1, source_target_pairs={{0,0},{1,8},{2,64},{3,72},{4,128},{5,136},{6,192},{7,200},{8,16},{... | collective-permute-start | bytes 294920 | tf_op jit(solution)/shard_map/ppermute | solution.py:360
  7.0 6.9 %collective-permute-start.1 = (f32[48,512]{1,0:T(8,128)S(1)}, f32[48,512]{1,0:T(8,128)S(1)}, u32[]{:S(2)}, u32[]{:S(2)}) collective-permute-start(f32[48,512]{1,0:T(8,128)S(1)} %get-tuple-element.28), channel_id=1, source_target_pairs={{0,128},{1,136},{2,192},{3,200},{4,0},{5,8},{6,64},{7,72},{8,144},... | collective-permute-start | bytes 294920 | tf_op jit(solution)/shard_map/ppermute | solution.py:361
  14.6 5.9 %collective-permute-done.1 = f32[48,512]{1,0:T(8,128)S(1)} collective-permute-done((f32[48,512]{1,0:T(8,128)S(1)}, f32[48,512]{1,0:T(8,128)S(1)}, u32[]{:S(2)}, u32[]{:S(2)}) %collective-permute-start.1) | collective-permute-done | bytes 98336 | tf_op jit(solution)/shard_map/ppermute | solution.py:361
  20.5 1.8 %collective-permute-start.3 = (f32[96,512]{1,0:T(8,128)S(1)}, f32[96,512]{1,0:T(8,128)S(1)}, u32[]{:S(2)}, u32[]{:S(2)}) collective-permute-start(f32[96,512]{1,0:T(8,128)S(1)} %constant_dynamic-update-slice_fusion.refs_0_), channel_id=1, source_target_pairs={{0,8},{1,9},{2,10},{3,11},{4,12},{5,13},{6,14},{7,15},{8,16},{9,17... | collective-permute-start | bytes 589832 | tf_op jit(solution)/shard_map/ppermute | solution.py:369
  23.4 3.6 %collective-permute-start.18 = (f32[2,48,512]{2,1,0:T(8,128)S(1)}, f32[2,48,512]{2,1,0:T(8,128)S(1)}, u32[]{:S(2)}, u32[]{:S(2)}) collective-permute-start(f32[2,48,512]{2,1,0:T(8,128)S(1)} %pad_maximum_fusion.1.refs_15_), channel_id=1, source_target_pairs={{0,4},{1,5},{2,6},{3,7},{4,0},{5,1},{6,2},{7,3},{8,12},{9,13},{10,... | collective-permute-start | bytes 589832 | tf_op jit(solution)/shard_map/ppermute | solution.py:383
  27.0 3.2 %collective-permute-start.5 = (f32[96,512]{1,0:T(8,128)S(1)}, f32[96,512]{1,0:T(8,128)S(1)}, u32[]{:S(2)}, u32[]{:S(2)}) collective-permute-start(f32[96,512]{1,0:T(8,128)S(1)} %collective-permute-done.3.refs_1_), channel_id=1, source_target_pairs={{0,8},{1,9},{2,10},{3,11},{4,12},{5,13},{6,14},{7,15},{8,16},{9,17... | collective-permute-start | bytes 589832 | tf_op jit(solution)/shard_map/ppermute | solution.py:369
  30.3 5.5 %collective-permute-done.6.refs_4_ = f32[96,512]{1,0:T(8,128)S(1)} collective-permute-done((f32[96,512]{1,0:T(8,128)S(1)}, f32[96,512]{1,0:T(8,128)S(1)}, u32[]{:S(2)}, u32[]{:S(2)}) %collective-permute-start.6) | collective-permute-done | bytes 196640 | tf_op jit(solution)/shard_map/ppermute | solution.py:370
  36.4 2.5 %collective-permute-start.11 = (f32[240,512]{1,0:T(8,128)S(1)}, f32[240,512]{1,0:T(8,128)S(1)}, u32[]{:S(2)}, u32[]{:S(2)}) collective-permute-start(f32[240,512]{1,0:T(8,128)S(1)} %slice_dynamic-update-slice_fusion), channel_id=1, source_target_pairs={{0,192},{1,193},{2,194},{3,195},{4,196},{5,197},{6,198},{7,199},{8... | collective-permute-start | bytes 1474568 | tf_op jit(solution)/shard_map/ppermute | solution.py:379
  38.9 1.5 %collective-permute-done.8.refs_6_ = f32[96,512]{1,0:T(8,128)S(1)} collective-permute-done((f32[96,512]{1,0:T(8,128)S(1)}, f32[96,512]{1,0:T(8,128)S(1)}, u32[]{:S(2)}, u32[]{:S(2)}) %collective-permute-start.8) | collective-permute-done | bytes 196640 | tf_op jit(solution)/shard_map/ppermute | solution.py:370
  41.5 4.7 %collective-permute-done.7.refs_5_ = f32[96,512]{1,0:T(8,128)S(1)} collective-permute-done((f32[96,512]{1,0:T(8,128)S(1)}, f32[96,512]{1,0:T(8,128)S(1)}, u32[]{:S(2)}, u32[]{:S(2)}) %collective-permute-start.7) | collective-permute-done | bytes 196640 | tf_op jit(solution)/shard_map/ppermute | solution.py:369
  46.2 4.1 %collective-permute-start.19 = (f32[2,48,512]{2,1,0:T(8,128)S(1)}, f32[2,48,512]{2,1,0:T(8,128)S(1)}, u32[]{:S(2)}, u32[]{:S(2)}) collective-permute-start(f32[2,48,512]{2,1,0:T(8,128)S(1)} %pad_maximum_fusion.1.refs_15_), channel_id=1, source_target_pairs={{0,6},{1,7},{2,0},{3,1},{4,2},{5,3},{6,4},{7,5},{8,14},{9,15},{10,... | collective-permute-start | bytes 589832 | tf_op jit(solution)/shard_map/ppermute | solution.py:383
  50.6 2.4 %collective-permute-done.19.refs_18_ = f32[2,48,512]{2,1,0:T(8,128)S(1)} collective-permute-done((f32[2,48,512]{2,1,0:T(8,128)S(1)}, f32[2,48,512]{2,1,0:T(8,128)S(1)}, u32[]{:S(2)}, u32[]{:S(2)}) %collective-permute-start.19) | collective-permute-done | bytes 196640 | tf_op jit(solution)/shard_map/ppermute | solution.py:383
  53.2 2.0 %collective-permute-done.9.refs_7_ = f32[48,512]{1,0:T(8,128)S(1)} collective-permute-done((f32[48,512]{1,0:T(8,128)S(1)}, f32[48,512]{1,0:T(8,128)S(1)}, u32[]{:S(2)}, u32[]{:S(2)}) %collective-permute-start.9) | collective-permute-done | bytes 98336 | tf_op jit(solution)/shard_map/ppermute | solution.py:372
  55.2 1.4 collective-permute-start.15
  58.2 2.8 %collective-permute-done.15.refs_13_ = f32[96,512]{1,0:T(8,128)S(1)} collective-permute-done((f32[96,512]{1,0:T(8,128)S(1)}, f32[96,512]{1,0:T(8,128)S(1)}, u32[]{:S(2)}, u32[]{:S(2)}) %collective-permute-start.15) | collective-permute-done | bytes 196640 | tf_op jit(solution)/shard_map/ppermute | solution.py:380
  61.0 2.0 %collective-permute-done.16.refs_14_ = f32[48,512]{1,0:T(8,128)S(1)} collective-permute-done((f32[48,512]{1,0:T(8,128)S(1)}, f32[48,512]{1,0:T(8,128)S(1)}, u32[]{:S(2)}, u32[]{:S(2)}) %collective-permute-start.16) | collective-permute-done | bytes 98336 | tf_op jit(solution)/shard_map/ppermute | solution.py:380
  63.0 3.9 %product_and_grams.1 = (f32[384,256]{1,0:T(8,128)S(1)}, f32[384,256]{1,0:T(8,128)S(1)}, f32[4,48,512]{2,1,0:T(8,128)S(1)}, f32[4,48,512]{2,1,0:T(8,128)S(1)}) custom-call(s32[4]{0:T(128)S(1)} %pad_add_fusion.place, f32[384,1536]{1,0:T(8,128)S(1)} %copy-done.1, f32[96,512]{1,0:T(8,128)S(1)} %constant_dynamic-update-slice_fusion.refs_0_, ...), custom_call_target="tpu_custom_call" | custom-call | tf_op jit(solution)/shard_map/product_and_grams/pallas_call | solution.py:197
  67.0 9.6 %collective-permute-start.20 = (f32[384,256]{1,0:T(8,128)S(1)}, f32[384,256]{1,0:T(8,128)S(1)}, u32[]{:S(2)}, u32[]{:S(2)}) collective-permute-start(f32[384,256]{1,0:T(8,128)S(1)} %get-tuple-element.34), channel_id=1, source_target_pairs={{0,1},{1,0},{2,3},{3,2},{4,5},{5,4},{6,7},{7,6},{8,9},{9,8},{10,11... | collective-permute-start | bytes 1179656 | tf_op jit(solution)/shard_map/ppermute | solution.py:389
  79.1 3.6 %all-to-all-start = ((f32[16,24,256]{2,1,0:T(8,128)}), f32[16,24,256]{2,1,0:T(8,128)S(1)}, u32[]{:S(2)}, u32[]{:S(2)}) async-start(f32[16,24,256]{2,1,0:T(8,128)} %bitcast.10), calls=%async_computation | async-start | bytes 786432 | tf_op jit(solution)/shard_map/all_to_all | solution.py:223
  84.2 2.4 %collective-permute-start.23 = (f32[48,512]{1,0:T(8,128)S(1)}, f32[48,512]{1,0:T(8,128)S(1)}, u32[]{:S(2)}, u32[]{:S(2)}) collective-permute-start(f32[48,512]{1,0:T(8,128)S(1)} %get-tuple-element.52), channel_id=1, source_target_pairs={{0,4},{1,5},{2,6},{3,7},{4,0},{5,1},{6,2},{7,3},{8,12},{9,13},{10,... | collective-permute-start | bytes 294920 | tf_op jit(solution)/shard_map/ppermute | solution.py:394
  87.7 4.5 %all-to-all-done = f32[16,24,256]{2,1,0:T(8,128)S(1)} async-done(((f32[16,24,256]{2,1,0:T(8,128)}), f32[16,24,256]{2,1,0:T(8,128)S(1)}, u32[]{:S(2)}, u32[]{:S(2)}) %all-to-all-start) | async-done | bytes 393248 | tf_op jit(solution)/shard_map/all_to_all | solution.py:223
  92.8 1.7 %collective-permute-done.23.y2 = f32[48,512]{1,0:T(8,128)S(1)} collective-permute-done((f32[48,512]{1,0:T(8,128)S(1)}, f32[48,512]{1,0:T(8,128)S(1)}, u32[]{:S(2)}, u32[]{:S(2)}) %collective-permute-start.23) | collective-permute-done | bytes 98336 | tf_op jit(solution)/shard_map/ppermute | solution.py:394
  95.4 6.4 %all-to-all-start.1 = ((f32[8,24,256]{2,1,0:T(8,128)}), f32[8,24,256]{2,1,0:T(8,128)S(1)}, u32[]{:S(2)}, u32[]{:S(2)}) async-start(f32[8,24,256]{2,1,0:T(8,128)} %broadcast_in_dim.7), calls=%async_computation.1 | async-start | bytes 393216 | tf_op jit(solution)/shard_map/all_to_all | solution.py:228
  101.9 5.0 %collective-permute-start.25 = (f32[48,512]{1,0:T(8,128)S(1)}, f32[48,512]{1,0:T(8,128)S(1)}, u32[]{:S(2)}, u32[]{:S(2)}) collective-permute-start(f32[48,512]{1,0:T(8,128)S(1)} %inverse_rows.1), channel_id=1, source_target_pairs={{0,0},{1,8},{2,16},{3,24},{4,32},{5,40},{6,48},{7,56},{8,64},{9,72... | collective-permute-start | bytes 294920 | tf_op jit(solution)/shard_map/ppermute | solution.py:398
  106.9 6.8 %collective-permute-done.25.rows = f32[48,512]{1,0:T(8,128)S(1)} collective-permute-done((f32[48,512]{1,0:T(8,128)S(1)}, f32[48,512]{1,0:T(8,128)S(1)}, u32[]{:S(2)}, u32[]{:S(2)}) %collective-permute-start.25) | collective-permute-done | bytes 98336 | tf_op jit(solution)/shard_map/ppermute | solution.py:398
  114.6 9.3 %all-to-all-start.2 = ((f32[16,24,256]{2,1,0:T(8,128)}), f32[16,24,256]{2,1,0:T(8,128)S(1)}, u32[]{:S(2)}, u32[]{:S(2)}) async-start(f32[16,24,256]{2,1,0:T(8,128)} %broadcast_in_dim.8), calls=%async_computation.2 | async-start | bytes 786432 | tf_op jit(solution)/shard_map/all_to_all | solution.py:228
  125.2 2.0 %collective-permute-start.26 = (f32[8,8,256]{2,1,0:T(8,128)S(1)}, f32[8,8,256]{2,1,0:T(8,128)S(1)}, u32[]{:S(2)}, u32[]{:S(2)}) collective-permute-start(f32[8,8,256]{2,1,0:T(8,128)S(1)} %get-tuple-element.44), channel_id=1, source_target_pairs={{0,1},{1,0},{2,3},{3,2},{4,5},{5,4},{6,7},{7,6},{8,9},{9,8},{10,11... | collective-permute-start | bytes 196616 | tf_op jit(solution)/shard_map/ppermute | solution.py:402
  128.0 4.2 %all-to-all-done.2 = f32[16,24,256]{2,1,0:T(8,128)S(1)} async-done(((f32[16,24,256]{2,1,0:T(8,128)}), f32[16,24,256]{2,1,0:T(8,128)S(1)}, u32[]{:S(2)}, u32[]{:S(2)}) %all-to-all-start.2) | async-done | bytes 393248 | tf_op jit(solution)/shard_map/all_to_all | solution.py:228
  132.2 3.0 %collective-permute-start.27 = (f32[384,256]{1,0:T(8,128)S(1)}, f32[384,256]{1,0:T(8,128)S(1)}, u32[]{:S(2)}, u32[]{:S(2)}) collective-permute-start(f32[384,256]{1,0:T(8,128)S(1)} %bitcast.34), channel_id=1, source_target_pairs={{0,1},{1,0},{2,3},{3,2},{4,5},{5,4},{6,7},{7,6},{8,9},{9,8},{10,11... | collective-permute-start | bytes 1179656 | tf_op jit(solution)/shard_map/ppermute | solution.py:404
  137.4 1.5 %collective-permute-start.30 = (f32[2,2,8,256]{3,2,1,0:T(8,128)S(1)}, f32[2,2,8,256]{3,2,1,0:T(8,128)S(1)}, u32[]{:S(2)}, u32[]{:S(2)}) collective-permute-start(f32[2,2,8,256]{3,2,1,0:T(8,128)S(1)} %get-tuple-element.57), channel_id=1, source_target_pairs={{0,6},{1,7},{2,0},{3,1},{4,2},{5,3},{6,4},{7,5},{8,14},{9,15},{10,... | collective-permute-start | bytes 98312 | tf_op jit(solution)/shard_map/ppermute | solution.py:310
  142.3 2.6 %final_blocks.1 = (f32[256,256]{1,0:T(8,128)}, f32[256,256]{1,0:T(8,128)}, f32[256,256]{1,0:T(8,128)}) custom-call(s32[4]{0:T(128)S(1)} %pad_add_fusion.place, f32[384,256]{1,0:T(8,128)S(1)} %bitcast.35, f32[384,256]{1,0:T(8,128)S(1)} %collective-permute-done.27.other, f32[256,256]{1,0:T(8,128)S(1)} %fusion.8.square_one, f32[256,256]{1,0:T(8,128)S(1)} %fusion.9.square_two, ...), custom_call_target="tpu_custom_call" | custom-call | tf_op jit(solution)/shard_map/final_blocks/pallas_call | solution.py:332
  (73 shorter events, 20.7 us)
Async XLA Ops:
  2.1 12.5 %collective-permute-start = (f32[48,512]{1,0:T(8,128)S(1)}, f32[48,512]{1,0:T(8,128)S(1)}, u32[]{:S(2)}, u32[]{:S(2)}) collective-permute-start(f32[48,512]{1,0:T(8,128)S(1)} %get-tuple-element.28), channel_id=1, source_target_pairs={{0,0},{1,8},{2,64},{3,72},{4,128},{5,136},{6,192},{7,200},{8,16},{... | collective-permute-start | bytes 294920 | tf_op jit(solution)/shard_map/ppermute | solution.py:360
  7.0 13.4 %collective-permute-start.1 = (f32[48,512]{1,0:T(8,128)S(1)}, f32[48,512]{1,0:T(8,128)S(1)}, u32[]{:S(2)}, u32[]{:S(2)}) collective-permute-start(f32[48,512]{1,0:T(8,128)S(1)} %get-tuple-element.28), channel_id=1, source_target_pairs={{0,128},{1,136},{2,192},{3,200},{4,0},{5,8},{6,64},{7,72},{8,144},... | collective-permute-start | bytes 294920 | tf_op jit(solution)/shard_map/ppermute | solution.py:361
  13.9 6.6 %collective-permute-start.2 = (f32[48,512]{1,0:T(8,128)S(1)}, f32[48,512]{1,0:T(8,128)S(1)}, u32[]{:S(2)}, u32[]{:S(2)}) collective-permute-start(f32[48,512]{1,0:T(8,128)S(1)} %get-tuple-element.28), channel_id=1, source_target_pairs={{0,1},{1,0},{2,3},{3,2},{4,5},{5,4},{6,7},{7,6},{8,9},{9,8},{10,11... | collective-permute-start | bytes 294920 | tf_op jit(solution)/shard_map/ppermute | solution.py:362
  20.5 6.5 %collective-permute-start.3 = (f32[96,512]{1,0:T(8,128)S(1)}, f32[96,512]{1,0:T(8,128)S(1)}, u32[]{:S(2)}, u32[]{:S(2)}) collective-permute-start(f32[96,512]{1,0:T(8,128)S(1)} %constant_dynamic-update-slice_fusion.refs_0_), channel_id=1, source_target_pairs={{0,8},{1,9},{2,10},{3,11},{4,12},{5,13},{6,14},{7,15},{8,16},{9,17... | collective-permute-start | bytes 589832 | tf_op jit(solution)/shard_map/ppermute | solution.py:369
  22.3 7.9 %collective-permute-start.4 = (f32[96,512]{1,0:T(8,128)S(1)}, f32[96,512]{1,0:T(8,128)S(1)}, u32[]{:S(2)}, u32[]{:S(2)}) collective-permute-start(f32[96,512]{1,0:T(8,128)S(1)} %constant_dynamic-update-slice_fusion.refs_0_), channel_id=1, source_target_pairs={{0,56},{1,57},{2,58},{3,59},{4,60},{5,61},{6,62},{7,63},{8,0},{9,1... | collective-permute-start | bytes 589832 | tf_op jit(solution)/shard_map/ppermute | solution.py:370
  23.3 27.1 %collective-permute-start.17 = (f32[2,48,512]{2,1,0:T(8,128)S(1)}, f32[2,48,512]{2,1,0:T(8,128)S(1)}, u32[]{:S(2)}, u32[]{:S(2)}) collective-permute-start(f32[2,48,512]{2,1,0:T(8,128)S(1)} %pad_maximum_fusion.1.refs_15_), channel_id=1, source_target_pairs={{0,2},{1,3},{2,4},{3,5},{4,6},{5,7},{6,0},{7,1},{8,10},{9,11},{10,... | collective-permute-start | bytes 589832 | tf_op jit(solution)/shard_map/ppermute | solution.py:383
  23.4 27.1 %collective-permute-start.18 = (f32[2,48,512]{2,1,0:T(8,128)S(1)}, f32[2,48,512]{2,1,0:T(8,128)S(1)}, u32[]{:S(2)}, u32[]{:S(2)}) collective-permute-start(f32[2,48,512]{2,1,0:T(8,128)S(1)} %pad_maximum_fusion.1.refs_15_), channel_id=1, source_target_pairs={{0,4},{1,5},{2,6},{3,7},{4,0},{5,1},{6,2},{7,3},{8,12},{9,13},{10,... | collective-permute-start | bytes 589832 | tf_op jit(solution)/shard_map/ppermute | solution.py:383
  27.0 9.4 %collective-permute-start.5 = (f32[96,512]{1,0:T(8,128)S(1)}, f32[96,512]{1,0:T(8,128)S(1)}, u32[]{:S(2)}, u32[]{:S(2)}) collective-permute-start(f32[96,512]{1,0:T(8,128)S(1)} %collective-permute-done.3.refs_1_), channel_id=1, source_target_pairs={{0,8},{1,9},{2,10},{3,11},{4,12},{5,13},{6,14},{7,15},{8,16},{9,17... | collective-permute-start | bytes 589832 | tf_op jit(solution)/shard_map/ppermute | solution.py:369
  30.2 5.6 %collective-permute-start.6 = (f32[96,512]{1,0:T(8,128)S(1)}, f32[96,512]{1,0:T(8,128)S(1)}, u32[]{:S(2)}, u32[]{:S(2)}) collective-permute-start(f32[96,512]{1,0:T(8,128)S(1)} %collective-permute-done.4.refs_2_), channel_id=1, source_target_pairs={{0,56},{1,57},{2,58},{3,59},{4,60},{5,61},{6,62},{7,63},{8,0},{9,1... | collective-permute-start | bytes 589832 | tf_op jit(solution)/shard_map/ppermute | solution.py:370
  35.8 4.5 %collective-permute-start.8 = (f32[96,512]{1,0:T(8,128)S(1)}, f32[96,512]{1,0:T(8,128)S(1)}, u32[]{:S(2)}, u32[]{:S(2)}) collective-permute-start(f32[96,512]{1,0:T(8,128)S(1)} %collective-permute-done.6.refs_4_), channel_id=1, source_target_pairs={{0,56},{1,57},{2,58},{3,59},{4,60},{5,61},{6,62},{7,63},{8,0},{9,1... | collective-permute-start | bytes 589832 | tf_op jit(solution)/shard_map/ppermute | solution.py:370
  36.4 26.7 %collective-permute-start.11 = (f32[240,512]{1,0:T(8,128)S(1)}, f32[240,512]{1,0:T(8,128)S(1)}, u32[]{:S(2)}, u32[]{:S(2)}) collective-permute-start(f32[240,512]{1,0:T(8,128)S(1)} %slice_dynamic-update-slice_fusion), channel_id=1, source_target_pairs={{0,192},{1,193},{2,194},{3,195},{4,196},{5,197},{6,198},{7,199},{8... | collective-permute-start | bytes 1474568 | tf_op jit(solution)/shard_map/ppermute | solution.py:379
  38.9 24.2 %collective-permute-start.14 = (f32[240,512]{1,0:T(8,128)S(1)}, f32[240,512]{1,0:T(8,128)S(1)}, u32[]{:S(2)}, u32[]{:S(2)}) collective-permute-start(f32[240,512]{1,0:T(8,128)S(1)} %slice_dynamic-update-slice_fusion), channel_id=1, source_target_pairs={{0,64},{1,65},{2,66},{3,67},{4,68},{5,69},{6,70},{7,71},{8,72},{9,... | collective-permute-start | bytes 1474568 | tf_op jit(solution)/shard_map/ppermute | solution.py:380
  40.4 5.9 %collective-permute-start.7 = (f32[96,512]{1,0:T(8,128)S(1)}, f32[96,512]{1,0:T(8,128)S(1)}, u32[]{:S(2)}, u32[]{:S(2)}) collective-permute-start(f32[96,512]{1,0:T(8,128)S(1)} %collective-permute-done.5.refs_3_), channel_id=1, source_target_pairs={{0,8},{1,9},{2,10},{3,11},{4,12},{5,13},{6,14},{7,15},{8,16},{9,17... | collective-permute-start | bytes 589832 | tf_op jit(solution)/shard_map/ppermute | solution.py:369
  46.2 6.7 %collective-permute-start.19 = (f32[2,48,512]{2,1,0:T(8,128)S(1)}, f32[2,48,512]{2,1,0:T(8,128)S(1)}, u32[]{:S(2)}, u32[]{:S(2)}) collective-permute-start(f32[2,48,512]{2,1,0:T(8,128)S(1)} %pad_maximum_fusion.1.refs_15_), channel_id=1, source_target_pairs={{0,6},{1,7},{2,0},{3,1},{4,2},{5,3},{6,4},{7,5},{8,14},{9,15},{10,... | collective-permute-start | bytes 589832 | tf_op jit(solution)/shard_map/ppermute | solution.py:383
  50.4 7.7 %collective-permute-start.12 = (f32[96,512]{1,0:T(8,128)S(1)}, f32[96,512]{1,0:T(8,128)S(1)}, u32[]{:S(2)}, u32[]{:S(2)}) collective-permute-start(f32[96,512]{1,0:T(8,128)S(1)} %pad_maximum_fusion), channel_id=1, source_target_pairs={{0,192},{1,193},{2,194},{3,195},{4,196},{5,197},{6,198},{7,199},{8... | collective-permute-start | bytes 589832 | tf_op jit(solution)/shard_map/ppermute | solution.py:379
  50.5 4.8 %collective-permute-start.9 = (f32[48,512]{1,0:T(8,128)S(1)}, f32[48,512]{1,0:T(8,128)S(1)}, u32[]{:S(2)}, u32[]{:S(2)}) collective-permute-start(f32[48,512]{1,0:T(8,128)S(1)} %slice.61), channel_id=1, source_target_pairs={{0,8},{1,9},{2,10},{3,11},{4,12},{5,13},{6,14},{7,15},{8,16},{9,17... | collective-permute-start | bytes 294920 | tf_op jit(solution)/shard_map/ppermute | solution.py:372
  55.2 5.7 %collective-permute-start.15 = (f32[96,512]{1,0:T(8,128)S(1)}, f32[96,512]{1,0:T(8,128)S(1)}, u32[]{:S(2)}, u32[]{:S(2)}) collective-permute-start(f32[96,512]{1,0:T(8,128)S(1)} %pad_maximum_fusion), channel_id=1, source_target_pairs={{0,64},{1,65},{2,66},{3,67},{4,68},{5,69},{6,70},{7,71},{8,72},{9,... | collective-permute-start | bytes 589832 | tf_op jit(solution)/shard_map/ppermute | solution.py:380
  56.7 4.3 %collective-permute-start.13 = (f32[48,512]{1,0:T(8,128)S(1)}, f32[48,512]{1,0:T(8,128)S(1)}, u32[]{:S(2)}, u32[]{:S(2)}) collective-permute-start(f32[48,512]{1,0:T(8,128)S(1)} %collective-permute-done.9.refs_7_), channel_id=1, source_target_pairs={{0,192},{1,193},{2,194},{3,195},{4,196},{5,197},{6,198},{7,199},{8... | collective-permute-start | bytes 294920 | tf_op jit(solution)/shard_map/ppermute | solution.py:379
  58.0 5.0 %collective-permute-start.16 = (f32[48,512]{1,0:T(8,128)S(1)}, f32[48,512]{1,0:T(8,128)S(1)}, u32[]{:S(2)}, u32[]{:S(2)}) collective-permute-start(f32[48,512]{1,0:T(8,128)S(1)} %collective-permute-done.9.refs_7_), channel_id=1, source_target_pairs={{0,64},{1,65},{2,66},{3,67},{4,68},{5,69},{6,70},{7,71},{8,72},{9,... | collective-permute-start | bytes 294920 | tf_op jit(solution)/shard_map/ppermute | solution.py:380
  67.0 11.0 %collective-permute-start.20 = (f32[384,256]{1,0:T(8,128)S(1)}, f32[384,256]{1,0:T(8,128)S(1)}, u32[]{:S(2)}, u32[]{:S(2)}) collective-permute-start(f32[384,256]{1,0:T(8,128)S(1)} %get-tuple-element.34), channel_id=1, source_target_pairs={{0,1},{1,0},{2,3},{3,2},{4,5},{5,4},{6,7},{7,6},{8,9},{9,8},{10,11... | collective-permute-start | bytes 1179656 | tf_op jit(solution)/shard_map/ppermute | solution.py:389
  78.8 3.9 %collective-permute-start.21 = (f32[4,48,512]{2,1,0:T(8,128)S(1)}, f32[4,48,512]{2,1,0:T(8,128)S(1)}, u32[]{:S(2)}, u32[]{:S(2)}) collective-permute-start(f32[4,48,512]{2,1,0:T(8,128)S(1)} %get-tuple-element.37), channel_id=1, source_target_pairs={{0,1},{1,0},{2,3},{3,2},{4,5},{5,4},{6,7},{7,6},{8,9},{9,8},{10,11... | collective-permute-start | bytes 1179656 | tf_op jit(solution)/shard_map/ppermute | solution.py:391
  79.1 13.1 %all-to-all-start = ((f32[16,24,256]{2,1,0:T(8,128)}), f32[16,24,256]{2,1,0:T(8,128)S(1)}, u32[]{:S(2)}, u32[]{:S(2)}) async-start(f32[16,24,256]{2,1,0:T(8,128)} %bitcast.10), calls=%async_computation | async-start | bytes 786432 | tf_op jit(solution)/shard_map/all_to_all | solution.py:223
  82.8 9.9 %collective-permute-start.22 = (f32[48,512]{1,0:T(8,128)S(1)}, f32[48,512]{1,0:T(8,128)S(1)}, u32[]{:S(2)}, u32[]{:S(2)}) collective-permute-start(f32[48,512]{1,0:T(8,128)S(1)} %get-tuple-element.53), channel_id=1, source_target_pairs={{0,2},{1,3},{2,4},{3,5},{4,6},{5,7},{6,0},{7,1},{8,10},{9,11},{10,... | collective-permute-start | bytes 294920 | tf_op jit(solution)/shard_map/ppermute | solution.py:394
  84.2 10.3 %collective-permute-start.23 = (f32[48,512]{1,0:T(8,128)S(1)}, f32[48,512]{1,0:T(8,128)S(1)}, u32[]{:S(2)}, u32[]{:S(2)}) collective-permute-start(f32[48,512]{1,0:T(8,128)S(1)} %get-tuple-element.52), channel_id=1, source_target_pairs={{0,4},{1,5},{2,6},{3,7},{4,0},{5,1},{6,2},{7,3},{8,12},{9,13},{10,... | collective-permute-start | bytes 294920 | tf_op jit(solution)/shard_map/ppermute | solution.py:394
  86.6 7.9 %collective-permute-start.24 = (f32[48,512]{1,0:T(8,128)S(1)}, f32[48,512]{1,0:T(8,128)S(1)}, u32[]{:S(2)}, u32[]{:S(2)}) collective-permute-start(f32[48,512]{1,0:T(8,128)S(1)} %get-tuple-element.51), channel_id=1, source_target_pairs={{0,6},{1,7},{2,0},{3,1},{4,2},{5,3},{6,4},{7,5},{8,14},{9,15},{10,... | collective-permute-start | bytes 294920 | tf_op jit(solution)/shard_map/ppermute | solution.py:394
  95.4 18.3 %all-to-all-start.1 = ((f32[8,24,256]{2,1,0:T(8,128)}), f32[8,24,256]{2,1,0:T(8,128)S(1)}, u32[]{:S(2)}, u32[]{:S(2)}) async-start(f32[8,24,256]{2,1,0:T(8,128)} %broadcast_in_dim.7), calls=%async_computation.1 | async-start | bytes 393216 | tf_op jit(solution)/shard_map/all_to_all | solution.py:228
  101.9 11.9 %collective-permute-start.25 = (f32[48,512]{1,0:T(8,128)S(1)}, f32[48,512]{1,0:T(8,128)S(1)}, u32[]{:S(2)}, u32[]{:S(2)}) collective-permute-start(f32[48,512]{1,0:T(8,128)S(1)} %inverse_rows.1), channel_id=1, source_target_pairs={{0,0},{1,8},{2,16},{3,24},{4,32},{5,40},{6,48},{7,56},{8,64},{9,72... | collective-permute-start | bytes 294920 | tf_op jit(solution)/shard_map/ppermute | solution.py:398
  114.6 17.7 %all-to-all-start.2 = ((f32[16,24,256]{2,1,0:T(8,128)}), f32[16,24,256]{2,1,0:T(8,128)S(1)}, u32[]{:S(2)}, u32[]{:S(2)}) async-start(f32[16,24,256]{2,1,0:T(8,128)} %broadcast_in_dim.8), calls=%async_computation.2 | async-start | bytes 786432 | tf_op jit(solution)/shard_map/all_to_all | solution.py:228
  132.2 10.1 %collective-permute-start.27 = (f32[384,256]{1,0:T(8,128)S(1)}, f32[384,256]{1,0:T(8,128)S(1)}, u32[]{:S(2)}, u32[]{:S(2)}) collective-permute-start(f32[384,256]{1,0:T(8,128)S(1)} %bitcast.34), channel_id=1, source_target_pairs={{0,1},{1,0},{2,3},{3,2},{4,5},{5,4},{6,7},{7,6},{8,9},{9,8},{10,11... | collective-permute-start | bytes 1179656 | tf_op jit(solution)/shard_map/ppermute | solution.py:404
  135.9 4.1 %collective-permute-start.28 = (f32[2,2,8,256]{3,2,1,0:T(8,128)S(1)}, f32[2,2,8,256]{3,2,1,0:T(8,128)S(1)}, u32[]{:S(2)}, u32[]{:S(2)}) collective-permute-start(f32[2,2,8,256]{3,2,1,0:T(8,128)S(1)} %get-tuple-element.59), channel_id=1, source_target_pairs={{0,2},{1,3},{2,4},{3,5},{4,6},{5,7},{6,0},{7,1},{8,10},{9,11},{10,... | collective-permute-start | bytes 98312 | tf_op jit(solution)/shard_map/ppermute | solution.py:310
  136.2 4.4 %collective-permute-start.29 = (f32[2,2,8,256]{3,2,1,0:T(8,128)S(1)}, f32[2,2,8,256]{3,2,1,0:T(8,128)S(1)}, u32[]{:S(2)}, u32[]{:S(2)}) collective-permute-start(f32[2,2,8,256]{3,2,1,0:T(8,128)S(1)} %get-tuple-element.60), channel_id=1, source_target_pairs={{0,4},{1,5},{2,6},{3,7},{4,0},{5,1},{6,2},{7,3},{8,12},{9,13},{10,... | collective-permute-start | bytes 98312 | tf_op jit(solution)/shard_map/ppermute | solution.py:310
  137.4 3.7 %collective-permute-start.30 = (f32[2,2,8,256]{3,2,1,0:T(8,128)S(1)}, f32[2,2,8,256]{3,2,1,0:T(8,128)S(1)}, u32[]{:S(2)}, u32[]{:S(2)}) collective-permute-start(f32[2,2,8,256]{3,2,1,0:T(8,128)S(1)} %get-tuple-element.57), channel_id=1, source_target_pairs={{0,6},{1,7},{2,0},{3,1},{4,2},{5,3},{6,4},{7,5},{8,14},{9,15},{10,... | collective-permute-start | bytes 98312 | tf_op jit(solution)/shard_map/ppermute | solution.py:310
  (7 other events, 328.3 us)

commit v6 on v5

--- a/solution.py
+++ b/solution.py
@@ -135,14 +135,14 @@
 
 
 RING = (0, -1, 1, -2, 2, -3, 3)
-BATCHES = ((0, -1, 1, -2, 2), (-3, 3), (4,))
+BATCHES = ((0, -1, 1, -2, 2), (-3, 3, 4))
 
 
 def product_kernel(place, a_ref, *refs):
     ring, (last_own, last_far) = refs[:7], refs[7:9]
-    above, below = refs[9:12], refs[12:15]
-    r0_ref, r1_ref, r2_ref, r3_ref = refs[15:19]
-    w_keep, w_send, y_keep, y_send, xh, xl, rh, rl, w_all, y_all = refs[19:]
+    above, below = refs[9:11], refs[11:13]
+    r0_ref, r1_ref, r2_ref, r3_ref = refs[13:17]
+    w_keep, w_send, y_keep, y_send, xh, xl, rh, rl, w_all, y_all = refs[17:]
     y, column, k, z = place[0], place[1], place[2], place[3]
 
     def put(step, offset, values):
@@ -196,7 +196,7 @@
     wide = 2 * WIDTH
     return pl.pallas_call(
         product_kernel,
-        in_specs=[SMEM] + [VMEM] * 20,
+        in_specs=[SMEM] + [VMEM] * 18,
         out_specs=[VMEM] * 4,
         out_shape=[
             jax.ShapeDtypeStruct((half, WIDTH), f32),
@@ -302,13 +302,13 @@
     )(place, *parts)
 
 
-def deliver(place, keep, arrived):
+def sent_over_x(keep, arrived):
     shape = (N_X, CAP, TILE_ROWS, WIDTH)
     pairs = jnp.stack([keep.reshape(shape), arrived.reshape(shape)], axis=1)
     parts = [pairs[0]]
     for step in range(1, N_X):
         parts.append(lax.ppermute(pairs[step], ROW_COL, along_x(step)))
-    return fill_slots(place, parts)
+    return parts
 
 
 def final_kernel(place, half, other, square_one, square_two, above, diag_one, cross_two, diag_two, w):
@@ -320,10 +320,11 @@
     w_cross = w[WIDTH : 2 * WIDTH]
     rows_dims = ((0,), (0,))
     one = square_one[...] + w[:WIDTH]
-    cross = w_cross - dot(one, above[...])
+    over = split(above[...])
+    cross = w_cross - three_pass(split(one), over, ((1,), (0,)))
     diag_one[...] = one
     cross_two[...] = cross
-    twice = dot(w_cross, above[...], rows_dims) + dot(above[...], cross, rows_dims)
+    twice = three_pass(split(w_cross), over, rows_dims) + three_pass(over, split(cross), rows_dims)
     diag_two[...] = square_two[...] + w[2 * WIDTH :] - twice
 
 
@@ -373,8 +374,7 @@
     last_far = lax.ppermute(down[ROWS:], ROW_COL, along_z(-1))
     batches = (
         jnp.concatenate([part[:ROWS] for part in ring[:5]], axis=0),
-        jnp.concatenate([part[:ROWS] for part in ring[5:]], axis=0),
-        last_own,
+        jnp.concatenate([part[:ROWS] for part in ring[5:]] + [last_own], axis=0),
     )
     above = [lax.ppermute(batch, ROW_COL, along_y(-1)) for batch in batches]
     below = [lax.ppermute(batch, ROW_COL, along_y(1)) for batch in batches]
@@ -402,12 +402,14 @@
     arrived = lax.ppermute(send, ROW_COL, other_core())
     w_half, arrived = lax.optimization_barrier((w_half, arrived))
     w_other = lax.ppermute(w_half, ROW_COL, other_core())
-    delivered = deliver(place, keep, arrived)
+    parts = sent_over_x(keep, arrived)
     square_one = dot(lower_one, lower_one, ((0,), (0,)))
     square_two = dot(lower_two, lower_two, ((0,), (0,)))
     diag_one, cross_two, diag_two = final_blocks(
         place, w_half, w_other, square_one, square_two, panel_above
     )
+    parts, diag_two = lax.optimization_barrier((parts, diag_two))
+    delivered = fill_slots(place, parts)
     return (inverse_one, diag_one, cross_two, diag_two, delivered)
 
 

time: 145 us -> 136 us (0.938)
  waiting for transfers between devices: 49.2 us -> 41.7 us
  starting transfers between devices: 80.4 us -> 78.7 us
    ppermute x3, waiting for transfers between devices: 7 us -> 0.01 us  [local(): down = lax.ppermute(down, ROW_COL, along_z(-1))]
    ppermute x1, waiting for transfers between devices: 0.01 us -> 3.5 us  [local(): last_far = lax.ppermute(down[ROWS:], ROW_COL, along_z(-1))]
    ppermute x1, starting transfers between devices: 9.63 us -> 7.15 us  [local(): w_own = w_keep + lax.ppermute(w_send, ROW_COL, other_core())]
    all_to_all x2, starting transfers between devices: 15.7 us -> 13.3 us  [copies_of(): return lax.all_to_all(copies, axis, 0, 0, tiled=True)]
    ppermute x1, starting transfers between devices: 0.11 us -> 2.11 us  [local(): last_own = lax.ppermute(up[:ROWS], ROW_COL, along_z(1))]
    all_to_all x1, starting transfers between devices: 3.55 us -> 5.49 us  [at_owner(): return lax.all_to_all(parts, axis, 0, 0, tiled=True)]
    ppermute x3 -> x2, waiting for transfers between devices: 4.8 us -> 2.98 us  [local(): below = [lax.ppermute(batch, ROW_COL, along_y(1)) for batch in batches]]
    ppermute x3, waiting for transfers between devices: 1.6 us -> 0.01 us  [sent_over_x(): parts.append(lax.ppermute(pairs[step], ROW_COL, along_x(step)))]
  transfers between devices with their start and end apart: 34 -> 32, of which waited for: 19 -> 16; matrix products, arithmetic and copies ran while one was open for 1% -> 1% of each run, Pallas kernels for 2% -> 2%
where the time goes in v6:
time: 136 us; the launch traced here: 135 us
  starting transfers between devices  78.7 us (58%)
  waiting for transfers between devices  41.7 us (31%)
  Pallas kernels  10 us (7%)
  local copies, waits for them, and re-layouts  1.6 us (1%)
    all_to_all x2, starting transfers between devices, copies_of(): return lax.all_to_all(copies, axis, 0, 0, tiled=True)  13.3 us
    ppermute x3, starting transfers between devices, local(): up = lax.ppermute(up, ROW_COL, along_z(1))  7.25 us
    ppermute x1, starting transfers between devices, local(): w_own = w_keep + lax.ppermute(w_send, ROW_COL, other_core())  7.15 us
    ppermute x1, starting transfers between devices, local(): far_block = lax.ppermute(panels, ROW_COL, to_column(2))  6.87 us
    ppermute x1, waiting for transfers between devices, local(): inverses = lax.ppermute(inverses, ROW_COL, moves(result_place))  6.82 us
    ppermute x3, starting transfers between devices, local(): row_panels.append(lax.ppermute(pair, ROW_COL, along_x(step)))  6.38 us
    ppermute x1, waiting for transfers between devices, local(): far_block = lax.ppermute(panels, ROW_COL, to_column(2))  5.89 us
    all_to_all x1, starting transfers between devices, at_owner(): return lax.all_to_all(parts, axis, 0, 0, tiled=True)  5.49 us
  transfers between devices with their start and end apart: 32, of which 16 were waited for; matrix products, arithmetic and copies ran while one was open for 1% of the time, Pallas kernels for 2%

profile of v6, /device:TPU:1, one launch (start us, length us, event | category | flops | bytes accessed | tf_op | source)
XLA Modules:
  0.0 135.2 jit_solution(7930109939955071305)
XLA Ops:
  0.7 1.4 %masked_panels.1 = (f32[48,512]{1,0:T(8,128)S(1)}, f32[48,512]{1,0:T(8,128)S(1)}) custom-call(s32[1]{0:T(128)} %bitcast.5.start, s32[84,128]{1,0:T(8,128)} %bitcast.41, s32[72,128]{1,0:T(8,128)} %bitcast.42, f32[48,256]{1,0:T(8,128)} %panel_one_hbm.1, f32[48,256]{1,0:T(8,128)} %panel_two_hbm.1), custom_call_target="tpu_custom_call" | custom-call | tf_op jit(solution)/shard_map/masked_panels/pallas_call | solution.py:100
  2.1 4.9 %collective-permute-start = (f32[48,512]{1,0:T(8,128)S(1)}, f32[48,512]{1,0:T(8,128)S(1)}, u32[]{:S(2)}, u32[]{:S(2)}) collective-permute-start(f32[48,512]{1,0:T(8,128)S(1)} %get-tuple-element.33), channel_id=1, source_target_pairs={{0,0},{1,8},{2,64},{3,72},{4,128},{5,136},{6,192},{7,200},{8,16},{... | collective-permute-start | bytes 294920 | tf_op jit(solution)/shard_map/ppermute | solution.py:361
  7.0 6.9 %collective-permute-start.1 = (f32[48,512]{1,0:T(8,128)S(1)}, f32[48,512]{1,0:T(8,128)S(1)}, u32[]{:S(2)}, u32[]{:S(2)}) collective-permute-start(f32[48,512]{1,0:T(8,128)S(1)} %get-tuple-element.33), channel_id=1, source_target_pairs={{0,128},{1,136},{2,192},{3,200},{4,0},{5,8},{6,64},{7,72},{8,144},... | collective-permute-start | bytes 294920 | tf_op jit(solution)/shard_map/ppermute | solution.py:362
  14.6 5.9 %collective-permute-done.1 = f32[48,512]{1,0:T(8,128)S(1)} collective-permute-done((f32[48,512]{1,0:T(8,128)S(1)}, f32[48,512]{1,0:T(8,128)S(1)}, u32[]{:S(2)}, u32[]{:S(2)}) %collective-permute-start.1) | collective-permute-done | bytes 98336 | tf_op jit(solution)/shard_map/ppermute | solution.py:362
  20.5 1.8 %collective-permute-start.3 = (f32[96,512]{1,0:T(8,128)S(1)}, f32[96,512]{1,0:T(8,128)S(1)}, u32[]{:S(2)}, u32[]{:S(2)}) collective-permute-start(f32[96,512]{1,0:T(8,128)S(1)} %constant_dynamic-update-slice_fusion.refs_0_), channel_id=1, source_target_pairs={{0,8},{1,9},{2,10},{3,11},{4,12},{5,13},{6,14},{7,15},{8,16},{9,17... | collective-permute-start | bytes 589832 | tf_op jit(solution)/shard_map/ppermute | solution.py:370
  23.4 3.6 %collective-permute-start.16 = (f32[2,48,512]{2,1,0:T(8,128)S(1)}, f32[2,48,512]{2,1,0:T(8,128)S(1)}, u32[]{:S(2)}, u32[]{:S(2)}) collective-permute-start(f32[2,48,512]{2,1,0:T(8,128)S(1)} %pad_maximum_fusion.1.refs_13_), channel_id=1, source_target_pairs={{0,4},{1,5},{2,6},{3,7},{4,0},{5,1},{6,2},{7,3},{8,12},{9,13},{10,... | collective-permute-start | bytes 589832 | tf_op jit(solution)/shard_map/ppermute | solution.py:383
  27.0 3.2 %collective-permute-start.5 = (f32[96,512]{1,0:T(8,128)S(1)}, f32[96,512]{1,0:T(8,128)S(1)}, u32[]{:S(2)}, u32[]{:S(2)}) collective-permute-start(f32[96,512]{1,0:T(8,128)S(1)} %collective-permute-done.3.refs_1_), channel_id=1, source_target_pairs={{0,8},{1,9},{2,10},{3,11},{4,12},{5,13},{6,14},{7,15},{8,16},{9,17... | collective-permute-start | bytes 589832 | tf_op jit(solution)/shard_map/ppermute | solution.py:370
  30.2 3.6 %collective-permute-done.5.refs_3_ = f32[96,512]{1,0:T(8,128)S(1)} collective-permute-done((f32[96,512]{1,0:T(8,128)S(1)}, f32[96,512]{1,0:T(8,128)S(1)}, u32[]{:S(2)}, u32[]{:S(2)}) %collective-permute-start.5) | collective-permute-done | bytes 196640 | tf_op jit(solution)/shard_map/ppermute | solution.py:370
  33.8 2.2 %collective-permute-start.7 = (f32[96,512]{1,0:T(8,128)S(1)}, f32[96,512]{1,0:T(8,128)S(1)}, u32[]{:S(2)}, u32[]{:S(2)}) collective-permute-start(f32[96,512]{1,0:T(8,128)S(1)} %collective-permute-done.5.refs_3_), channel_id=1, source_target_pairs={{0,8},{1,9},{2,10},{3,11},{4,12},{5,13},{6,14},{7,15},{8,16},{9,17... | collective-permute-start | bytes 589832 | tf_op jit(solution)/shard_map/ppermute | solution.py:370
  36.6 2.3 %collective-permute-start.11 = (f32[240,512]{1,0:T(8,128)S(1)}, f32[240,512]{1,0:T(8,128)S(1)}, u32[]{:S(2)}, u32[]{:S(2)}) collective-permute-start(f32[240,512]{1,0:T(8,128)S(1)} %slice_dynamic-update-slice_fusion), channel_id=1, source_target_pairs={{0,192},{1,193},{2,194},{3,195},{4,196},{5,197},{6,198},{7,199},{8... | collective-permute-start | bytes 1474568 | tf_op jit(solution)/shard_map/ppermute | solution.py:379
  40.1 1.5 %collective-permute-start.13 = (f32[240,512]{1,0:T(8,128)S(1)}, f32[240,512]{1,0:T(8,128)S(1)}, u32[]{:S(2)}, u32[]{:S(2)}) collective-permute-start(f32[240,512]{1,0:T(8,128)S(1)} %slice_dynamic-update-slice_fusion), channel_id=1, source_target_pairs={{0,64},{1,65},{2,66},{3,67},{4,68},{5,69},{6,70},{7,71},{8,72},{9,... | collective-permute-start | bytes 1474568 | tf_op jit(solution)/shard_map/ppermute | solution.py:380
  41.6 2.1 %collective-permute-start.9 = (f32[48,512]{1,0:T(8,128)S(1)}, f32[48,512]{1,0:T(8,128)S(1)}, u32[]{:S(2)}, u32[]{:S(2)}) collective-permute-start(f32[48,512]{1,0:T(8,128)S(1)} %slice.61), channel_id=1, source_target_pairs={{0,8},{1,9},{2,10},{3,11},{4,12},{5,13},{6,14},{7,15},{8,16},{9,17... | collective-permute-start | bytes 294920 | tf_op jit(solution)/shard_map/ppermute | solution.py:373
  43.8 2.7 %collective-permute-done.9.refs_7_ = f32[48,512]{1,0:T(8,128)S(1)} collective-permute-done((f32[48,512]{1,0:T(8,128)S(1)}, f32[48,512]{1,0:T(8,128)S(1)}, u32[]{:S(2)}, u32[]{:S(2)}) %collective-permute-start.9) | collective-permute-done | bytes 98336 | tf_op jit(solution)/shard_map/ppermute | solution.py:373
  46.4 2.7 %collective-permute-start.17 = (f32[2,48,512]{2,1,0:T(8,128)S(1)}, f32[2,48,512]{2,1,0:T(8,128)S(1)}, u32[]{:S(2)}, u32[]{:S(2)}) collective-permute-start(f32[2,48,512]{2,1,0:T(8,128)S(1)} %pad_maximum_fusion.1.refs_13_), channel_id=1, source_target_pairs={{0,6},{1,7},{2,0},{3,1},{4,2},{5,3},{6,4},{7,5},{8,14},{9,15},{10,... | collective-permute-start | bytes 589832 | tf_op jit(solution)/shard_map/ppermute | solution.py:383
  52.0 3.5 %collective-permute-done.10.refs_8_ = f32[48,512]{1,0:T(8,128)S(1)} collective-permute-done((f32[48,512]{1,0:T(8,128)S(1)}, f32[48,512]{1,0:T(8,128)S(1)}, u32[]{:S(2)}, u32[]{:S(2)}) %collective-permute-start.10) | collective-permute-done | bytes 98336 | tf_op jit(solution)/shard_map/ppermute | solution.py:374
  55.6 3.0 %collective-permute-done.14.refs_12_ = f32[144,512]{1,0:T(8,128)S(1)} collective-permute-done((f32[144,512]{1,0:T(8,128)S(1)}, f32[144,512]{1,0:T(8,128)S(1)}, u32[]{:S(2)}, u32[]{:S(2)}) %collective-permute-start.14) | collective-permute-done | bytes 294944 | tf_op jit(solution)/shard_map/ppermute | solution.py:380
  58.6 3.9 %product_and_grams.1 = (f32[384,256]{1,0:T(8,128)S(1)}, f32[384,256]{1,0:T(8,128)S(1)}, f32[4,48,512]{2,1,0:T(8,128)S(1)}, f32[4,48,512]{2,1,0:T(8,128)S(1)}) custom-call(s32[4]{0:T(128)S(1)} %pad_add_fusion.place, f32[384,1536]{1,0:T(8,128)S(1)} %copy-done.1, f32[96,512]{1,0:T(8,128)S(1)} %constant_dynamic-update-slice_fusion.refs_0_, ...), custom_call_target="tpu_custom_call" | custom-call | tf_op jit(solution)/shard_map/product_and_grams/pallas_call | solution.py:197
  62.5 7.1 %collective-permute-start.18 = (f32[384,256]{1,0:T(8,128)S(1)}, f32[384,256]{1,0:T(8,128)S(1)}, u32[]{:S(2)}, u32[]{:S(2)}) collective-permute-start(f32[384,256]{1,0:T(8,128)S(1)} %get-tuple-element.39), channel_id=1, source_target_pairs={{0,1},{1,0},{2,3},{3,2},{4,5},{5,4},{6,7},{7,6},{8,9},{9,8},{10,11... | collective-permute-start | bytes 1179656 | tf_op jit(solution)/shard_map/ppermute | solution.py:389
  69.7 1.3 collective-permute-done.18
  72.2 5.5 %all-to-all-start = ((f32[16,24,256]{2,1,0:T(8,128)}), f32[16,24,256]{2,1,0:T(8,128)S(1)}, u32[]{:S(2)}, u32[]{:S(2)}) async-start(f32[16,24,256]{2,1,0:T(8,128)} %bitcast.10), calls=%async_computation | async-start | bytes 786432 | tf_op jit(solution)/shard_map/all_to_all | solution.py:223
  77.8 1.4 %collective-permute-start.20 = (f32[48,512]{1,0:T(8,128)S(1)}, f32[48,512]{1,0:T(8,128)S(1)}, u32[]{:S(2)}, u32[]{:S(2)}) collective-permute-start(f32[48,512]{1,0:T(8,128)S(1)} %get-tuple-element.63), channel_id=1, source_target_pairs={{0,2},{1,3},{2,4},{3,5},{4,6},{5,7},{6,0},{7,1},{8,10},{9,11},{10,... | collective-permute-start | bytes 294920 | tf_op jit(solution)/shard_map/ppermute | solution.py:394
  79.3 2.4 %collective-permute-start.21 = (f32[48,512]{1,0:T(8,128)S(1)}, f32[48,512]{1,0:T(8,128)S(1)}, u32[]{:S(2)}, u32[]{:S(2)}) collective-permute-start(f32[48,512]{1,0:T(8,128)S(1)} %get-tuple-element.62), channel_id=1, source_target_pairs={{0,4},{1,5},{2,6},{3,7},{4,0},{5,1},{6,2},{7,3},{8,12},{9,13},{10,... | collective-permute-start | bytes 294920 | tf_op jit(solution)/shard_map/ppermute | solution.py:394
  82.8 4.3 %all-to-all-done = f32[16,24,256]{2,1,0:T(8,128)S(1)} async-done(((f32[16,24,256]{2,1,0:T(8,128)}), f32[16,24,256]{2,1,0:T(8,128)S(1)}, u32[]{:S(2)}, u32[]{:S(2)}) %all-to-all-start) | async-done | bytes 393248 | tf_op jit(solution)/shard_map/all_to_all | solution.py:223
  87.9 1.7 %collective-permute-done.21.y2 = f32[48,512]{1,0:T(8,128)S(1)} collective-permute-done((f32[48,512]{1,0:T(8,128)S(1)}, f32[48,512]{1,0:T(8,128)S(1)}, u32[]{:S(2)}, u32[]{:S(2)}) %collective-permute-start.21) | collective-permute-done | bytes 98336 | tf_op jit(solution)/shard_map/ppermute | solution.py:394
  90.5 4.0 %all-to-all-start.1 = ((f32[8,24,256]{2,1,0:T(8,128)}), f32[8,24,256]{2,1,0:T(8,128)S(1)}, u32[]{:S(2)}, u32[]{:S(2)}) async-start(f32[8,24,256]{2,1,0:T(8,128)} %broadcast_in_dim.7), calls=%async_computation.1 | async-start | bytes 393216 | tf_op jit(solution)/shard_map/all_to_all | solution.py:228
  94.5 5.1 %collective-permute-start.23 = (f32[48,512]{1,0:T(8,128)S(1)}, f32[48,512]{1,0:T(8,128)S(1)}, u32[]{:S(2)}, u32[]{:S(2)}) collective-permute-start(f32[48,512]{1,0:T(8,128)S(1)} %inverse_rows.1), channel_id=1, source_target_pairs={{0,0},{1,8},{2,16},{3,24},{4,32},{5,40},{6,48},{7,56},{8,64},{9,72... | collective-permute-start | bytes 294920 | tf_op jit(solution)/shard_map/ppermute | solution.py:398
  99.6 6.8 %collective-permute-done.23.rows = f32[48,512]{1,0:T(8,128)S(1)} collective-permute-done((f32[48,512]{1,0:T(8,128)S(1)}, f32[48,512]{1,0:T(8,128)S(1)}, u32[]{:S(2)}, u32[]{:S(2)}) %collective-permute-start.23) | collective-permute-done | bytes 98336 | tf_op jit(solution)/shard_map/ppermute | solution.py:398
  107.2 9.3 %all-to-all-start.2 = ((f32[16,24,256]{2,1,0:T(8,128)}), f32[16,24,256]{2,1,0:T(8,128)S(1)}, u32[]{:S(2)}, u32[]{:S(2)}) async-start(f32[16,24,256]{2,1,0:T(8,128)} %broadcast_in_dim.8), calls=%async_computation.2 | async-start | bytes 786432 | tf_op jit(solution)/shard_map/all_to_all | solution.py:228
  117.8 1.9 %collective-permute-start.24 = (f32[8,8,256]{2,1,0:T(8,128)S(1)}, f32[8,8,256]{2,1,0:T(8,128)S(1)}, u32[]{:S(2)}, u32[]{:S(2)}) collective-permute-start(f32[8,8,256]{2,1,0:T(8,128)S(1)} %get-tuple-element.49), channel_id=1, source_target_pairs={{0,1},{1,0},{2,3},{3,2},{4,5},{5,4},{6,7},{7,6},{8,9},{9,8},{10,11... | collective-permute-start | bytes 196616 | tf_op jit(solution)/shard_map/ppermute | solution.py:402
  120.7 4.2 %all-to-all-done.2 = f32[16,24,256]{2,1,0:T(8,128)S(1)} async-done(((f32[16,24,256]{2,1,0:T(8,128)}), f32[16,24,256]{2,1,0:T(8,128)S(1)}, u32[]{:S(2)}, u32[]{:S(2)}) %all-to-all-start.2) | async-done | bytes 393248 | tf_op jit(solution)/shard_map/all_to_all | solution.py:228
  124.9 3.0 %collective-permute-start.25 = (f32[384,256]{1,0:T(8,128)S(1)}, f32[384,256]{1,0:T(8,128)S(1)}, u32[]{:S(2)}, u32[]{:S(2)}) collective-permute-start(f32[384,256]{1,0:T(8,128)S(1)} %bitcast.34), channel_id=1, source_target_pairs={{0,1},{1,0},{2,3},{3,2},{4,5},{5,4},{6,7},{7,6},{8,9},{9,8},{10,11... | collective-permute-start | bytes 1179656 | tf_op jit(solution)/shard_map/ppermute | solution.py:404
  131.9 2.0 %final_blocks.1 = (f32[256,256]{1,0:T(8,128)}, f32[256,256]{1,0:T(8,128)}, f32[256,256]{1,0:T(8,128)}) custom-call(s32[4]{0:T(128)S(1)} %pad_add_fusion.place, f32[384,256]{1,0:T(8,128)S(1)} %bitcast.35, f32[384,256]{1,0:T(8,128)S(1)} %collective-permute-done.25.other, f32[256,256]{1,0:T(8,128)S(1)} %fusion.8.square_one, f32[256,256]{1,0:T(8,128)S(1)} %fusion.9.square_two, ...), custom_call_target="tpu_custom_call" | custom-call | tf_op jit(solution)/shard_map/final_blocks/pallas_call | solution.py:333
  (69 shorter events, 18.9 us)
Async XLA Ops:
  2.1 12.5 %collective-permute-start = (f32[48,512]{1,0:T(8,128)S(1)}, f32[48,512]{1,0:T(8,128)S(1)}, u32[]{:S(2)}, u32[]{:S(2)}) collective-permute-start(f32[48,512]{1,0:T(8,128)S(1)} %get-tuple-element.33), channel_id=1, source_target_pairs={{0,0},{1,8},{2,64},{3,72},{4,128},{5,136},{6,192},{7,200},{8,16},{... | collective-permute-start | bytes 294920 | tf_op jit(solution)/shard_map/ppermute | solution.py:361
  7.0 13.4 %collective-permute-start.1 = (f32[48,512]{1,0:T(8,128)S(1)}, f32[48,512]{1,0:T(8,128)S(1)}, u32[]{:S(2)}, u32[]{:S(2)}) collective-permute-start(f32[48,512]{1,0:T(8,128)S(1)} %get-tuple-element.33), channel_id=1, source_target_pairs={{0,128},{1,136},{2,192},{3,200},{4,0},{5,8},{6,64},{7,72},{8,144},... | collective-permute-start | bytes 294920 | tf_op jit(solution)/shard_map/ppermute | solution.py:362
  13.9 6.6 %collective-permute-start.2 = (f32[48,512]{1,0:T(8,128)S(1)}, f32[48,512]{1,0:T(8,128)S(1)}, u32[]{:S(2)}, u32[]{:S(2)}) collective-permute-start(f32[48,512]{1,0:T(8,128)S(1)} %get-tuple-element.33), channel_id=1, source_target_pairs={{0,1},{1,0},{2,3},{3,2},{4,5},{5,4},{6,7},{7,6},{8,9},{9,8},{10,11... | collective-permute-start | bytes 294920 | tf_op jit(solution)/shard_map/ppermute | solution.py:363
  20.5 6.5 %collective-permute-start.3 = (f32[96,512]{1,0:T(8,128)S(1)}, f32[96,512]{1,0:T(8,128)S(1)}, u32[]{:S(2)}, u32[]{:S(2)}) collective-permute-start(f32[96,512]{1,0:T(8,128)S(1)} %constant_dynamic-update-slice_fusion.refs_0_), channel_id=1, source_target_pairs={{0,8},{1,9},{2,10},{3,11},{4,12},{5,13},{6,14},{7,15},{8,16},{9,17... | collective-permute-start | bytes 589832 | tf_op jit(solution)/shard_map/ppermute | solution.py:370
  22.3 7.9 %collective-permute-start.4 = (f32[96,512]{1,0:T(8,128)S(1)}, f32[96,512]{1,0:T(8,128)S(1)}, u32[]{:S(2)}, u32[]{:S(2)}) collective-permute-start(f32[96,512]{1,0:T(8,128)S(1)} %constant_dynamic-update-slice_fusion.refs_0_), channel_id=1, source_target_pairs={{0,56},{1,57},{2,58},{3,59},{4,60},{5,61},{6,62},{7,63},{8,0},{9,1... | collective-permute-start | bytes 589832 | tf_op jit(solution)/shard_map/ppermute | solution.py:371
  23.3 25.9 %collective-permute-start.15 = (f32[2,48,512]{2,1,0:T(8,128)S(1)}, f32[2,48,512]{2,1,0:T(8,128)S(1)}, u32[]{:S(2)}, u32[]{:S(2)}) collective-permute-start(f32[2,48,512]{2,1,0:T(8,128)S(1)} %pad_maximum_fusion.1.refs_13_), channel_id=1, source_target_pairs={{0,2},{1,3},{2,4},{3,5},{4,6},{5,7},{6,0},{7,1},{8,10},{9,11},{10,... | collective-permute-start | bytes 589832 | tf_op jit(solution)/shard_map/ppermute | solution.py:383
  23.4 26.8 %collective-permute-start.16 = (f32[2,48,512]{2,1,0:T(8,128)S(1)}, f32[2,48,512]{2,1,0:T(8,128)S(1)}, u32[]{:S(2)}, u32[]{:S(2)}) collective-permute-start(f32[2,48,512]{2,1,0:T(8,128)S(1)} %pad_maximum_fusion.1.refs_13_), channel_id=1, source_target_pairs={{0,4},{1,5},{2,6},{3,7},{4,0},{5,1},{6,2},{7,3},{8,12},{9,13},{10,... | collective-permute-start | bytes 589832 | tf_op jit(solution)/shard_map/ppermute | solution.py:383
  27.0 6.9 %collective-permute-start.5 = (f32[96,512]{1,0:T(8,128)S(1)}, f32[96,512]{1,0:T(8,128)S(1)}, u32[]{:S(2)}, u32[]{:S(2)}) collective-permute-start(f32[96,512]{1,0:T(8,128)S(1)} %collective-permute-done.3.refs_1_), channel_id=1, source_target_pairs={{0,8},{1,9},{2,10},{3,11},{4,12},{5,13},{6,14},{7,15},{8,16},{9,17... | collective-permute-start | bytes 589832 | tf_op jit(solution)/shard_map/ppermute | solution.py:370
  30.2 5.9 %collective-permute-start.6 = (f32[96,512]{1,0:T(8,128)S(1)}, f32[96,512]{1,0:T(8,128)S(1)}, u32[]{:S(2)}, u32[]{:S(2)}) collective-permute-start(f32[96,512]{1,0:T(8,128)S(1)} %collective-permute-done.4.refs_2_), channel_id=1, source_target_pairs={{0,56},{1,57},{2,58},{3,59},{4,60},{5,61},{6,62},{7,63},{8,0},{9,1... | collective-permute-start | bytes 589832 | tf_op jit(solution)/shard_map/ppermute | solution.py:371
  33.8 6.3 %collective-permute-start.7 = (f32[96,512]{1,0:T(8,128)S(1)}, f32[96,512]{1,0:T(8,128)S(1)}, u32[]{:S(2)}, u32[]{:S(2)}) collective-permute-start(f32[96,512]{1,0:T(8,128)S(1)} %collective-permute-done.5.refs_3_), channel_id=1, source_target_pairs={{0,8},{1,9},{2,10},{3,11},{4,12},{5,13},{6,14},{7,15},{8,16},{9,17... | collective-permute-start | bytes 589832 | tf_op jit(solution)/shard_map/ppermute | solution.py:370
  36.0 5.6 %collective-permute-start.8 = (f32[96,512]{1,0:T(8,128)S(1)}, f32[96,512]{1,0:T(8,128)S(1)}, u32[]{:S(2)}, u32[]{:S(2)}) collective-permute-start(f32[96,512]{1,0:T(8,128)S(1)} %collective-permute-done.6.refs_4_), channel_id=1, source_target_pairs={{0,56},{1,57},{2,58},{3,59},{4,60},{5,61},{6,62},{7,63},{8,0},{9,1... | collective-permute-start | bytes 589832 | tf_op jit(solution)/shard_map/ppermute | solution.py:371
  36.6 19.0 %collective-permute-start.11 = (f32[240,512]{1,0:T(8,128)S(1)}, f32[240,512]{1,0:T(8,128)S(1)}, u32[]{:S(2)}, u32[]{:S(2)}) collective-permute-start(f32[240,512]{1,0:T(8,128)S(1)} %slice_dynamic-update-slice_fusion), channel_id=1, source_target_pairs={{0,192},{1,193},{2,194},{3,195},{4,196},{5,197},{6,198},{7,199},{8... | collective-permute-start | bytes 1474568 | tf_op jit(solution)/shard_map/ppermute | solution.py:379
  40.1 15.4 %collective-permute-start.13 = (f32[240,512]{1,0:T(8,128)S(1)}, f32[240,512]{1,0:T(8,128)S(1)}, u32[]{:S(2)}, u32[]{:S(2)}) collective-permute-start(f32[240,512]{1,0:T(8,128)S(1)} %slice_dynamic-update-slice_fusion), channel_id=1, source_target_pairs={{0,64},{1,65},{2,66},{3,67},{4,68},{5,69},{6,70},{7,71},{8,72},{9,... | collective-permute-start | bytes 1474568 | tf_op jit(solution)/shard_map/ppermute | solution.py:380
  41.6 4.8 %collective-permute-start.9 = (f32[48,512]{1,0:T(8,128)S(1)}, f32[48,512]{1,0:T(8,128)S(1)}, u32[]{:S(2)}, u32[]{:S(2)}) collective-permute-start(f32[48,512]{1,0:T(8,128)S(1)} %slice.61), channel_id=1, source_target_pairs={{0,8},{1,9},{2,10},{3,11},{4,12},{5,13},{6,14},{7,15},{8,16},{9,17... | collective-permute-start | bytes 294920 | tf_op jit(solution)/shard_map/ppermute | solution.py:373
  46.4 5.3 %collective-permute-start.17 = (f32[2,48,512]{2,1,0:T(8,128)S(1)}, f32[2,48,512]{2,1,0:T(8,128)S(1)}, u32[]{:S(2)}, u32[]{:S(2)}) collective-permute-start(f32[2,48,512]{2,1,0:T(8,128)S(1)} %pad_maximum_fusion.1.refs_13_), channel_id=1, source_target_pairs={{0,6},{1,7},{2,0},{3,1},{4,2},{5,3},{6,4},{7,5},{8,14},{9,15},{10,... | collective-permute-start | bytes 589832 | tf_op jit(solution)/shard_map/ppermute | solution.py:383
  49.2 6.4 %collective-permute-start.12 = (f32[144,512]{1,0:T(8,128)S(1)}, f32[144,512]{1,0:T(8,128)S(1)}, u32[]{:S(2)}, u32[]{:S(2)}) collective-permute-start(f32[144,512]{1,0:T(8,128)S(1)} %pad_maximum_fusion), channel_id=1, source_target_pairs={{0,192},{1,193},{2,194},{3,195},{4,196},{5,197},{6,198},{7,199},{8... | collective-permute-start | bytes 884744 | tf_op jit(solution)/shard_map/ppermute | solution.py:379
  50.2 8.4 %collective-permute-start.14 = (f32[144,512]{1,0:T(8,128)S(1)}, f32[144,512]{1,0:T(8,128)S(1)}, u32[]{:S(2)}, u32[]{:S(2)}) collective-permute-start(f32[144,512]{1,0:T(8,128)S(1)} %pad_maximum_fusion), channel_id=1, source_target_pairs={{0,64},{1,65},{2,66},{3,67},{4,68},{5,69},{6,70},{7,71},{8,72},{9,... | collective-permute-start | bytes 884744 | tf_op jit(solution)/shard_map/ppermute | solution.py:380
  51.7 3.8 %collective-permute-start.10 = (f32[48,512]{1,0:T(8,128)S(1)}, f32[48,512]{1,0:T(8,128)S(1)}, u32[]{:S(2)}, u32[]{:S(2)}) collective-permute-start(f32[48,512]{1,0:T(8,128)S(1)} %get-tuple-element.66), channel_id=1, source_target_pairs={{0,56},{1,57},{2,58},{3,59},{4,60},{5,61},{6,62},{7,63},{8,0},{9,1... | collective-permute-start | bytes 294920 | tf_op jit(solution)/shard_map/ppermute | solution.py:374
  62.5 8.5 %collective-permute-start.18 = (f32[384,256]{1,0:T(8,128)S(1)}, f32[384,256]{1,0:T(8,128)S(1)}, u32[]{:S(2)}, u32[]{:S(2)}) collective-permute-start(f32[384,256]{1,0:T(8,128)S(1)} %get-tuple-element.39), channel_id=1, source_target_pairs={{0,1},{1,0},{2,3},{3,2},{4,5},{5,4},{6,7},{7,6},{8,9},{9,8},{10,11... | collective-permute-start | bytes 1179656 | tf_op jit(solution)/shard_map/ppermute | solution.py:389
  71.8 5.9 %collective-permute-start.19 = (f32[4,48,512]{2,1,0:T(8,128)S(1)}, f32[4,48,512]{2,1,0:T(8,128)S(1)}, u32[]{:S(2)}, u32[]{:S(2)}) collective-permute-start(f32[4,48,512]{2,1,0:T(8,128)S(1)} %get-tuple-element.42), channel_id=1, source_target_pairs={{0,1},{1,0},{2,3},{3,2},{4,5},{5,4},{6,7},{7,6},{8,9},{9,8},{10,11... | collective-permute-start | bytes 1179656 | tf_op jit(solution)/shard_map/ppermute | solution.py:391
  72.2 15.0 %all-to-all-start = ((f32[16,24,256]{2,1,0:T(8,128)}), f32[16,24,256]{2,1,0:T(8,128)S(1)}, u32[]{:S(2)}, u32[]{:S(2)}) async-start(f32[16,24,256]{2,1,0:T(8,128)} %bitcast.10), calls=%async_computation | async-start | bytes 786432 | tf_op jit(solution)/shard_map/all_to_all | solution.py:223
  77.8 10.0 %collective-permute-start.20 = (f32[48,512]{1,0:T(8,128)S(1)}, f32[48,512]{1,0:T(8,128)S(1)}, u32[]{:S(2)}, u32[]{:S(2)}) collective-permute-start(f32[48,512]{1,0:T(8,128)S(1)} %get-tuple-element.63), channel_id=1, source_target_pairs={{0,2},{1,3},{2,4},{3,5},{4,6},{5,7},{6,0},{7,1},{8,10},{9,11},{10,... | collective-permute-start | bytes 294920 | tf_op jit(solution)/shard_map/ppermute | solution.py:394
  79.3 10.3 %collective-permute-start.21 = (f32[48,512]{1,0:T(8,128)S(1)}, f32[48,512]{1,0:T(8,128)S(1)}, u32[]{:S(2)}, u32[]{:S(2)}) collective-permute-start(f32[48,512]{1,0:T(8,128)S(1)} %get-tuple-element.62), channel_id=1, source_target_pairs={{0,4},{1,5},{2,6},{3,7},{4,0},{5,1},{6,2},{7,3},{8,12},{9,13},{10,... | collective-permute-start | bytes 294920 | tf_op jit(solution)/shard_map/ppermute | solution.py:394
  81.7 7.9 %collective-permute-start.22 = (f32[48,512]{1,0:T(8,128)S(1)}, f32[48,512]{1,0:T(8,128)S(1)}, u32[]{:S(2)}, u32[]{:S(2)}) collective-permute-start(f32[48,512]{1,0:T(8,128)S(1)} %get-tuple-element.61), channel_id=1, source_target_pairs={{0,6},{1,7},{2,0},{3,1},{4,2},{5,3},{6,4},{7,5},{8,14},{9,15},{10,... | collective-permute-start | bytes 294920 | tf_op jit(solution)/shard_map/ppermute | solution.py:394
  90.5 15.9 %all-to-all-start.1 = ((f32[8,24,256]{2,1,0:T(8,128)}), f32[8,24,256]{2,1,0:T(8,128)S(1)}, u32[]{:S(2)}, u32[]{:S(2)}) async-start(f32[8,24,256]{2,1,0:T(8,128)} %broadcast_in_dim.7), calls=%async_computation.1 | async-start | bytes 393216 | tf_op jit(solution)/shard_map/all_to_all | solution.py:228
  94.5 11.9 %collective-permute-start.23 = (f32[48,512]{1,0:T(8,128)S(1)}, f32[48,512]{1,0:T(8,128)S(1)}, u32[]{:S(2)}, u32[]{:S(2)}) collective-permute-start(f32[48,512]{1,0:T(8,128)S(1)} %inverse_rows.1), channel_id=1, source_target_pairs={{0,0},{1,8},{2,16},{3,24},{4,32},{5,40},{6,48},{7,56},{8,64},{9,72... | collective-permute-start | bytes 294920 | tf_op jit(solution)/shard_map/ppermute | solution.py:398
  107.2 17.6 %all-to-all-start.2 = ((f32[16,24,256]{2,1,0:T(8,128)}), f32[16,24,256]{2,1,0:T(8,128)S(1)}, u32[]{:S(2)}, u32[]{:S(2)}) async-start(f32[16,24,256]{2,1,0:T(8,128)} %broadcast_in_dim.8), calls=%async_computation.2 | async-start | bytes 786432 | tf_op jit(solution)/shard_map/all_to_all | solution.py:228
  117.8 2.8 %collective-permute-start.24 = (f32[8,8,256]{2,1,0:T(8,128)S(1)}, f32[8,8,256]{2,1,0:T(8,128)S(1)}, u32[]{:S(2)}, u32[]{:S(2)}) collective-permute-start(f32[8,8,256]{2,1,0:T(8,128)S(1)} %get-tuple-element.49), channel_id=1, source_target_pairs={{0,1},{1,0},{2,3},{3,2},{4,5},{5,4},{6,7},{7,6},{8,9},{9,8},{10,11... | collective-permute-start | bytes 196616 | tf_op jit(solution)/shard_map/ppermute | solution.py:402
  124.9 7.1 %collective-permute-start.25 = (f32[384,256]{1,0:T(8,128)S(1)}, f32[384,256]{1,0:T(8,128)S(1)}, u32[]{:S(2)}, u32[]{:S(2)}) collective-permute-start(f32[384,256]{1,0:T(8,128)S(1)} %bitcast.34), channel_id=1, source_target_pairs={{0,1},{1,0},{2,3},{3,2},{4,5},{5,4},{6,7},{7,6},{8,9},{9,8},{10,11... | collective-permute-start | bytes 1179656 | tf_op jit(solution)/shard_map/ppermute | solution.py:404
  128.5 5.5 %collective-permute-start.26 = (f32[2,2,8,256]{3,2,1,0:T(8,128)S(1)}, f32[2,2,8,256]{3,2,1,0:T(8,128)S(1)}, u32[]{:S(2)}, u32[]{:S(2)}) collective-permute-start(f32[2,2,8,256]{3,2,1,0:T(8,128)S(1)} %get-tuple-element.69), channel_id=1, source_target_pairs={{0,2},{1,3},{2,4},{3,5},{4,6},{5,7},{6,0},{7,1},{8,10},{9,11},{10,... | collective-permute-start | bytes 98312 | tf_op jit(solution)/shard_map/ppermute | solution.py:310
  128.8 5.1 %collective-permute-start.27 = (f32[2,2,8,256]{3,2,1,0:T(8,128)S(1)}, f32[2,2,8,256]{3,2,1,0:T(8,128)S(1)}, u32[]{:S(2)}, u32[]{:S(2)}) collective-permute-start(f32[2,2,8,256]{3,2,1,0:T(8,128)S(1)} %get-tuple-element.70), channel_id=1, source_target_pairs={{0,4},{1,5},{2,6},{3,7},{4,0},{5,1},{6,2},{7,3},{8,12},{9,13},{10,... | collective-permute-start | bytes 98312 | tf_op jit(solution)/shard_map/ppermute | solution.py:310
  130.0 3.9 %collective-permute-start.28 = (f32[2,2,8,256]{3,2,1,0:T(8,128)S(1)}, f32[2,2,8,256]{3,2,1,0:T(8,128)S(1)}, u32[]{:S(2)}, u32[]{:S(2)}) collective-permute-start(f32[2,2,8,256]{3,2,1,0:T(8,128)S(1)} %get-tuple-element.67), channel_id=1, source_target_pairs={{0,6},{1,7},{2,0},{3,1},{4,2},{5,3},{6,4},{7,5},{8,14},{9,15},{10,... | collective-permute-start | bytes 98312 | tf_op jit(solution)/shard_map/ppermute | solution.py:310
  (5 other events, 304.6 us)

commit v7 on v6

--- a/solution.py
+++ b/solution.py
@@ -17,6 +17,7 @@
 ROWS = 48
 WIDTH = 256
 TILES, TILE_ROWS = 6, 8
+WAIT = 100_000_000
 SMALL = pltpu.CompilerParams(vmem_limit_bytes=6 * 1024 * 1024)
 SMEM = pl.BlockSpec(memory_space=pltpu.SMEM)
 VMEM = pl.BlockSpec(memory_space=pltpu.VMEM)
@@ -37,7 +38,7 @@
 
 
 def to_column(step):
-    return moves(lambda y, z, x, k: ((x + step) % N_Y, 2 * (z % 4) + k, y, z // 4))
+    return moves(lambda y, z, x, k: ((x + step) % N_Y, 7 - z if k else z, y, z // 4))
 
 
 def result_place(y, z, x, k):
@@ -138,39 +139,61 @@
 BATCHES = ((0, -1, 1, -2, 2), (-3, 3, 4))
 
 
-def product_kernel(place, a_ref, *refs):
-    ring, (last_own, last_far) = refs[:7], refs[7:9]
-    above, below = refs[9:11], refs[11:13]
-    r0_ref, r1_ref, r2_ref, r3_ref = refs[13:17]
-    w_keep, w_send, y_keep, y_send, xh, xl, rh, rl, w_all, y_all = refs[17:]
-    y, column, k, z = place[0], place[1], place[2], place[3]
-
-    def put(step, offset, values):
-        x = lax.rem(y + step, N_X)
-        at = lax.rem(z + N_Z + offset, N_Z)
-        first = lax.div(at, 2) * 384 + x * 96 + lax.rem(at, 2) * ROWS
-        first = pl.multiple_of(first, 16)
-        high, low = split(values)
-        xh[pl.ds(first, ROWS), :] = high
-        xl[pl.ds(first, ROWS), :] = low
-
+def put_block(place, step, offset, values, high_ref, low_ref):
+    y, k, z = place[0], place[2], place[3]
+    x = lax.rem(y + step, N_X)
+    at = lax.rem(z + N_Z + offset, N_Z)
+    near = lax.div(at, 4) == k
+    line = lax.rem(jnp.where(near, at, N_Z - 1 - at), 4)
+    first = pl.multiple_of(line * 384 + x * 96 + jnp.where(near, 0, ROWS), 16)
+    high, low = split(values)
+    high_ref[pl.ds(first, ROWS), :] = high
+    low_ref[pl.ds(first, ROWS), :] = low
+
+
+def operands_kernel(place, a_ref, *refs):
+    ring, last_own, above, below, rows = refs[:7], refs[7], refs[8], refs[9], refs[10:12]
+    ah, al, xh, xl, rh, rl = refs[12:]
+    column, k = place[1], place[2]
+    ah[...], al[...] = split(a_ref[...])
     for offset, ref in zip(RING, ring):
-        put(0, offset, ref[:ROWS])
-        put(2, offset, ref[ROWS:])
-    put(0, 4, last_own[...])
-    put(2, 4, last_far[...])
-    for step, batches in ((1, above), (3, below)):
-        for offsets, ref in zip(BATCHES, batches):
-            for i, offset in enumerate(offsets):
-                put(step, offset, ref[i * ROWS : (i + 1) * ROWS])
-    for step, r_ref in enumerate((r0_ref, r1_ref, r2_ref, r3_ref)):
+        put_block(place, 0, offset, ref[:ROWS], xh, xl)
+        put_block(place, 2, offset, ref[ROWS:], xh, xl)
+    put_block(place, 0, 4, last_own[...], xh, xl)
+    for step, ref in ((1, above), (3, below)):
+        for i, offset in enumerate(BATCHES[0]):
+            put_block(place, step, offset, ref[i * ROWS : (i + 1) * ROWS], xh, xl)
+    for step in range(N_X):
         x = lax.rem(column + N_X - step, N_X)
-        for part, core in ((0, k), (1, 1 - k)):
-            high, low = split(r_ref[part])
+        for r_ref, core in zip(rows, (k, 1 - k)):
+            high, low = split(r_ref[step])
             at = pl.multiple_of((x * N_K + core) * ROWS, 16)
             rh[pl.ds(at, ROWS), :] = high
             rl[pl.ds(at, ROWS), :] = low
-    product = three_pass(split(a_ref[...]), (xh[...], xl[...]), ((1,), (0,)))
+
+
+def operands(place, ancestor, arrays):
+    shapes = [ancestor.shape] * 2 + [(1536, 2 * WIDTH)] * 2 + [(384, 2 * WIDTH)] * 2
+    return pl.pallas_call(
+        operands_kernel,
+        in_specs=[SMEM] + [VMEM] * 13,
+        out_specs=[VMEM] * 6,
+        out_shape=[jax.ShapeDtypeStruct(shape, jnp.bfloat16) for shape in shapes],
+        compiler_params=pltpu.CompilerParams(vmem_limit_bytes=16 * 1024 * 1024),
+        name="operands",
+    )(place, ancestor, *arrays)
+
+
+def product_kernel(
+    place, ah, al, rh, rl, last_far, above, below, xh_in, xl_in,
+    w_keep, w_send, y_keep, y_send, xh, xl, w_all, y_all,
+):
+    column, k = place[1], place[2]
+    put_block(place, 2, 4, last_far[...], xh, xl)
+    for step, ref in ((1, above), (3, below)):
+        for i, offset in enumerate(BATCHES[1]):
+            put_block(place, step, offset, ref[i * ROWS : (i + 1) * ROWS], xh, xl)
+    product = three_pass((ah[...], al[...]), (xh[...], xl[...]), ((1,), (0,)))
     for block in range(N_COL):
         y_all[block] = product[block * ROWS : (block + 1) * ROWS]
     high, low = split(product)
@@ -190,31 +213,32 @@
         y_send[step] = y_all[x * N_K + 1 - k]
 
 
-def product_and_grams(place, ancestor, gathered):
-    f32, bf16 = jnp.float32, jnp.bfloat16
+def product_and_grams(place, prepared, arrays):
+    f32 = jnp.float32
     half = 3 * WIDTH // 2
     wide = 2 * WIDTH
+    ah, al, xh, xl, rh, rl = prepared
+    blocks = jax.ShapeDtypeStruct(xh.shape, xh.dtype)
     return pl.pallas_call(
         product_kernel,
-        in_specs=[SMEM] + [VMEM] * 18,
-        out_specs=[VMEM] * 4,
+        in_specs=[SMEM] + [VMEM] * 9,
+        out_specs=[VMEM] * 6,
         out_shape=[
             jax.ShapeDtypeStruct((half, WIDTH), f32),
             jax.ShapeDtypeStruct((half, WIDTH), f32),
             jax.ShapeDtypeStruct((N_X, ROWS, wide), f32),
             jax.ShapeDtypeStruct((N_X, ROWS, wide), f32),
+            blocks,
+            blocks,
         ],
+        input_output_aliases={8: 4, 9: 5},
         scratch_shapes=[
-            pltpu.VMEM((1536, wide), bf16),
-            pltpu.VMEM((1536, wide), bf16),
-            pltpu.VMEM((384, wide), bf16),
-            pltpu.VMEM((384, wide), bf16),
             pltpu.VMEM((3 * WIDTH, WIDTH), f32),
             pltpu.VMEM((N_COL, ROWS, wide), f32),
         ],
         compiler_params=pltpu.CompilerParams(vmem_limit_bytes=24 * 1024 * 1024),
         name="product_and_grams",
-    )(place, ancestor, *gathered)
+    )(place, ah, al, rh, rl, *arrays, xh, xl)[:4]
 
 
 def at_owner(value, axis):
@@ -244,6 +268,24 @@
         compiler_params=SMALL,
         name="inverse_rows",
     )(*parts, masks, panel_above)
+
+
+def square_kernel(lower_one, lower_two, square_one, square_two):
+    for lower, square in ((lower_one, square_one), (lower_two, square_two)):
+        square[...] = dot(lower[...], lower[...], ((0,), (0,)))
+
+
+def square_blocks(lower_one, lower_two):
+    block = jax.ShapeDtypeStruct((WIDTH, WIDTH), jnp.float32)
+    return pl.pallas_call(
+        square_kernel,
+        in_specs=[VMEM] * 2,
+        out_specs=[VMEM] * 2,
+        out_shape=[block] * 2,
+        compiler_params=SMALL,
+        cost_estimate=pl.CostEstimate(flops=0, transcendentals=0, bytes_accessed=WAIT),
+        name="square_blocks",
+    )(lower_one, lower_two)
 
 
 def pick_kernel(place, owner, rows, one, keep, send):
@@ -360,9 +402,10 @@
     )
     block = lax.ppermute(panels, ROW_COL, to_column(0))
     far_block = lax.ppermute(panels, ROW_COL, to_column(2))
-    sibling = lax.ppermute(panels, ROW_COL, other_core())
-    block, far_block, sibling = lax.optimization_barrier((block, far_block, sibling))
-    pair = jnp.stack([panels, sibling])
+    over_x = [panels]
+    for step in range(1, N_X):
+        over_x.append(lax.ppermute(panels, ROW_COL, along_x(step)))
+    block, far_block, over_x = lax.optimization_barrier((block, far_block, over_x))
     both = jnp.concatenate([block, far_block], axis=0)
     ring = [both]
     up = down = both
@@ -378,13 +421,13 @@
     )
     above = [lax.ppermute(batch, ROW_COL, along_y(-1)) for batch in batches]
     below = [lax.ppermute(batch, ROW_COL, along_y(1)) for batch in batches]
-    row_panels = [pair]
-    for step in range(1, N_X):
-        row_panels.append(lax.ppermute(pair, ROW_COL, along_x(step)))
+    own_core = jnp.stack(over_x)
+    row_panels = (own_core, lax.ppermute(own_core, ROW_COL, other_core()))
+    prepared = operands(
+        place, ancestor_inverse, (*ring, last_own, above[0], below[0], *row_panels)
+    )
     w_keep, w_send, y_keep, y_send = product_and_grams(
-        place,
-        ancestor_inverse,
-        (*ring, last_own, last_far, *above, *below, *row_panels),
+        place, prepared, (last_far, above[1], below[1])
     )
     w_own = w_keep + lax.ppermute(w_send, ROW_COL, other_core())
     y_send, w_own = lax.optimization_barrier((y_send, w_own))
@@ -394,21 +437,24 @@
         y_parts.append(lax.ppermute(y_own[step], ROW_COL, along_x(step)))
     w_part = jnp.sum(at_owner(w_own, PLANE), axis=0)
     inverses = inverse_rows(y_parts, masks, panel_above)
-    w_part, inverses = lax.optimization_barrier((w_part, inverses))
+    w_part, inverses, lower_one, lower_two = lax.optimization_barrier(
+        (w_part, inverses, lower_one, lower_two)
+    )
+    squares = square_blocks(lower_one, lower_two)
     inverses = lax.ppermute(inverses, ROW_COL, moves(result_place))
-    w_parts, inverses = lax.optimization_barrier((copies_of(w_part, "row_1"), inverses))
+    w_parts, inverses, squares = lax.optimization_barrier(
+        (copies_of(w_part, "row_1"), inverses, squares)
+    )
+    square_one, square_two = squares
     w_half = copies_of(jnp.sum(w_parts, axis=0), PLANE).reshape(w_own.shape)
     inverse_one, keep, send = pick_tiles(place, tile_owner, inverses)
     arrived = lax.ppermute(send, ROW_COL, other_core())
-    w_half, arrived = lax.optimization_barrier((w_half, arrived))
+    parts = sent_over_x(keep, arrived)
+    w_half, _ = lax.optimization_barrier((w_half, parts))
     w_other = lax.ppermute(w_half, ROW_COL, other_core())
-    parts = sent_over_x(keep, arrived)
-    square_one = dot(lower_one, lower_one, ((0,), (0,)))
-    square_two = dot(lower_two, lower_two, ((0,), (0,)))
     diag_one, cross_two, diag_two = final_blocks(
         place, w_half, w_other, square_one, square_two, panel_above
     )
-    parts, diag_two = lax.optimization_barrier((parts, diag_two))
     delivered = fill_slots(place, parts)
     return (inverse_one, diag_one, cross_two, diag_two, delivered)
 

time: 136 us -> 133 us (0.978)
  waiting for transfers between devices: 41.7 us -> 39.5 us
  Pallas kernels: 10 us -> 11.4 us
    ppermute x2, starting transfers between devices: 3.34 us -> 9.69 us  [local(): above = [lax.ppermute(batch, ROW_COL, along_y(-1)) for batch in batches]]
    ppermute x3, waiting for transfers between devices: 0.01 us -> 6.28 us  [local(): down = lax.ppermute(down, ROW_COL, along_z(-1))]
    ppermute x1, waiting for transfers between devices: 5.89 us -> 0.01 us  [local(): far_block = lax.ppermute(panels, ROW_COL, to_column(2))]
    all_to_all x2, waiting for transfers between devices: 4.22 us -> 0.01 us  [copies_of(): return lax.all_to_all(copies, axis, 0, 0, tiled=True)]
    ppermute x1, waiting for transfers between devices: 0.69 us -> 4.6 us  [local(): block = lax.ppermute(panels, ROW_COL, to_column(0))]
    ppermute x3, waiting for transfers between devices: 4.87 us -> 1.49 us  [local(): up = lax.ppermute(up, ROW_COL, along_z(1))]
    ppermute x1, starting transfers between devices: 4.94 us -> 1.91 us  [local(): block = lax.ppermute(panels, ROW_COL, to_column(0))]
    ppermute x1, starting transfers between devices: 6.87 us -> 9.61 us  [local(): far_block = lax.ppermute(panels, ROW_COL, to_column(2))]
  transfers between devices with their start and end apart: 32 -> 32, of which waited for: 16 -> 17; matrix products, arithmetic and copies ran while one was open for 1% -> 0% of each run, Pallas kernels for 2% -> 3%
where the time goes in v7:
time: 133 us; the launch traced here: 132 us
  starting transfers between devices  77.6 us (58%)
  waiting for transfers between devices  39.5 us (30%)
  Pallas kernels  11.4 us (9%)
  local copies, waits for them, and re-layouts  1.6 us (1%)
    all_to_all x2, starting transfers between devices, copies_of(): return lax.all_to_all(copies, axis, 0, 0, tiled=True)  12.7 us
    ppermute x2, starting transfers between devices, local(): above = [lax.ppermute(batch, ROW_COL, along_y(-1)) for batch in batches]  9.69 us
    ppermute x1, starting transfers between devices, local(): far_block = lax.ppermute(panels, ROW_COL, to_column(2))  9.61 us
    ppermute x3, starting transfers between devices, local(): up = lax.ppermute(up, ROW_COL, along_z(1))  7.83 us
    ppermute x1, waiting for transfers between devices, local(): inverses = lax.ppermute(inverses, ROW_COL, moves(result_place))  6.47 us
    ppermute x3, waiting for transfers between devices, local(): down = lax.ppermute(down, ROW_COL, along_z(-1))  6.28 us
    all_to_all x1, starting transfers between devices, at_owner(): return lax.all_to_all(parts, axis, 0, 0, tiled=True)  6.27 us
    all_to_all x1, waiting for transfers between devices, at_owner(): return lax.all_to_all(parts, axis, 0, 0, tiled=True)  5.53 us
  transfers between devices with their start and end apart: 32, of which 17 were waited for; matrix products, arithmetic and copies ran while one was open for 0% of the time, Pallas kernels for 3%

profile of v7, /device:TPU:1, one launch (start us, length us, event | category | flops | bytes accessed | tf_op | source)
XLA Modules:
  0.0 132.1 jit_solution(8291728842445932378)
XLA Ops:
  1.9 3.4 %collective-permute-start.4 = (f32[48,512]{1,0:T(8,128)S(1)}, f32[48,512]{1,0:T(8,128)S(1)}, u32[]{:S(2)}, u32[]{:S(2)}) collective-permute-start(f32[48,512]{1,0:T(8,128)S(1)} %get-tuple-element.45), channel_id=1, source_target_pairs={{0,6},{1,7},{2,0},{3,1},{4,2},{5,3},{6,4},{7,5},{8,14},{9,15},{10,... | collective-permute-start | bytes 294920 | tf_op jit(solution)/shard_map/ppermute | solution.py:407
  6.4 9.6 %collective-permute-start.1 = (f32[48,512]{1,0:T(8,128)S(1)}, f32[48,512]{1,0:T(8,128)S(1)}, u32[]{:S(2)}, u32[]{:S(2)}) collective-permute-start(f32[48,512]{1,0:T(8,128)S(1)} %get-tuple-element.45), channel_id=1, source_target_pairs={{0,128},{1,184},{2,192},{3,248},{4,0},{5,56},{6,64},{7,120},{8,136... | collective-permute-start | bytes 294920 | tf_op jit(solution)/shard_map/ppermute | solution.py:404
  16.0 1.9 %collective-permute-start = (f32[48,512]{1,0:T(8,128)S(1)}, f32[48,512]{1,0:T(8,128)S(1)}, u32[]{:S(2)}, u32[]{:S(2)}) collective-permute-start(f32[48,512]{1,0:T(8,128)S(1)} %get-tuple-element.45), channel_id=1, source_target_pairs={{0,0},{1,56},{2,64},{3,120},{4,128},{5,184},{6,192},{7,248},{8,8},... | collective-permute-start | bytes 294920 | tf_op jit(solution)/shard_map/ppermute | solution.py:403
  18.0 4.6 %collective-permute-done = f32[48,512]{1,0:T(8,128)S(1)} collective-permute-done((f32[48,512]{1,0:T(8,128)S(1)}, f32[48,512]{1,0:T(8,128)S(1)}, u32[]{:S(2)}, u32[]{:S(2)}) %collective-permute-start) | collective-permute-done | bytes 98336 | tf_op jit(solution)/shard_map/ppermute | solution.py:403
  22.7 3.5 %collective-permute-start.5 = (f32[96,512]{1,0:T(8,128)S(1)}, f32[96,512]{1,0:T(8,128)S(1)}, u32[]{:S(2)}, u32[]{:S(2)}) collective-permute-start(f32[96,512]{1,0:T(8,128)S(1)} %constant_dynamic-update-slice_fusion.refs_0_), channel_id=1, source_target_pairs={{0,8},{1,9},{2,10},{3,11},{4,12},{5,13},{6,14},{7,15},{8,16},{9,17... | collective-permute-start | bytes 589832 | tf_op jit(solution)/shard_map/ppermute | solution.py:413
  26.4 3.1 %collective-permute-done.6.refs_2_ = f32[96,512]{1,0:T(8,128)S(1)} collective-permute-done((f32[96,512]{1,0:T(8,128)S(1)}, f32[96,512]{1,0:T(8,128)S(1)}, u32[]{:S(2)}, u32[]{:S(2)}) %collective-permute-start.6) | collective-permute-done | bytes 196640 | tf_op jit(solution)/shard_map/ppermute | solution.py:414
  29.6 2.2 %collective-permute-start.7 = (f32[96,512]{1,0:T(8,128)S(1)}, f32[96,512]{1,0:T(8,128)S(1)}, u32[]{:S(2)}, u32[]{:S(2)}) collective-permute-start(f32[96,512]{1,0:T(8,128)S(1)} %collective-permute-done.5.refs_1_), channel_id=1, source_target_pairs={{0,8},{1,9},{2,10},{3,11},{4,12},{5,13},{6,14},{7,15},{8,16},{9,17... | collective-permute-start | bytes 589832 | tf_op jit(solution)/shard_map/ppermute | solution.py:413
  31.9 3.1 %collective-permute-done.8.refs_4_ = f32[96,512]{1,0:T(8,128)S(1)} collective-permute-done((f32[96,512]{1,0:T(8,128)S(1)}, f32[96,512]{1,0:T(8,128)S(1)}, u32[]{:S(2)}, u32[]{:S(2)}) %collective-permute-start.8) | collective-permute-done | bytes 196640 | tf_op jit(solution)/shard_map/ppermute | solution.py:414
  35.2 1.3 %collective-permute-done.7.refs_3_ = f32[96,512]{1,0:T(8,128)S(1)} collective-permute-done((f32[96,512]{1,0:T(8,128)S(1)}, f32[96,512]{1,0:T(8,128)S(1)}, u32[]{:S(2)}, u32[]{:S(2)}) %collective-permute-start.7) | collective-permute-done | bytes 196640 | tf_op jit(solution)/shard_map/ppermute | solution.py:413
  36.6 2.1 %collective-permute-start.9 = (f32[96,512]{1,0:T(8,128)S(1)}, f32[96,512]{1,0:T(8,128)S(1)}, u32[]{:S(2)}, u32[]{:S(2)}) collective-permute-start(f32[96,512]{1,0:T(8,128)S(1)} %collective-permute-done.7.refs_3_), channel_id=1, source_target_pairs={{0,8},{1,9},{2,10},{3,11},{4,12},{5,13},{6,14},{7,15},{8,16},{9,17... | collective-permute-start | bytes 589832 | tf_op jit(solution)/shard_map/ppermute | solution.py:413
  38.7 2.9 %collective-permute-start.13 = (f32[240,512]{1,0:T(8,128)S(1)}, f32[240,512]{1,0:T(8,128)S(1)}, u32[]{:S(2)}, u32[]{:S(2)}) collective-permute-start(f32[240,512]{1,0:T(8,128)S(1)} %slice_dynamic-update-slice_fusion), channel_id=1, source_target_pairs={{0,64},{1,65},{2,66},{3,67},{4,68},{5,69},{6,70},{7,71},{8,72},{9,... | collective-permute-start | bytes 1474568 | tf_op jit(solution)/shard_map/ppermute | solution.py:423
  41.6 3.9 %collective-permute-start.12 = (f32[240,512]{1,0:T(8,128)S(1)}, f32[240,512]{1,0:T(8,128)S(1)}, u32[]{:S(2)}, u32[]{:S(2)}) collective-permute-start(f32[240,512]{1,0:T(8,128)S(1)} %slice_dynamic-update-slice_fusion), channel_id=1, source_target_pairs={{0,192},{1,193},{2,194},{3,195},{4,196},{5,197},{6,198},{7,199},{8... | collective-permute-start | bytes 1474568 | tf_op jit(solution)/shard_map/ppermute | solution.py:422
  45.6 4.9 %collective-permute-done.11.refs_7_ = f32[48,512]{1,0:T(8,128)S(1)} collective-permute-done((f32[48,512]{1,0:T(8,128)S(1)}, f32[48,512]{1,0:T(8,128)S(1)}, u32[]{:S(2)}, u32[]{:S(2)}) %collective-permute-start.11) | collective-permute-done | bytes 98336 | tf_op jit(solution)/shard_map/ppermute | solution.py:416
  50.7 5.8 %collective-permute-start.16 = (f32[144,512]{1,0:T(8,128)S(1)}, f32[144,512]{1,0:T(8,128)S(1)}, u32[]{:S(2)}, u32[]{:S(2)}) collective-permute-start(f32[144,512]{1,0:T(8,128)S(1)} %pad_maximum_fusion.1), channel_id=1, source_target_pairs={{0,192},{1,193},{2,194},{3,195},{4,196},{5,197},{6,198},{7,199},{8... | collective-permute-start | bytes 884744 | tf_op jit(solution)/shard_map/ppermute | solution.py:422
  57.9 2.1 %collective-permute-done.15.last_far = f32[48,512]{1,0:T(8,128)S(1)} collective-permute-done((f32[48,512]{1,0:T(8,128)S(1)}, f32[48,512]{1,0:T(8,128)S(1)}, u32[]{:S(2)}, u32[]{:S(2)}) %collective-permute-start.15) | collective-permute-done | bytes 98336 | tf_op jit(solution)/shard_map/ppermute | solution.py:417
  60.3 3.4 %product_and_grams.1 = (f32[384,256]{1,0:T(8,128)S(1)}, f32[384,256]{1,0:T(8,128)S(1)}, f32[4,48,512]{2,1,0:T(8,128)S(1)}, f32[4,48,512]{2,1,0:T(8,128)S(1)}, bf...) custom-call(s32[4]{0:T(128)S(1)} %pad_add_fusion.place, ...), custom_call_target="tpu_custom_call", output_to_operand_aliasing={{4}: (8, {}), {5}: (9, {})} | custom-call | tf_op jit(solution)/shard_map/product_and_grams/pallas_call | solution.py:222
  63.8 4.8 %collective-permute-start.18 = (f32[384,256]{1,0:T(8,128)S(1)}, f32[384,256]{1,0:T(8,128)S(1)}, u32[]{:S(2)}, u32[]{:S(2)}) collective-permute-start(f32[384,256]{1,0:T(8,128)S(1)} %get-tuple-element.57), channel_id=1, source_target_pairs={{0,1},{1,0},{2,3},{3,2},{4,5},{5,4},{6,7},{7,6},{8,9},{9,8},{10,11... | collective-permute-start | bytes 1179656 | tf_op jit(solution)/shard_map/ppermute | solution.py:432
  68.6 1.3 %collective-permute-done.18 = f32[384,256]{1,0:T(8,128)S(1)} collective-permute-done((f32[384,256]{1,0:T(8,128)S(1)}, f32[384,256]{1,0:T(8,128)S(1)}, u32[]{:S(2)}, u32[]{:S(2)}) %collective-permute-start.18) | collective-permute-done | bytes 393248 | tf_op jit(solution)/shard_map/ppermute | solution.py:432
  71.1 6.3 %all-to-all-start = ((f32[16,24,256]{2,1,0:T(8,128)}), f32[16,24,256]{2,1,0:T(8,128)S(1)}, u32[]{:S(2)}, u32[]{:S(2)}) async-start(f32[16,24,256]{2,1,0:T(8,128)} %bitcast.12), calls=%async_computation | async-start | bytes 786432 | tf_op jit(solution)/shard_map/all_to_all | solution.py:247
  77.5 2.6 %collective-permute-start.22 = (f32[48,512]{1,0:T(8,128)S(1)}, f32[48,512]{1,0:T(8,128)S(1)}, u32[]{:S(2)}, u32[]{:S(2)}) collective-permute-start(f32[48,512]{1,0:T(8,128)S(1)} %get-tuple-element.79), channel_id=1, source_target_pairs={{0,6},{1,7},{2,0},{3,1},{4,2},{5,3},{6,4},{7,5},{8,14},{9,15},{10,... | collective-permute-start | bytes 294920 | tf_op jit(solution)/shard_map/ppermute | solution.py:437
  81.3 5.5 %all-to-all-done = f32[16,24,256]{2,1,0:T(8,128)S(1)} async-done(((f32[16,24,256]{2,1,0:T(8,128)}), f32[16,24,256]{2,1,0:T(8,128)S(1)}, u32[]{:S(2)}, u32[]{:S(2)}) %all-to-all-start) | async-done | bytes 393248 | tf_op jit(solution)/shard_map/all_to_all | solution.py:247
  87.2 2.3 %collective-permute-done.20.y1 = f32[48,512]{1,0:T(8,128)S(1)} collective-permute-done((f32[48,512]{1,0:T(8,128)S(1)}, f32[48,512]{1,0:T(8,128)S(1)}, u32[]{:S(2)}, u32[]{:S(2)}) %collective-permute-start.20) | collective-permute-done | bytes 98336 | tf_op jit(solution)/shard_map/ppermute | solution.py:437
  90.4 3.5 %all-to-all-start.1 = ((f32[8,24,256]{2,1,0:T(8,128)}), f32[8,24,256]{2,1,0:T(8,128)S(1)}, u32[]{:S(2)}, u32[]{:S(2)}) async-start(f32[8,24,256]{2,1,0:T(8,128)} %broadcast_in_dim.7), calls=%async_computation.1 | async-start | bytes 393216 | tf_op jit(solution)/shard_map/all_to_all | solution.py:252
  94.0 4.6 %collective-permute-start.23 = (f32[48,512]{1,0:T(8,128)S(1)}, f32[48,512]{1,0:T(8,128)S(1)}, u32[]{:S(2)}, u32[]{:S(2)}) collective-permute-start(f32[48,512]{1,0:T(8,128)S(1)} %inverse_rows.1), channel_id=1, source_target_pairs={{0,0},{1,8},{2,16},{3,24},{4,32},{5,40},{6,48},{7,56},{8,64},{9,72... | collective-permute-start | bytes 294920 | tf_op jit(solution)/shard_map/ppermute | solution.py:444
  99.3 6.5 %collective-permute-done.23.rows = f32[48,512]{1,0:T(8,128)S(1)} collective-permute-done((f32[48,512]{1,0:T(8,128)S(1)}, f32[48,512]{1,0:T(8,128)S(1)}, u32[]{:S(2)}, u32[]{:S(2)}) %collective-permute-start.23) | collective-permute-done | bytes 98336 | tf_op jit(solution)/shard_map/ppermute | solution.py:444
  106.6 9.2 %all-to-all-start.2 = ((f32[16,24,256]{2,1,0:T(8,128)}), f32[16,24,256]{2,1,0:T(8,128)S(1)}, u32[]{:S(2)}, u32[]{:S(2)}) async-start(f32[16,24,256]{2,1,0:T(8,128)} %broadcast_in_dim.8), calls=%async_computation.2 | async-start | bytes 786432 | tf_op jit(solution)/shard_map/all_to_all | solution.py:252
  117.0 1.8 %collective-permute-start.24 = (f32[8,8,256]{2,1,0:T(8,128)S(1)}, f32[8,8,256]{2,1,0:T(8,128)S(1)}, u32[]{:S(2)}, u32[]{:S(2)}) collective-permute-start(f32[8,8,256]{2,1,0:T(8,128)S(1)} %get-tuple-element.72), channel_id=1, source_target_pairs={{0,1},{1,0},{2,3},{3,2},{4,5},{5,4},{6,7},{7,6},{8,9},{9,8},{10,11... | collective-permute-start | bytes 196616 | tf_op jit(solution)/shard_map/ppermute | solution.py:451
  119.7 2.9 %collective-permute-start.27 = (f32[2,2,8,256]{3,2,1,0:T(8,128)S(1)}, f32[2,2,8,256]{3,2,1,0:T(8,128)S(1)}, u32[]{:S(2)}, u32[]{:S(2)}) collective-permute-start(f32[2,2,8,256]{3,2,1,0:T(8,128)S(1)} %get-tuple-element.85), channel_id=1, source_target_pairs={{0,6},{1,7},{2,0},{3,1},{4,2},{5,3},{6,4},{7,5},{8,14},{9,15},{10,... | collective-permute-start | bytes 98312 | tf_op jit(solution)/shard_map/ppermute | solution.py:352
  122.6 1.8 %collective-permute-start.26 = (f32[2,2,8,256]{3,2,1,0:T(8,128)S(1)}, f32[2,2,8,256]{3,2,1,0:T(8,128)S(1)}, u32[]{:S(2)}, u32[]{:S(2)}) collective-permute-start(f32[2,2,8,256]{3,2,1,0:T(8,128)S(1)} %get-tuple-element.88), channel_id=1, source_target_pairs={{0,4},{1,5},{2,6},{3,7},{4,0},{5,1},{6,2},{7,3},{8,12},{9,13},{10,... | collective-permute-start | bytes 98312 | tf_op jit(solution)/shard_map/ppermute | solution.py:352
  124.4 2.3 %collective-permute-done.25.p1 = f32[2,2,8,256]{3,2,1,0:T(8,128)S(1)} collective-permute-done((f32[2,2,8,256]{3,2,1,0:T(8,128)S(1)}, f32[2,2,8,256]{3,2,1,0:T(8,128)S(1)}, u32[]{:S(2)}, u32[]{:S(2)}) %collective-permute-start.25) | collective-permute-done | bytes 32800 | tf_op jit(solution)/shard_map/ppermute | solution.py:352
  127.1 1.6 %collective-permute-start.28 = (f32[384,256]{1,0:T(8,128)S(1)}, f32[384,256]{1,0:T(8,128)S(1)}, u32[]{:S(2)}, u32[]{:S(2)}) collective-permute-start(f32[384,256]{1,0:T(8,128)S(1)} %bitcast.32), channel_id=1, source_target_pairs={{0,1},{1,0},{2,3},{3,2},{4,5},{5,4},{6,7},{7,6},{8,9},{9,8},{10,11... | collective-permute-start | bytes 1179656 | tf_op jit(solution)/shard_map/ppermute | solution.py:454
  130.1 2.0 %final_blocks.1 = (f32[256,256]{1,0:T(8,128)}, f32[256,256]{1,0:T(8,128)}, f32[256,256]{1,0:T(8,128)}) custom-call(s32[4]{0:T(128)S(1)} %pad_add_fusion.place, f32[384,256]{1,0:T(8,128)S(1)} %bitcast.33, f32[384,256]{1,0:T(8,128)S(1)} %collective-permute-done.28.other, f32[256,256]{1,0:T(8,128)S(1)} %get-tuple-element.74.square_one, ...), custom_call_target="tpu_custom_call" | custom-call | tf_op jit(solution)/shard_map/final_blocks/pallas_call | solution.py:375
  (69 shorter events, 14.2 us)
Async XLA Ops:
  1.9 16.0 %collective-permute-start.4 = (f32[48,512]{1,0:T(8,128)S(1)}, f32[48,512]{1,0:T(8,128)S(1)}, u32[]{:S(2)}, u32[]{:S(2)}) collective-permute-start(f32[48,512]{1,0:T(8,128)S(1)} %get-tuple-element.45), channel_id=1, source_target_pairs={{0,6},{1,7},{2,0},{3,1},{4,2},{5,3},{6,4},{7,5},{8,14},{9,15},{10,... | collective-permute-start | bytes 294920 | tf_op jit(solution)/shard_map/ppermute | solution.py:407
  5.3 12.7 %collective-permute-start.3 = (f32[48,512]{1,0:T(8,128)S(1)}, f32[48,512]{1,0:T(8,128)S(1)}, u32[]{:S(2)}, u32[]{:S(2)}) collective-permute-start(f32[48,512]{1,0:T(8,128)S(1)} %get-tuple-element.45), channel_id=1, source_target_pairs={{0,4},{1,5},{2,6},{3,7},{4,0},{5,1},{6,2},{7,3},{8,12},{9,13},{10,... | collective-permute-start | bytes 294920 | tf_op jit(solution)/shard_map/ppermute | solution.py:407
  5.8 12.2 %collective-permute-start.2 = (f32[48,512]{1,0:T(8,128)S(1)}, f32[48,512]{1,0:T(8,128)S(1)}, u32[]{:S(2)}, u32[]{:S(2)}) collective-permute-start(f32[48,512]{1,0:T(8,128)S(1)} %get-tuple-element.45), channel_id=1, source_target_pairs={{0,2},{1,3},{2,4},{3,5},{4,6},{5,7},{6,0},{7,1},{8,10},{9,11},{10,... | collective-permute-start | bytes 294920 | tf_op jit(solution)/shard_map/ppermute | solution.py:407
  6.4 11.6 %collective-permute-start.1 = (f32[48,512]{1,0:T(8,128)S(1)}, f32[48,512]{1,0:T(8,128)S(1)}, u32[]{:S(2)}, u32[]{:S(2)}) collective-permute-start(f32[48,512]{1,0:T(8,128)S(1)} %get-tuple-element.45), channel_id=1, source_target_pairs={{0,128},{1,184},{2,192},{3,248},{4,0},{5,56},{6,64},{7,120},{8,136... | collective-permute-start | bytes 294920 | tf_op jit(solution)/shard_map/ppermute | solution.py:404
  16.0 6.6 %collective-permute-start = (f32[48,512]{1,0:T(8,128)S(1)}, f32[48,512]{1,0:T(8,128)S(1)}, u32[]{:S(2)}, u32[]{:S(2)}) collective-permute-start(f32[48,512]{1,0:T(8,128)S(1)} %get-tuple-element.45), channel_id=1, source_target_pairs={{0,0},{1,56},{2,64},{3,120},{4,128},{5,184},{6,192},{7,248},{8,8},... | collective-permute-start | bytes 294920 | tf_op jit(solution)/shard_map/ppermute | solution.py:403
  22.6 6.9 %collective-permute-start.6 = (f32[96,512]{1,0:T(8,128)S(1)}, f32[96,512]{1,0:T(8,128)S(1)}, u32[]{:S(2)}, u32[]{:S(2)}) collective-permute-start(f32[96,512]{1,0:T(8,128)S(1)} %constant_dynamic-update-slice_fusion.refs_0_), channel_id=1, source_target_pairs={{0,56},{1,57},{2,58},{3,59},{4,60},{5,61},{6,62},{7,63},{8,0},{9,1... | collective-permute-start | bytes 589832 | tf_op jit(solution)/shard_map/ppermute | solution.py:414
  22.7 6.9 %collective-permute-start.5 = (f32[96,512]{1,0:T(8,128)S(1)}, f32[96,512]{1,0:T(8,128)S(1)}, u32[]{:S(2)}, u32[]{:S(2)}) collective-permute-start(f32[96,512]{1,0:T(8,128)S(1)} %constant_dynamic-update-slice_fusion.refs_0_), channel_id=1, source_target_pairs={{0,8},{1,9},{2,10},{3,11},{4,12},{5,13},{6,14},{7,15},{8,16},{9,17... | collective-permute-start | bytes 589832 | tf_op jit(solution)/shard_map/ppermute | solution.py:413
  26.3 30.2 %collective-permute-start.14 = (f32[4,48,512]{2,1,0:T(8,128)S(1)}, f32[4,48,512]{2,1,0:T(8,128)S(1)}, u32[]{:S(2)}, u32[]{:S(2)}) collective-permute-start(f32[4,48,512]{2,1,0:T(8,128)S(1)} %pad_maximum_fusion.refs_10_), channel_id=1, source_target_pairs={{0,1},{1,0},{2,3},{3,2},{4,5},{5,4},{6,7},{7,6},{8,9},{9,8},{10,11... | collective-permute-start | bytes 1179656 | tf_op jit(solution)/shard_map/ppermute | solution.py:425
  29.5 5.5 %collective-permute-start.8 = (f32[96,512]{1,0:T(8,128)S(1)}, f32[96,512]{1,0:T(8,128)S(1)}, u32[]{:S(2)}, u32[]{:S(2)}) collective-permute-start(f32[96,512]{1,0:T(8,128)S(1)} %collective-permute-done.6.refs_2_), channel_id=1, source_target_pairs={{0,56},{1,57},{2,58},{3,59},{4,60},{5,61},{6,62},{7,63},{8,0},{9,1... | collective-permute-start | bytes 589832 | tf_op jit(solution)/shard_map/ppermute | solution.py:414
  29.6 6.9 %collective-permute-start.7 = (f32[96,512]{1,0:T(8,128)S(1)}, f32[96,512]{1,0:T(8,128)S(1)}, u32[]{:S(2)}, u32[]{:S(2)}) collective-permute-start(f32[96,512]{1,0:T(8,128)S(1)} %collective-permute-done.5.refs_1_), channel_id=1, source_target_pairs={{0,8},{1,9},{2,10},{3,11},{4,12},{5,13},{6,14},{7,15},{8,16},{9,17... | collective-permute-start | bytes 589832 | tf_op jit(solution)/shard_map/ppermute | solution.py:413
  35.0 10.6 %collective-permute-start.10 = (f32[96,512]{1,0:T(8,128)S(1)}, f32[96,512]{1,0:T(8,128)S(1)}, u32[]{:S(2)}, u32[]{:S(2)}) collective-permute-start(f32[96,512]{1,0:T(8,128)S(1)} %collective-permute-done.8.refs_4_), channel_id=1, source_target_pairs={{0,56},{1,57},{2,58},{3,59},{4,60},{5,61},{6,62},{7,63},{8,0},{9,1... | collective-permute-start | bytes 589832 | tf_op jit(solution)/shard_map/ppermute | solution.py:414
  36.6 9.0 %collective-permute-start.9 = (f32[96,512]{1,0:T(8,128)S(1)}, f32[96,512]{1,0:T(8,128)S(1)}, u32[]{:S(2)}, u32[]{:S(2)}) collective-permute-start(f32[96,512]{1,0:T(8,128)S(1)} %collective-permute-done.7.refs_3_), channel_id=1, source_target_pairs={{0,8},{1,9},{2,10},{3,11},{4,12},{5,13},{6,14},{7,15},{8,16},{9,17... | collective-permute-start | bytes 589832 | tf_op jit(solution)/shard_map/ppermute | solution.py:413
  38.7 17.8 %collective-permute-start.13 = (f32[240,512]{1,0:T(8,128)S(1)}, f32[240,512]{1,0:T(8,128)S(1)}, u32[]{:S(2)}, u32[]{:S(2)}) collective-permute-start(f32[240,512]{1,0:T(8,128)S(1)} %slice_dynamic-update-slice_fusion), channel_id=1, source_target_pairs={{0,64},{1,65},{2,66},{3,67},{4,68},{5,69},{6,70},{7,71},{8,72},{9,... | collective-permute-start | bytes 1474568 | tf_op jit(solution)/shard_map/ppermute | solution.py:423
  41.6 15.0 %collective-permute-start.12 = (f32[240,512]{1,0:T(8,128)S(1)}, f32[240,512]{1,0:T(8,128)S(1)}, u32[]{:S(2)}, u32[]{:S(2)}) collective-permute-start(f32[240,512]{1,0:T(8,128)S(1)} %slice_dynamic-update-slice_fusion), channel_id=1, source_target_pairs={{0,192},{1,193},{2,194},{3,195},{4,196},{5,197},{6,198},{7,199},{8... | collective-permute-start | bytes 1474568 | tf_op jit(solution)/shard_map/ppermute | solution.py:422
  45.5 5.1 %collective-permute-start.11 = (f32[48,512]{1,0:T(8,128)S(1)}, f32[48,512]{1,0:T(8,128)S(1)}, u32[]{:S(2)}, u32[]{:S(2)}) collective-permute-start(f32[48,512]{1,0:T(8,128)S(1)} %slice.61), channel_id=1, source_target_pairs={{0,8},{1,9},{2,10},{3,11},{4,12},{5,13},{6,14},{7,15},{8,16},{9,17... | collective-permute-start | bytes 294920 | tf_op jit(solution)/shard_map/ppermute | solution.py:416
  50.6 9.7 %collective-permute-start.17 = (f32[144,512]{1,0:T(8,128)S(1)}, f32[144,512]{1,0:T(8,128)S(1)}, u32[]{:S(2)}, u32[]{:S(2)}) collective-permute-start(f32[144,512]{1,0:T(8,128)S(1)} %pad_maximum_fusion.1), channel_id=1, source_target_pairs={{0,64},{1,65},{2,66},{3,67},{4,68},{5,69},{6,70},{7,71},{8,72},{9,... | collective-permute-start | bytes 884744 | tf_op jit(solution)/shard_map/ppermute | solution.py:423
  50.7 9.6 %collective-permute-start.16 = (f32[144,512]{1,0:T(8,128)S(1)}, f32[144,512]{1,0:T(8,128)S(1)}, u32[]{:S(2)}, u32[]{:S(2)}) collective-permute-start(f32[144,512]{1,0:T(8,128)S(1)} %pad_maximum_fusion.1), channel_id=1, source_target_pairs={{0,192},{1,193},{2,194},{3,195},{4,196},{5,197},{6,198},{7,199},{8... | collective-permute-start | bytes 884744 | tf_op jit(solution)/shard_map/ppermute | solution.py:422
  56.5 3.5 %collective-permute-start.15 = (f32[48,512]{1,0:T(8,128)S(1)}, f32[48,512]{1,0:T(8,128)S(1)}, u32[]{:S(2)}, u32[]{:S(2)}) collective-permute-start(f32[48,512]{1,0:T(8,128)S(1)} %get-tuple-element.84), channel_id=1, source_target_pairs={{0,56},{1,57},{2,58},{3,59},{4,60},{5,61},{6,62},{7,63},{8,0},{9,1... | collective-permute-start | bytes 294920 | tf_op jit(solution)/shard_map/ppermute | solution.py:417
  63.8 6.2 %collective-permute-start.18 = (f32[384,256]{1,0:T(8,128)S(1)}, f32[384,256]{1,0:T(8,128)S(1)}, u32[]{:S(2)}, u32[]{:S(2)}) collective-permute-start(f32[384,256]{1,0:T(8,128)S(1)} %get-tuple-element.57), channel_id=1, source_target_pairs={{0,1},{1,0},{2,3},{3,2},{4,5},{5,4},{6,7},{7,6},{8,9},{9,8},{10,11... | collective-permute-start | bytes 1179656 | tf_op jit(solution)/shard_map/ppermute | solution.py:432
  70.8 6.7 %collective-permute-start.19 = (f32[4,48,512]{2,1,0:T(8,128)S(1)}, f32[4,48,512]{2,1,0:T(8,128)S(1)}, u32[]{:S(2)}, u32[]{:S(2)}) collective-permute-start(f32[4,48,512]{2,1,0:T(8,128)S(1)} %get-tuple-element.60), channel_id=1, source_target_pairs={{0,1},{1,0},{2,3},{3,2},{4,5},{5,4},{6,7},{7,6},{8,9},{9,8},{10,11... | collective-permute-start | bytes 1179656 | tf_op jit(solution)/shard_map/ppermute | solution.py:434
  71.1 15.8 %all-to-all-start = ((f32[16,24,256]{2,1,0:T(8,128)}), f32[16,24,256]{2,1,0:T(8,128)S(1)}, u32[]{:S(2)}, u32[]{:S(2)}) async-start(f32[16,24,256]{2,1,0:T(8,128)} %bitcast.12), calls=%async_computation | async-start | bytes 786432 | tf_op jit(solution)/shard_map/all_to_all | solution.py:247
  77.5 9.4 %collective-permute-start.22 = (f32[48,512]{1,0:T(8,128)S(1)}, f32[48,512]{1,0:T(8,128)S(1)}, u32[]{:S(2)}, u32[]{:S(2)}) collective-permute-start(f32[48,512]{1,0:T(8,128)S(1)} %get-tuple-element.79), channel_id=1, source_target_pairs={{0,6},{1,7},{2,0},{3,1},{4,2},{5,3},{6,4},{7,5},{8,14},{9,15},{10,... | collective-permute-start | bytes 294920 | tf_op jit(solution)/shard_map/ppermute | solution.py:437
  80.2 7.0 %collective-permute-start.21 = (f32[48,512]{1,0:T(8,128)S(1)}, f32[48,512]{1,0:T(8,128)S(1)}, u32[]{:S(2)}, u32[]{:S(2)}) collective-permute-start(f32[48,512]{1,0:T(8,128)S(1)} %get-tuple-element.80), channel_id=1, source_target_pairs={{0,4},{1,5},{2,6},{3,7},{4,0},{5,1},{6,2},{7,3},{8,12},{9,13},{10,... | collective-permute-start | bytes 294920 | tf_op jit(solution)/shard_map/ppermute | solution.py:437
  80.8 8.7 %collective-permute-start.20 = (f32[48,512]{1,0:T(8,128)S(1)}, f32[48,512]{1,0:T(8,128)S(1)}, u32[]{:S(2)}, u32[]{:S(2)}) collective-permute-start(f32[48,512]{1,0:T(8,128)S(1)} %get-tuple-element.81), channel_id=1, source_target_pairs={{0,2},{1,3},{2,4},{3,5},{4,6},{5,7},{6,0},{7,1},{8,10},{9,11},{10,... | collective-permute-start | bytes 294920 | tf_op jit(solution)/shard_map/ppermute | solution.py:437
  90.4 15.3 %all-to-all-start.1 = ((f32[8,24,256]{2,1,0:T(8,128)}), f32[8,24,256]{2,1,0:T(8,128)S(1)}, u32[]{:S(2)}, u32[]{:S(2)}) async-start(f32[8,24,256]{2,1,0:T(8,128)} %broadcast_in_dim.7), calls=%async_computation.1 | async-start | bytes 393216 | tf_op jit(solution)/shard_map/all_to_all | solution.py:252
  94.0 11.8 %collective-permute-start.23 = (f32[48,512]{1,0:T(8,128)S(1)}, f32[48,512]{1,0:T(8,128)S(1)}, u32[]{:S(2)}, u32[]{:S(2)}) collective-permute-start(f32[48,512]{1,0:T(8,128)S(1)} %inverse_rows.1), channel_id=1, source_target_pairs={{0,0},{1,8},{2,16},{3,24},{4,32},{5,40},{6,48},{7,56},{8,64},{9,72... | collective-permute-start | bytes 294920 | tf_op jit(solution)/shard_map/ppermute | solution.py:444
  106.6 20.6 %all-to-all-start.2 = ((f32[16,24,256]{2,1,0:T(8,128)}), f32[16,24,256]{2,1,0:T(8,128)S(1)}, u32[]{:S(2)}, u32[]{:S(2)}) async-start(f32[16,24,256]{2,1,0:T(8,128)} %broadcast_in_dim.8), calls=%async_computation.2 | async-start | bytes 786432 | tf_op jit(solution)/shard_map/all_to_all | solution.py:252
  117.0 2.7 %collective-permute-start.24 = (f32[8,8,256]{2,1,0:T(8,128)S(1)}, f32[8,8,256]{2,1,0:T(8,128)S(1)}, u32[]{:S(2)}, u32[]{:S(2)}) collective-permute-start(f32[8,8,256]{2,1,0:T(8,128)S(1)} %get-tuple-element.72), channel_id=1, source_target_pairs={{0,1},{1,0},{2,3},{3,2},{4,5},{5,4},{6,7},{7,6},{8,9},{9,8},{10,11... | collective-permute-start | bytes 196616 | tf_op jit(solution)/shard_map/ppermute | solution.py:451
  119.7 4.7 %collective-permute-start.27 = (f32[2,2,8,256]{3,2,1,0:T(8,128)S(1)}, f32[2,2,8,256]{3,2,1,0:T(8,128)S(1)}, u32[]{:S(2)}, u32[]{:S(2)}) collective-permute-start(f32[2,2,8,256]{3,2,1,0:T(8,128)S(1)} %get-tuple-element.85), channel_id=1, source_target_pairs={{0,6},{1,7},{2,0},{3,1},{4,2},{5,3},{6,4},{7,5},{8,14},{9,15},{10,... | collective-permute-start | bytes 98312 | tf_op jit(solution)/shard_map/ppermute | solution.py:352
  122.6 4.0 %collective-permute-start.25 = (f32[2,2,8,256]{3,2,1,0:T(8,128)S(1)}, f32[2,2,8,256]{3,2,1,0:T(8,128)S(1)}, u32[]{:S(2)}, u32[]{:S(2)}) collective-permute-start(f32[2,2,8,256]{3,2,1,0:T(8,128)S(1)} %get-tuple-element.87), channel_id=1, source_target_pairs={{0,2},{1,3},{2,4},{3,5},{4,6},{5,7},{6,0},{7,1},{8,10},{9,11},{10,... | collective-permute-start | bytes 98312 | tf_op jit(solution)/shard_map/ppermute | solution.py:352
  122.6 4.5 %collective-permute-start.26 = (f32[2,2,8,256]{3,2,1,0:T(8,128)S(1)}, f32[2,2,8,256]{3,2,1,0:T(8,128)S(1)}, u32[]{:S(2)}, u32[]{:S(2)}) collective-permute-start(f32[2,2,8,256]{3,2,1,0:T(8,128)S(1)} %get-tuple-element.88), channel_id=1, source_target_pairs={{0,4},{1,5},{2,6},{3,7},{4,0},{5,1},{6,2},{7,3},{8,12},{9,13},{10,... | collective-permute-start | bytes 98312 | tf_op jit(solution)/shard_map/ppermute | solution.py:352
  127.1 3.0 %collective-permute-start.28 = (f32[384,256]{1,0:T(8,128)S(1)}, f32[384,256]{1,0:T(8,128)S(1)}, u32[]{:S(2)}, u32[]{:S(2)}) collective-permute-start(f32[384,256]{1,0:T(8,128)S(1)} %bitcast.32), channel_id=1, source_target_pairs={{0,1},{1,0},{2,3},{3,2},{4,5},{5,4},{6,7},{7,6},{8,9},{9,8},{10,11... | collective-permute-start | bytes 1179656 | tf_op jit(solution)/shard_map/ppermute | solution.py:454
  (5 other events, 141.4 us)

commit v8 on v7

--- a/solution.py
+++ b/solution.py
@@ -400,11 +400,11 @@
     panels, masks = masked_panels(
         start.astype(jnp.int32)[None], struct_one, struct_two, panel_one, panel_two
     )
-    block = lax.ppermute(panels, ROW_COL, to_column(0))
-    far_block = lax.ppermute(panels, ROW_COL, to_column(2))
     over_x = [panels]
     for step in range(1, N_X):
         over_x.append(lax.ppermute(panels, ROW_COL, along_x(step)))
+    far_block = lax.ppermute(panels, ROW_COL, to_column(2))
+    block = lax.ppermute(panels, ROW_COL, to_column(0))
     block, far_block, over_x = lax.optimization_barrier((block, far_block, over_x))
     both = jnp.concatenate([block, far_block], axis=0)
     ring = [both]

time: 133 us -> 133 us (level)
  no operation moved by 1% of the time
where the time goes in v8:
time: 133 us; the launch traced here: 132 us
  starting transfers between devices  77.6 us (58%)
  waiting for transfers between devices  39.5 us (30%)
  Pallas kernels  11.4 us (9%)
  local copies, waits for them, and re-layouts  1.6 us (1%)
    all_to_all x2, starting transfers between devices, copies_of(): return lax.all_to_all(copies, axis, 0, 0, tiled=True)  12.7 us
    ppermute x2, starting transfers between devices, local(): above = [lax.ppermute(batch, ROW_COL, along_y(-1)) for batch in batches]  9.69 us
    ppermute x1, starting transfers between devices, local(): far_block = lax.ppermute(panels, ROW_COL, to_column(2))  9.61 us
    ppermute x3, starting transfers between devices, local(): up = lax.ppermute(up, ROW_COL, along_z(1))  7.83 us
    ppermute x1, waiting for transfers between devices, local(): inverses = lax.ppermute(inverses, ROW_COL, moves(result_place))  6.47 us
    ppermute x3, waiting for transfers between devices, local(): down = lax.ppermute(down, ROW_COL, along_z(-1))  6.28 us
    all_to_all x1, starting transfers between devices, at_owner(): return lax.all_to_all(parts, axis, 0, 0, tiled=True)  6.27 us
    all_to_all x1, waiting for transfers between devices, at_owner(): return lax.all_to_all(parts, axis, 0, 0, tiled=True)  5.53 us
  transfers between devices with their start and end apart: 32, of which 17 were waited for; matrix products, arithmetic and copies ran while one was open for 0% of the time, Pallas kernels for 3%

profile of v8, /device:TPU:1, one launch (start us, length us, event | category | flops | bytes accessed | tf_op | source)
XLA Modules:
  0.0 132.1 jit_solution(8291728842445932378)
XLA Ops:
  1.9 3.4 %collective-permute-start.4 = (f32[48,512]{1,0:T(8,128)S(1)}, f32[48,512]{1,0:T(8,128)S(1)}, u32[]{:S(2)}, u32[]{:S(2)}) collective-permute-start(f32[48,512]{1,0:T(8,128)S(1)} %get-tuple-element.45), channel_id=1, source_target_pairs={{0,6},{1,7},{2,0},{3,1},{4,2},{5,3},{6,4},{7,5},{8,14},{9,15},{10,... | collective-permute-start | bytes 294920 | tf_op jit(solution)/shard_map/ppermute | solution.py:405
  6.4 9.6 %collective-permute-start.1 = (f32[48,512]{1,0:T(8,128)S(1)}, f32[48,512]{1,0:T(8,128)S(1)}, u32[]{:S(2)}, u32[]{:S(2)}) collective-permute-start(f32[48,512]{1,0:T(8,128)S(1)} %get-tuple-element.45), channel_id=1, source_target_pairs={{0,128},{1,184},{2,192},{3,248},{4,0},{5,56},{6,64},{7,120},{8,136... | collective-permute-start | bytes 294920 | tf_op jit(solution)/shard_map/ppermute | solution.py:406
  16.0 1.9 %collective-permute-start = (f32[48,512]{1,0:T(8,128)S(1)}, f32[48,512]{1,0:T(8,128)S(1)}, u32[]{:S(2)}, u32[]{:S(2)}) collective-permute-start(f32[48,512]{1,0:T(8,128)S(1)} %get-tuple-element.45), channel_id=1, source_target_pairs={{0,0},{1,56},{2,64},{3,120},{4,128},{5,184},{6,192},{7,248},{8,8},... | collective-permute-start | bytes 294920 | tf_op jit(solution)/shard_map/ppermute | solution.py:407
  18.0 4.6 %collective-permute-done = f32[48,512]{1,0:T(8,128)S(1)} collective-permute-done((f32[48,512]{1,0:T(8,128)S(1)}, f32[48,512]{1,0:T(8,128)S(1)}, u32[]{:S(2)}, u32[]{:S(2)}) %collective-permute-start) | collective-permute-done | bytes 98336 | tf_op jit(solution)/shard_map/ppermute | solution.py:407
  22.7 3.5 %collective-permute-start.5 = (f32[96,512]{1,0:T(8,128)S(1)}, f32[96,512]{1,0:T(8,128)S(1)}, u32[]{:S(2)}, u32[]{:S(2)}) collective-permute-start(f32[96,512]{1,0:T(8,128)S(1)} %constant_dynamic-update-slice_fusion.refs_0_), channel_id=1, source_target_pairs={{0,8},{1,9},{2,10},{3,11},{4,12},{5,13},{6,14},{7,15},{8,16},{9,17... | collective-permute-start | bytes 589832 | tf_op jit(solution)/shard_map/ppermute | solution.py:413
  26.4 3.1 %collective-permute-done.6.refs_2_ = f32[96,512]{1,0:T(8,128)S(1)} collective-permute-done((f32[96,512]{1,0:T(8,128)S(1)}, f32[96,512]{1,0:T(8,128)S(1)}, u32[]{:S(2)}, u32[]{:S(2)}) %collective-permute-start.6) | collective-permute-done | bytes 196640 | tf_op jit(solution)/shard_map/ppermute | solution.py:414
  29.6 2.2 %collective-permute-start.7 = (f32[96,512]{1,0:T(8,128)S(1)}, f32[96,512]{1,0:T(8,128)S(1)}, u32[]{:S(2)}, u32[]{:S(2)}) collective-permute-start(f32[96,512]{1,0:T(8,128)S(1)} %collective-permute-done.5.refs_1_), channel_id=1, source_target_pairs={{0,8},{1,9},{2,10},{3,11},{4,12},{5,13},{6,14},{7,15},{8,16},{9,17... | collective-permute-start | bytes 589832 | tf_op jit(solution)/shard_map/ppermute | solution.py:413
  31.9 3.1 %collective-permute-done.8.refs_4_ = f32[96,512]{1,0:T(8,128)S(1)} collective-permute-done((f32[96,512]{1,0:T(8,128)S(1)}, f32[96,512]{1,0:T(8,128)S(1)}, u32[]{:S(2)}, u32[]{:S(2)}) %collective-permute-start.8) | collective-permute-done | bytes 196640 | tf_op jit(solution)/shard_map/ppermute | solution.py:414
  35.2 1.3 %collective-permute-done.7.refs_3_ = f32[96,512]{1,0:T(8,128)S(1)} collective-permute-done((f32[96,512]{1,0:T(8,128)S(1)}, f32[96,512]{1,0:T(8,128)S(1)}, u32[]{:S(2)}, u32[]{:S(2)}) %collective-permute-start.7) | collective-permute-done | bytes 196640 | tf_op jit(solution)/shard_map/ppermute | solution.py:413
  36.6 2.1 %collective-permute-start.9 = (f32[96,512]{1,0:T(8,128)S(1)}, f32[96,512]{1,0:T(8,128)S(1)}, u32[]{:S(2)}, u32[]{:S(2)}) collective-permute-start(f32[96,512]{1,0:T(8,128)S(1)} %collective-permute-done.7.refs_3_), channel_id=1, source_target_pairs={{0,8},{1,9},{2,10},{3,11},{4,12},{5,13},{6,14},{7,15},{8,16},{9,17... | collective-permute-start | bytes 589832 | tf_op jit(solution)/shard_map/ppermute | solution.py:413
  38.7 2.9 %collective-permute-start.13 = (f32[240,512]{1,0:T(8,128)S(1)}, f32[240,512]{1,0:T(8,128)S(1)}, u32[]{:S(2)}, u32[]{:S(2)}) collective-permute-start(f32[240,512]{1,0:T(8,128)S(1)} %slice_dynamic-update-slice_fusion), channel_id=1, source_target_pairs={{0,64},{1,65},{2,66},{3,67},{4,68},{5,69},{6,70},{7,71},{8,72},{9,... | collective-permute-start | bytes 1474568 | tf_op jit(solution)/shard_map/ppermute | solution.py:423
  41.6 3.9 %collective-permute-start.12 = (f32[240,512]{1,0:T(8,128)S(1)}, f32[240,512]{1,0:T(8,128)S(1)}, u32[]{:S(2)}, u32[]{:S(2)}) collective-permute-start(f32[240,512]{1,0:T(8,128)S(1)} %slice_dynamic-update-slice_fusion), channel_id=1, source_target_pairs={{0,192},{1,193},{2,194},{3,195},{4,196},{5,197},{6,198},{7,199},{8... | collective-permute-start | bytes 1474568 | tf_op jit(solution)/shard_map/ppermute | solution.py:422
  45.6 4.9 %collective-permute-done.11.refs_7_ = f32[48,512]{1,0:T(8,128)S(1)} collective-permute-done((f32[48,512]{1,0:T(8,128)S(1)}, f32[48,512]{1,0:T(8,128)S(1)}, u32[]{:S(2)}, u32[]{:S(2)}) %collective-permute-start.11) | collective-permute-done | bytes 98336 | tf_op jit(solution)/shard_map/ppermute | solution.py:416
  50.7 5.8 %collective-permute-start.16 = (f32[144,512]{1,0:T(8,128)S(1)}, f32[144,512]{1,0:T(8,128)S(1)}, u32[]{:S(2)}, u32[]{:S(2)}) collective-permute-start(f32[144,512]{1,0:T(8,128)S(1)} %pad_maximum_fusion.1), channel_id=1, source_target_pairs={{0,192},{1,193},{2,194},{3,195},{4,196},{5,197},{6,198},{7,199},{8... | collective-permute-start | bytes 884744 | tf_op jit(solution)/shard_map/ppermute | solution.py:422
  57.9 2.1 %collective-permute-done.15.last_far = f32[48,512]{1,0:T(8,128)S(1)} collective-permute-done((f32[48,512]{1,0:T(8,128)S(1)}, f32[48,512]{1,0:T(8,128)S(1)}, u32[]{:S(2)}, u32[]{:S(2)}) %collective-permute-start.15) | collective-permute-done | bytes 98336 | tf_op jit(solution)/shard_map/ppermute | solution.py:417
  60.3 3.4 %product_and_grams.1 = (f32[384,256]{1,0:T(8,128)S(1)}, f32[384,256]{1,0:T(8,128)S(1)}, f32[4,48,512]{2,1,0:T(8,128)S(1)}, f32[4,48,512]{2,1,0:T(8,128)S(1)}, bf...) custom-call(s32[4]{0:T(128)S(1)} %pad_add_fusion.place, ...), custom_call_target="tpu_custom_call", output_to_operand_aliasing={{4}: (8, {}), {5}: (9, {})} | custom-call | tf_op jit(solution)/shard_map/product_and_grams/pallas_call | solution.py:222
  63.8 4.8 %collective-permute-start.18 = (f32[384,256]{1,0:T(8,128)S(1)}, f32[384,256]{1,0:T(8,128)S(1)}, u32[]{:S(2)}, u32[]{:S(2)}) collective-permute-start(f32[384,256]{1,0:T(8,128)S(1)} %get-tuple-element.57), channel_id=1, source_target_pairs={{0,1},{1,0},{2,3},{3,2},{4,5},{5,4},{6,7},{7,6},{8,9},{9,8},{10,11... | collective-permute-start | bytes 1179656 | tf_op jit(solution)/shard_map/ppermute | solution.py:432
  68.6 1.3 %collective-permute-done.18 = f32[384,256]{1,0:T(8,128)S(1)} collective-permute-done((f32[384,256]{1,0:T(8,128)S(1)}, f32[384,256]{1,0:T(8,128)S(1)}, u32[]{:S(2)}, u32[]{:S(2)}) %collective-permute-start.18) | collective-permute-done | bytes 393248 | tf_op jit(solution)/shard_map/ppermute | solution.py:432
  71.1 6.3 %all-to-all-start = ((f32[16,24,256]{2,1,0:T(8,128)}), f32[16,24,256]{2,1,0:T(8,128)S(1)}, u32[]{:S(2)}, u32[]{:S(2)}) async-start(f32[16,24,256]{2,1,0:T(8,128)} %bitcast.12), calls=%async_computation | async-start | bytes 786432 | tf_op jit(solution)/shard_map/all_to_all | solution.py:247
  77.5 2.6 %collective-permute-start.22 = (f32[48,512]{1,0:T(8,128)S(1)}, f32[48,512]{1,0:T(8,128)S(1)}, u32[]{:S(2)}, u32[]{:S(2)}) collective-permute-start(f32[48,512]{1,0:T(8,128)S(1)} %get-tuple-element.79), channel_id=1, source_target_pairs={{0,6},{1,7},{2,0},{3,1},{4,2},{5,3},{6,4},{7,5},{8,14},{9,15},{10,... | collective-permute-start | bytes 294920 | tf_op jit(solution)/shard_map/ppermute | solution.py:437
  81.3 5.5 %all-to-all-done = f32[16,24,256]{2,1,0:T(8,128)S(1)} async-done(((f32[16,24,256]{2,1,0:T(8,128)}), f32[16,24,256]{2,1,0:T(8,128)S(1)}, u32[]{:S(2)}, u32[]{:S(2)}) %all-to-all-start) | async-done | bytes 393248 | tf_op jit(solution)/shard_map/all_to_all | solution.py:247
  87.2 2.3 %collective-permute-done.20.y1 = f32[48,512]{1,0:T(8,128)S(1)} collective-permute-done((f32[48,512]{1,0:T(8,128)S(1)}, f32[48,512]{1,0:T(8,128)S(1)}, u32[]{:S(2)}, u32[]{:S(2)}) %collective-permute-start.20) | collective-permute-done | bytes 98336 | tf_op jit(solution)/shard_map/ppermute | solution.py:437
  90.4 3.5 %all-to-all-start.1 = ((f32[8,24,256]{2,1,0:T(8,128)}), f32[8,24,256]{2,1,0:T(8,128)S(1)}, u32[]{:S(2)}, u32[]{:S(2)}) async-start(f32[8,24,256]{2,1,0:T(8,128)} %broadcast_in_dim.7), calls=%async_computation.1 | async-start | bytes 393216 | tf_op jit(solution)/shard_map/all_to_all | solution.py:252
  94.0 4.6 %collective-permute-start.23 = (f32[48,512]{1,0:T(8,128)S(1)}, f32[48,512]{1,0:T(8,128)S(1)}, u32[]{:S(2)}, u32[]{:S(2)}) collective-permute-start(f32[48,512]{1,0:T(8,128)S(1)} %inverse_rows.1), channel_id=1, source_target_pairs={{0,0},{1,8},{2,16},{3,24},{4,32},{5,40},{6,48},{7,56},{8,64},{9,72... | collective-permute-start | bytes 294920 | tf_op jit(solution)/shard_map/ppermute | solution.py:444
  99.3 6.5 %collective-permute-done.23.rows = f32[48,512]{1,0:T(8,128)S(1)} collective-permute-done((f32[48,512]{1,0:T(8,128)S(1)}, f32[48,512]{1,0:T(8,128)S(1)}, u32[]{:S(2)}, u32[]{:S(2)}) %collective-permute-start.23) | collective-permute-done | bytes 98336 | tf_op jit(solution)/shard_map/ppermute | solution.py:444
  106.6 9.2 %all-to-all-start.2 = ((f32[16,24,256]{2,1,0:T(8,128)}), f32[16,24,256]{2,1,0:T(8,128)S(1)}, u32[]{:S(2)}, u32[]{:S(2)}) async-start(f32[16,24,256]{2,1,0:T(8,128)} %broadcast_in_dim.8), calls=%async_computation.2 | async-start | bytes 786432 | tf_op jit(solution)/shard_map/all_to_all | solution.py:252
  117.0 1.8 %collective-permute-start.24 = (f32[8,8,256]{2,1,0:T(8,128)S(1)}, f32[8,8,256]{2,1,0:T(8,128)S(1)}, u32[]{:S(2)}, u32[]{:S(2)}) collective-permute-start(f32[8,8,256]{2,1,0:T(8,128)S(1)} %get-tuple-element.72), channel_id=1, source_target_pairs={{0,1},{1,0},{2,3},{3,2},{4,5},{5,4},{6,7},{7,6},{8,9},{9,8},{10,11... | collective-permute-start | bytes 196616 | tf_op jit(solution)/shard_map/ppermute | solution.py:451
  119.7 2.9 %collective-permute-start.27 = (f32[2,2,8,256]{3,2,1,0:T(8,128)S(1)}, f32[2,2,8,256]{3,2,1,0:T(8,128)S(1)}, u32[]{:S(2)}, u32[]{:S(2)}) collective-permute-start(f32[2,2,8,256]{3,2,1,0:T(8,128)S(1)} %get-tuple-element.85), channel_id=1, source_target_pairs={{0,6},{1,7},{2,0},{3,1},{4,2},{5,3},{6,4},{7,5},{8,14},{9,15},{10,... | collective-permute-start | bytes 98312 | tf_op jit(solution)/shard_map/ppermute | solution.py:352
  122.6 1.8 %collective-permute-start.26 = (f32[2,2,8,256]{3,2,1,0:T(8,128)S(1)}, f32[2,2,8,256]{3,2,1,0:T(8,128)S(1)}, u32[]{:S(2)}, u32[]{:S(2)}) collective-permute-start(f32[2,2,8,256]{3,2,1,0:T(8,128)S(1)} %get-tuple-element.88), channel_id=1, source_target_pairs={{0,4},{1,5},{2,6},{3,7},{4,0},{5,1},{6,2},{7,3},{8,12},{9,13},{10,... | collective-permute-start | bytes 98312 | tf_op jit(solution)/shard_map/ppermute | solution.py:352
  124.4 2.3 %collective-permute-done.25.p1 = f32[2,2,8,256]{3,2,1,0:T(8,128)S(1)} collective-permute-done((f32[2,2,8,256]{3,2,1,0:T(8,128)S(1)}, f32[2,2,8,256]{3,2,1,0:T(8,128)S(1)}, u32[]{:S(2)}, u32[]{:S(2)}) %collective-permute-start.25) | collective-permute-done | bytes 32800 | tf_op jit(solution)/shard_map/ppermute | solution.py:352
  127.1 1.6 %collective-permute-start.28 = (f32[384,256]{1,0:T(8,128)S(1)}, f32[384,256]{1,0:T(8,128)S(1)}, u32[]{:S(2)}, u32[]{:S(2)}) collective-permute-start(f32[384,256]{1,0:T(8,128)S(1)} %bitcast.32), channel_id=1, source_target_pairs={{0,1},{1,0},{2,3},{3,2},{4,5},{5,4},{6,7},{7,6},{8,9},{9,8},{10,11... | collective-permute-start | bytes 1179656 | tf_op jit(solution)/shard_map/ppermute | solution.py:454
  130.1 2.0 %final_blocks.1 = (f32[256,256]{1,0:T(8,128)}, f32[256,256]{1,0:T(8,128)}, f32[256,256]{1,0:T(8,128)}) custom-call(s32[4]{0:T(128)S(1)} %pad_add_fusion.place, f32[384,256]{1,0:T(8,128)S(1)} %bitcast.33, f32[384,256]{1,0:T(8,128)S(1)} %collective-permute-done.28.other, f32[256,256]{1,0:T(8,128)S(1)} %get-tuple-element.74.square_one, ...), custom_call_target="tpu_custom_call" | custom-call | tf_op jit(solution)/shard_map/final_blocks/pallas_call | solution.py:375
  (69 shorter events, 14.2 us)
Async XLA Ops:
  1.9 16.0 %collective-permute-start.4 = (f32[48,512]{1,0:T(8,128)S(1)}, f32[48,512]{1,0:T(8,128)S(1)}, u32[]{:S(2)}, u32[]{:S(2)}) collective-permute-start(f32[48,512]{1,0:T(8,128)S(1)} %get-tuple-element.45), channel_id=1, source_target_pairs={{0,6},{1,7},{2,0},{3,1},{4,2},{5,3},{6,4},{7,5},{8,14},{9,15},{10,... | collective-permute-start | bytes 294920 | tf_op jit(solution)/shard_map/ppermute | solution.py:405
  5.3 12.7 %collective-permute-start.3 = (f32[48,512]{1,0:T(8,128)S(1)}, f32[48,512]{1,0:T(8,128)S(1)}, u32[]{:S(2)}, u32[]{:S(2)}) collective-permute-start(f32[48,512]{1,0:T(8,128)S(1)} %get-tuple-element.45), channel_id=1, source_target_pairs={{0,4},{1,5},{2,6},{3,7},{4,0},{5,1},{6,2},{7,3},{8,12},{9,13},{10,... | collective-permute-start | bytes 294920 | tf_op jit(solution)/shard_map/ppermute | solution.py:405
  5.8 12.2 %collective-permute-start.2 = (f32[48,512]{1,0:T(8,128)S(1)}, f32[48,512]{1,0:T(8,128)S(1)}, u32[]{:S(2)}, u32[]{:S(2)}) collective-permute-start(f32[48,512]{1,0:T(8,128)S(1)} %get-tuple-element.45), channel_id=1, source_target_pairs={{0,2},{1,3},{2,4},{3,5},{4,6},{5,7},{6,0},{7,1},{8,10},{9,11},{10,... | collective-permute-start | bytes 294920 | tf_op jit(solution)/shard_map/ppermute | solution.py:405
  6.4 11.6 %collective-permute-start.1 = (f32[48,512]{1,0:T(8,128)S(1)}, f32[48,512]{1,0:T(8,128)S(1)}, u32[]{:S(2)}, u32[]{:S(2)}) collective-permute-start(f32[48,512]{1,0:T(8,128)S(1)} %get-tuple-element.45), channel_id=1, source_target_pairs={{0,128},{1,184},{2,192},{3,248},{4,0},{5,56},{6,64},{7,120},{8,136... | collective-permute-start | bytes 294920 | tf_op jit(solution)/shard_map/ppermute | solution.py:406
  16.0 6.6 %collective-permute-start = (f32[48,512]{1,0:T(8,128)S(1)}, f32[48,512]{1,0:T(8,128)S(1)}, u32[]{:S(2)}, u32[]{:S(2)}) collective-permute-start(f32[48,512]{1,0:T(8,128)S(1)} %get-tuple-element.45), channel_id=1, source_target_pairs={{0,0},{1,56},{2,64},{3,120},{4,128},{5,184},{6,192},{7,248},{8,8},... | collective-permute-start | bytes 294920 | tf_op jit(solution)/shard_map/ppermute | solution.py:407
  22.6 6.9 %collective-permute-start.6 = (f32[96,512]{1,0:T(8,128)S(1)}, f32[96,512]{1,0:T(8,128)S(1)}, u32[]{:S(2)}, u32[]{:S(2)}) collective-permute-start(f32[96,512]{1,0:T(8,128)S(1)} %constant_dynamic-update-slice_fusion.refs_0_), channel_id=1, source_target_pairs={{0,56},{1,57},{2,58},{3,59},{4,60},{5,61},{6,62},{7,63},{8,0},{9,1... | collective-permute-start | bytes 589832 | tf_op jit(solution)/shard_map/ppermute | solution.py:414
  22.7 6.9 %collective-permute-start.5 = (f32[96,512]{1,0:T(8,128)S(1)}, f32[96,512]{1,0:T(8,128)S(1)}, u32[]{:S(2)}, u32[]{:S(2)}) collective-permute-start(f32[96,512]{1,0:T(8,128)S(1)} %constant_dynamic-update-slice_fusion.refs_0_), channel_id=1, source_target_pairs={{0,8},{1,9},{2,10},{3,11},{4,12},{5,13},{6,14},{7,15},{8,16},{9,17... | collective-permute-start | bytes 589832 | tf_op jit(solution)/shard_map/ppermute | solution.py:413
  26.3 30.2 %collective-permute-start.14 = (f32[4,48,512]{2,1,0:T(8,128)S(1)}, f32[4,48,512]{2,1,0:T(8,128)S(1)}, u32[]{:S(2)}, u32[]{:S(2)}) collective-permute-start(f32[4,48,512]{2,1,0:T(8,128)S(1)} %pad_maximum_fusion.refs_10_), channel_id=1, source_target_pairs={{0,1},{1,0},{2,3},{3,2},{4,5},{5,4},{6,7},{7,6},{8,9},{9,8},{10,11... | collective-permute-start | bytes 1179656 | tf_op jit(solution)/shard_map/ppermute | solution.py:425
  29.5 5.5 %collective-permute-start.8 = (f32[96,512]{1,0:T(8,128)S(1)}, f32[96,512]{1,0:T(8,128)S(1)}, u32[]{:S(2)}, u32[]{:S(2)}) collective-permute-start(f32[96,512]{1,0:T(8,128)S(1)} %collective-permute-done.6.refs_2_), channel_id=1, source_target_pairs={{0,56},{1,57},{2,58},{3,59},{4,60},{5,61},{6,62},{7,63},{8,0},{9,1... | collective-permute-start | bytes 589832 | tf_op jit(solution)/shard_map/ppermute | solution.py:414
  29.6 6.9 %collective-permute-start.7 = (f32[96,512]{1,0:T(8,128)S(1)}, f32[96,512]{1,0:T(8,128)S(1)}, u32[]{:S(2)}, u32[]{:S(2)}) collective-permute-start(f32[96,512]{1,0:T(8,128)S(1)} %collective-permute-done.5.refs_1_), channel_id=1, source_target_pairs={{0,8},{1,9},{2,10},{3,11},{4,12},{5,13},{6,14},{7,15},{8,16},{9,17... | collective-permute-start | bytes 589832 | tf_op jit(solution)/shard_map/ppermute | solution.py:413
  35.0 10.6 %collective-permute-start.10 = (f32[96,512]{1,0:T(8,128)S(1)}, f32[96,512]{1,0:T(8,128)S(1)}, u32[]{:S(2)}, u32[]{:S(2)}) collective-permute-start(f32[96,512]{1,0:T(8,128)S(1)} %collective-permute-done.8.refs_4_), channel_id=1, source_target_pairs={{0,56},{1,57},{2,58},{3,59},{4,60},{5,61},{6,62},{7,63},{8,0},{9,1... | collective-permute-start | bytes 589832 | tf_op jit(solution)/shard_map/ppermute | solution.py:414
  36.6 9.0 %collective-permute-start.9 = (f32[96,512]{1,0:T(8,128)S(1)}, f32[96,512]{1,0:T(8,128)S(1)}, u32[]{:S(2)}, u32[]{:S(2)}) collective-permute-start(f32[96,512]{1,0:T(8,128)S(1)} %collective-permute-done.7.refs_3_), channel_id=1, source_target_pairs={{0,8},{1,9},{2,10},{3,11},{4,12},{5,13},{6,14},{7,15},{8,16},{9,17... | collective-permute-start | bytes 589832 | tf_op jit(solution)/shard_map/ppermute | solution.py:413
  38.7 17.8 %collective-permute-start.13 = (f32[240,512]{1,0:T(8,128)S(1)}, f32[240,512]{1,0:T(8,128)S(1)}, u32[]{:S(2)}, u32[]{:S(2)}) collective-permute-start(f32[240,512]{1,0:T(8,128)S(1)} %slice_dynamic-update-slice_fusion), channel_id=1, source_target_pairs={{0,64},{1,65},{2,66},{3,67},{4,68},{5,69},{6,70},{7,71},{8,72},{9,... | collective-permute-start | bytes 1474568 | tf_op jit(solution)/shard_map/ppermute | solution.py:423
  41.6 15.0 %collective-permute-start.12 = (f32[240,512]{1,0:T(8,128)S(1)}, f32[240,512]{1,0:T(8,128)S(1)}, u32[]{:S(2)}, u32[]{:S(2)}) collective-permute-start(f32[240,512]{1,0:T(8,128)S(1)} %slice_dynamic-update-slice_fusion), channel_id=1, source_target_pairs={{0,192},{1,193},{2,194},{3,195},{4,196},{5,197},{6,198},{7,199},{8... | collective-permute-start | bytes 1474568 | tf_op jit(solution)/shard_map/ppermute | solution.py:422
  45.5 5.1 %collective-permute-start.11 = (f32[48,512]{1,0:T(8,128)S(1)}, f32[48,512]{1,0:T(8,128)S(1)}, u32[]{:S(2)}, u32[]{:S(2)}) collective-permute-start(f32[48,512]{1,0:T(8,128)S(1)} %slice.61), channel_id=1, source_target_pairs={{0,8},{1,9},{2,10},{3,11},{4,12},{5,13},{6,14},{7,15},{8,16},{9,17... | collective-permute-start | bytes 294920 | tf_op jit(solution)/shard_map/ppermute | solution.py:416
  50.6 9.7 %collective-permute-start.17 = (f32[144,512]{1,0:T(8,128)S(1)}, f32[144,512]{1,0:T(8,128)S(1)}, u32[]{:S(2)}, u32[]{:S(2)}) collective-permute-start(f32[144,512]{1,0:T(8,128)S(1)} %pad_maximum_fusion.1), channel_id=1, source_target_pairs={{0,64},{1,65},{2,66},{3,67},{4,68},{5,69},{6,70},{7,71},{8,72},{9,... | collective-permute-start | bytes 884744 | tf_op jit(solution)/shard_map/ppermute | solution.py:423
  50.7 9.6 %collective-permute-start.16 = (f32[144,512]{1,0:T(8,128)S(1)}, f32[144,512]{1,0:T(8,128)S(1)}, u32[]{:S(2)}, u32[]{:S(2)}) collective-permute-start(f32[144,512]{1,0:T(8,128)S(1)} %pad_maximum_fusion.1), channel_id=1, source_target_pairs={{0,192},{1,193},{2,194},{3,195},{4,196},{5,197},{6,198},{7,199},{8... | collective-permute-start | bytes 884744 | tf_op jit(solution)/shard_map/ppermute | solution.py:422
  56.5 3.5 %collective-permute-start.15 = (f32[48,512]{1,0:T(8,128)S(1)}, f32[48,512]{1,0:T(8,128)S(1)}, u32[]{:S(2)}, u32[]{:S(2)}) collective-permute-start(f32[48,512]{1,0:T(8,128)S(1)} %get-tuple-element.84), channel_id=1, source_target_pairs={{0,56},{1,57},{2,58},{3,59},{4,60},{5,61},{6,62},{7,63},{8,0},{9,1... | collective-permute-start | bytes 294920 | tf_op jit(solution)/shard_map/ppermute | solution.py:417
  63.8 6.2 %collective-permute-start.18 = (f32[384,256]{1,0:T(8,128)S(1)}, f32[384,256]{1,0:T(8,128)S(1)}, u32[]{:S(2)}, u32[]{:S(2)}) collective-permute-start(f32[384,256]{1,0:T(8,128)S(1)} %get-tuple-element.57), channel_id=1, source_target_pairs={{0,1},{1,0},{2,3},{3,2},{4,5},{5,4},{6,7},{7,6},{8,9},{9,8},{10,11... | collective-permute-start | bytes 1179656 | tf_op jit(solution)/shard_map/ppermute | solution.py:432
  70.8 6.7 %collective-permute-start.19 = (f32[4,48,512]{2,1,0:T(8,128)S(1)}, f32[4,48,512]{2,1,0:T(8,128)S(1)}, u32[]{:S(2)}, u32[]{:S(2)}) collective-permute-start(f32[4,48,512]{2,1,0:T(8,128)S(1)} %get-tuple-element.60), channel_id=1, source_target_pairs={{0,1},{1,0},{2,3},{3,2},{4,5},{5,4},{6,7},{7,6},{8,9},{9,8},{10,11... | collective-permute-start | bytes 1179656 | tf_op jit(solution)/shard_map/ppermute | solution.py:434
  71.1 15.8 %all-to-all-start = ((f32[16,24,256]{2,1,0:T(8,128)}), f32[16,24,256]{2,1,0:T(8,128)S(1)}, u32[]{:S(2)}, u32[]{:S(2)}) async-start(f32[16,24,256]{2,1,0:T(8,128)} %bitcast.12), calls=%async_computation | async-start | bytes 786432 | tf_op jit(solution)/shard_map/all_to_all | solution.py:247
  77.5 9.4 %collective-permute-start.22 = (f32[48,512]{1,0:T(8,128)S(1)}, f32[48,512]{1,0:T(8,128)S(1)}, u32[]{:S(2)}, u32[]{:S(2)}) collective-permute-start(f32[48,512]{1,0:T(8,128)S(1)} %get-tuple-element.79), channel_id=1, source_target_pairs={{0,6},{1,7},{2,0},{3,1},{4,2},{5,3},{6,4},{7,5},{8,14},{9,15},{10,... | collective-permute-start | bytes 294920 | tf_op jit(solution)/shard_map/ppermute | solution.py:437
  80.2 7.0 %collective-permute-start.21 = (f32[48,512]{1,0:T(8,128)S(1)}, f32[48,512]{1,0:T(8,128)S(1)}, u32[]{:S(2)}, u32[]{:S(2)}) collective-permute-start(f32[48,512]{1,0:T(8,128)S(1)} %get-tuple-element.80), channel_id=1, source_target_pairs={{0,4},{1,5},{2,6},{3,7},{4,0},{5,1},{6,2},{7,3},{8,12},{9,13},{10,... | collective-permute-start | bytes 294920 | tf_op jit(solution)/shard_map/ppermute | solution.py:437
  80.8 8.7 %collective-permute-start.20 = (f32[48,512]{1,0:T(8,128)S(1)}, f32[48,512]{1,0:T(8,128)S(1)}, u32[]{:S(2)}, u32[]{:S(2)}) collective-permute-start(f32[48,512]{1,0:T(8,128)S(1)} %get-tuple-element.81), channel_id=1, source_target_pairs={{0,2},{1,3},{2,4},{3,5},{4,6},{5,7},{6,0},{7,1},{8,10},{9,11},{10,... | collective-permute-start | bytes 294920 | tf_op jit(solution)/shard_map/ppermute | solution.py:437
  90.4 15.3 %all-to-all-start.1 = ((f32[8,24,256]{2,1,0:T(8,128)}), f32[8,24,256]{2,1,0:T(8,128)S(1)}, u32[]{:S(2)}, u32[]{:S(2)}) async-start(f32[8,24,256]{2,1,0:T(8,128)} %broadcast_in_dim.7), calls=%async_computation.1 | async-start | bytes 393216 | tf_op jit(solution)/shard_map/all_to_all | solution.py:252
  94.0 11.8 %collective-permute-start.23 = (f32[48,512]{1,0:T(8,128)S(1)}, f32[48,512]{1,0:T(8,128)S(1)}, u32[]{:S(2)}, u32[]{:S(2)}) collective-permute-start(f32[48,512]{1,0:T(8,128)S(1)} %inverse_rows.1), channel_id=1, source_target_pairs={{0,0},{1,8},{2,16},{3,24},{4,32},{5,40},{6,48},{7,56},{8,64},{9,72... | collective-permute-start | bytes 294920 | tf_op jit(solution)/shard_map/ppermute | solution.py:444
  106.6 20.6 %all-to-all-start.2 = ((f32[16,24,256]{2,1,0:T(8,128)}), f32[16,24,256]{2,1,0:T(8,128)S(1)}, u32[]{:S(2)}, u32[]{:S(2)}) async-start(f32[16,24,256]{2,1,0:T(8,128)} %broadcast_in_dim.8), calls=%async_computation.2 | async-start | bytes 786432 | tf_op jit(solution)/shard_map/all_to_all | solution.py:252
  117.0 2.7 %collective-permute-start.24 = (f32[8,8,256]{2,1,0:T(8,128)S(1)}, f32[8,8,256]{2,1,0:T(8,128)S(1)}, u32[]{:S(2)}, u32[]{:S(2)}) collective-permute-start(f32[8,8,256]{2,1,0:T(8,128)S(1)} %get-tuple-element.72), channel_id=1, source_target_pairs={{0,1},{1,0},{2,3},{3,2},{4,5},{5,4},{6,7},{7,6},{8,9},{9,8},{10,11... | collective-permute-start | bytes 196616 | tf_op jit(solution)/shard_map/ppermute | solution.py:451
  119.7 4.7 %collective-permute-start.27 = (f32[2,2,8,256]{3,2,1,0:T(8,128)S(1)}, f32[2,2,8,256]{3,2,1,0:T(8,128)S(1)}, u32[]{:S(2)}, u32[]{:S(2)}) collective-permute-start(f32[2,2,8,256]{3,2,1,0:T(8,128)S(1)} %get-tuple-element.85), channel_id=1, source_target_pairs={{0,6},{1,7},{2,0},{3,1},{4,2},{5,3},{6,4},{7,5},{8,14},{9,15},{10,... | collective-permute-start | bytes 98312 | tf_op jit(solution)/shard_map/ppermute | solution.py:352
  122.6 4.0 %collective-permute-start.25 = (f32[2,2,8,256]{3,2,1,0:T(8,128)S(1)}, f32[2,2,8,256]{3,2,1,0:T(8,128)S(1)}, u32[]{:S(2)}, u32[]{:S(2)}) collective-permute-start(f32[2,2,8,256]{3,2,1,0:T(8,128)S(1)} %get-tuple-element.87), channel_id=1, source_target_pairs={{0,2},{1,3},{2,4},{3,5},{4,6},{5,7},{6,0},{7,1},{8,10},{9,11},{10,... | collective-permute-start | bytes 98312 | tf_op jit(solution)/shard_map/ppermute | solution.py:352
  122.6 4.5 %collective-permute-start.26 = (f32[2,2,8,256]{3,2,1,0:T(8,128)S(1)}, f32[2,2,8,256]{3,2,1,0:T(8,128)S(1)}, u32[]{:S(2)}, u32[]{:S(2)}) collective-permute-start(f32[2,2,8,256]{3,2,1,0:T(8,128)S(1)} %get-tuple-element.88), channel_id=1, source_target_pairs={{0,4},{1,5},{2,6},{3,7},{4,0},{5,1},{6,2},{7,3},{8,12},{9,13},{10,... | collective-permute-start | bytes 98312 | tf_op jit(solution)/shard_map/ppermute | solution.py:352
  127.1 3.0 %collective-permute-start.28 = (f32[384,256]{1,0:T(8,128)S(1)}, f32[384,256]{1,0:T(8,128)S(1)}, u32[]{:S(2)}, u32[]{:S(2)}) collective-permute-start(f32[384,256]{1,0:T(8,128)S(1)} %bitcast.32), channel_id=1, source_target_pairs={{0,1},{1,0},{2,3},{3,2},{4,5},{5,4},{6,7},{7,6},{8,9},{9,8},{10,11... | collective-permute-start | bytes 1179656 | tf_op jit(solution)/shard_map/ppermute | solution.py:454
  (5 other events, 141.4 us)
